TPU v7x, 512 devices: a whole 4x8x8 slice. The times are simulated.
512 devices in a mesh: src: 4 (over x_hi, core), depth: 8 (over y), lat: 16 (over z, x_lo).
Axes of the slice: x: 4 (x_hi: 2, x_lo: 2; x = x_hi * 2 + x_lo), y: 8, z: 8, core: 2. Of those that a mesh axis runs over, the one named last changes fastest.
Arguments:
- conductivity: float32 [128, 128, 128], P('depth', 'lat'), may hold values from 0.2 to 2
- e_start: float32 [8, 3, 128, 128, 128], P('src', None, 'depth', 'lat'), may hold values from -6 to 6
- h_start: float32 [8, 3, 128, 128, 128], P('src', None, 'depth', 'lat'), may hold values from -6 to 6
- e_weight: float32 [8, 3, 128, 128, 128], P('src', None, 'depth', 'lat'), may hold values from -6 to 6
- h_weight: float32 [8, 3, 128, 128, 128], P('src', None, 'depth', 'lat'), may hold values from -6 to 6
- source_amp: float32 [8, 3], P('src'), may hold values from -12 to 12
- tow_cell: int32 [8], P('src'), may hold values from 0 to 2097151
- rec_cell: int32 [8, 16, 16], P('depth', 'lat'), may hold values from 0 to 16383
- rec_owner: int32 [8, 16, 16, 1], P('depth', 'lat'), may hold values from 0 to 15; in each aligned block of 16 rows (0 to 15, 16 to 31, ..., all dimensions but the last counted through in order) at most 2 rows name the same one
Outputs:
- grad: float32 [128, 128, 128], P('depth', 'lat')
- line_samples: float32 [8, 8, 16, 16, 2, 9], P('src', 'depth', 'lat')
Inputs may be any that keep to these rules, and one draw needn't show every extreme that they name: `tow_cell`: a flat cell of the whole grid. `rec_cell`: a local flat cell of the receiver's block; cells may repeat. `rec_owner`: among the 16 receivers of one block, at most 2 have the same owner, and in some block exactly 2 do.
All inputs are finite; a program needn't handle non-finite values.
Results may differ from a plain program's by a relative error of at most 0.0003.
Values sent between devices are 32-bit elements; how exact they have to be, the bound alone decides.
No kernel may reach another device: no remote copies, remote signals or barrier semaphores. Data moves between devices by JAX's collectives and lax.ppermute only.
A program may use at most 128 MiB of HBM per device.

v0:
```python
import jax
import jax.numpy as jnp
from jax import lax
from jax.sharding import PartitionSpec as P

ch_coef = 0.5
loss_rate = 0.5


def passed_along(block, axis, distance):
    devices = range(lax.axis_size(axis))
    route = [(i - distance, i) for i in devices if i - distance in devices]
    return lax.ppermute(block, axis, route)


def component(field, k):
    return field[..., k, :, :, :]


def curl_upper(field, rim_z, rim_x):
    fx = component(field, 0)
    fy = component(field, 1)
    fz = component(field, 2)
    zx = jnp.concatenate([fx, component(rim_z, 0)], axis=-3)[..., 1:, :, :] - fx
    zy = jnp.concatenate([fy, component(rim_z, 1)], axis=-3)[..., 1:, :, :] - fy
    xy = jnp.concatenate([fy, component(rim_x, 0)], axis=-2)[..., :, 1:, :] - fy
    xz = jnp.concatenate([fz, component(rim_x, 1)], axis=-2)[..., :, 1:, :] - fz
    yz = jnp.concatenate([fz[..., 1:], jnp.zeros_like(fz[..., :1])], axis=-1) - fz
    yx = jnp.concatenate([fx[..., 1:], jnp.zeros_like(fx[..., :1])], axis=-1) - fx
    return jnp.stack([yz - zy, zx - xz, xy - yx], axis=-4)


def curl_lower(field, rim_z, rim_x):
    fx = component(field, 0)
    fy = component(field, 1)
    fz = component(field, 2)
    zx = fx - jnp.concatenate([component(rim_z, 0), fx], axis=-3)[..., :-1, :, :]
    zy = fy - jnp.concatenate([component(rim_z, 1), fy], axis=-3)[..., :-1, :, :]
    xy = fy - jnp.concatenate([component(rim_x, 0), fy], axis=-2)[..., :, :-1, :]
    xz = fz - jnp.concatenate([component(rim_x, 1), fz], axis=-2)[..., :, :-1, :]
    yz = fz - jnp.concatenate([jnp.zeros_like(fz[..., :1]), fz[..., :-1]], axis=-1)
    yx = fx - jnp.concatenate([jnp.zeros_like(fx[..., :1]), fx[..., :-1]], axis=-1)
    return jnp.stack([yz - zy, zx - xz, xy - yx], axis=-4)


def coefficients(sigma):
    denom = 1.0 + loss_rate * sigma
    decay = (1.0 - loss_rate * sigma) / denom
    gain = ch_coef / denom
    decay_slope = -2.0 * loss_rate / (denom * denom)
    gain_slope = -ch_coef * loss_rate / (denom * denom)
    return (decay, gain, decay_slope, gain_slope)


def upper_rims(field):
    rim_z = passed_along(field[:, 0:2, 0:1], "depth", -1)
    rim_x = passed_along(field[:, 1:3, :, 0:1], "lat", -1)
    return (rim_z, rim_x)


def lower_rims(field):
    rim_z = passed_along(field[:, 0:2, -1:], "depth", 1)
    rim_x = passed_along(field[:, 1:3, :, -1:], "lat", 1)
    return (rim_z, rim_x)


def leap_one(first, second, scale):
    scaled = scale * first
    rim_z, rim_x = upper_rims(scaled)
    updated = second + curl_upper(scaled, rim_z, rim_x)
    low_z, low_x = lower_rims(updated)
    return (updated, curl_lower(updated, low_z, low_x))


def per_device(
    conductivity, e_start, h_start, e_weight, h_weight, source_amp, tow_cell, rec_cell, rec_owner
):
    groups, _, depth_cells, lat_cells, width = e_start.shape
    steps_total = source_amp.shape[1]
    tiles = lax.axis_size("lat")
    capacity = max(2, rec_cell.shape[-1] // tiles)
    depth_at = lax.axis_index("depth")
    lat_at = lax.axis_index("lat")
    decay, gain, decay_slope, gain_slope = coefficients(conductivity)
    margin = 0
    decay_use, gain_use = (decay, gain)
    e_field, h_field, lam_e, lam_h = (e_start, h_start, e_weight, h_weight)

    def leap(first, second, scale):
        return leap_one(first, second, scale)

    plane = lat_cells * tiles * width
    local_z = tow_cell // plane - depth_at * depth_cells + margin
    local_x = tow_cell // width % (lat_cells * tiles) - lat_at * lat_cells + margin
    local_y = tow_cell % width
    grid_z = jnp.arange(depth_cells + 2 * margin)[:, None, None]
    grid_x = jnp.arange(lat_cells + 2 * margin)[None, :, None]
    grid_y = jnp.arange(width)[None, None, :]
    point = (
        (grid_z[None] == local_z[:, None, None, None])
        & (grid_x[None] == local_x[:, None, None, None])
        & (grid_y[None] == local_y[:, None, None, None])
    ).astype(jnp.float32)
    blank = jnp.zeros_like(point)
    owner = rec_owner.reshape(-1)
    cells = rec_cell.reshape(-1)
    order = jnp.arange(owner.shape[0])
    rank = jnp.sum(
        ((owner[:, None] == owner[None, :]) & (order[None, :] < order[:, None])).astype(jnp.int32),
        axis=1,
    )
    hot = (
        (owner[:, None, None] == jnp.arange(tiles)[:, None])
        & (rank[:, None, None] == jnp.arange(capacity)[None, :])
    ).astype(jnp.float32)
    kept = []
    delivered = []
    for step in range(steps_total):
        h_field, turned = leap(e_field, h_field, -ch_coef)
        source = source_amp[:, step][:, None, None, None] * point
        drive = turned - jnp.stack([source, blank, blank], axis=1)
        kept.append((e_field, drive))
        e_field = decay_use * e_field + gain_use * drive
        sampled = jnp.take(e_field.reshape(groups, 3, -1), cells, axis=2)
        placed = jnp.sum(sampled[:, :, :, None, None] * hot[None, None], axis=2)
        delivered.append(
            lax.all_to_all(
                jnp.transpose(placed, (0, 2, 3, 1)), "lat", split_axis=1, concat_axis=1, tiled=True
            )
        )
    received = jnp.concatenate(delivered, axis=-1)
    line_samples = received.reshape(groups, 1, 1, tiles, capacity, 3 * steps_total)
    local = jnp.zeros((depth_cells, lat_cells, width), jnp.float32)
    for step in range(steps_total - 1, -1, -1):
        e_old, drive = kept[step]
        weight_now = lam_e
        term = jnp.sum(
            decay_slope * e_old * weight_now + gain_slope * drive * weight_now, axis=(0, 1)
        )
        local = local + term
        if step > 0:
            lam_h, turned = leap(lam_e, lam_h, gain)
            lam_e = decay_use * lam_e - ch_coef * turned
    total = lax.psum(local, "src")
    return (total, line_samples)


def solution(mesh):
    placed = (
        P("depth", "lat", None),
        P("src", None, "depth", "lat", None),
        P("src", None, "depth", "lat", None),
        P("src", None, "depth", "lat", None),
        P("src", None, "depth", "lat", None),
        P("src", None),
        P("src"),
        P("depth", "lat", None),
        P("depth", "lat", None, None),
    )
    return jax.shard_map(
        per_device,
        mesh=mesh,
        in_specs=placed,
        out_specs=(P("depth", "lat", None), P("src", "depth", "lat", None, None, None)),
        check_vma=False,
    )
```

profile of v0, /device:TPU:1, one launch (start us, length us, event | category | flops | bytes accessed | tf_op | source)
XLA Modules:
  0.0 280.9 jit_solution(6807090759365684788)
XLA Ops:
  8.3 1.3 collective-permute-start
  9.6 1.3 collective-permute-start.1
  13.2 1.2 compare_and_fusion
  16.4 1.5 multiply_divide_fusion.1
  19.2 1.1 maximum_add_fusion
  20.3 4.7 %collective-permute-start.2 = (f32[2,2,1,8,128]{4,0,3,2,1:T(2,128)S(1)}, f32[2,2,1,8,128]{4,0,3,2,1:T(2,128)S(1)}, u32[]{:S(2)}, u32[]{:S(2)}) collective-permute-start(f32[2,2,1,8,128]{4,0,3,2,1:T(2,128)S(1)} %bitcast.362), channel_id=1, source_target_pairs={{0,16},{16,32},{32,48},{48,64},{64,80},{80,96},{96,112},{1,17},{17... | collective-permute-start | bytes 49160 | tf_op jit(solution)/shard_map/ppermute | solution.py:13
  25.0 4.0 %collective-permute-start.3 = (f32[2,2,16,1,128]{4,2,0,3,1:T(8,128)S(1)}, f32[2,2,16,1,128]{4,2,0,3,1:T(8,128)S(1)}, u32[]{:S(2)}, u32[]{:S(2)}) collective-permute-start(f32[2,2,16,1,128]{4,2,0,3,1:T(8,128)S(1)} %slice.636), channel_id=1, source_target_pairs={{0,1},{1,2},{2,3},{3,4},{4,5},{5,6},{6,7},{7,8},{8,9},{9,10},{10,1... | collective-permute-start | bytes 98312 | tf_op jit(solution)/shard_map/ppermute | solution.py:13
  30.3 1.2 multiply_add_fusion.2
  31.6 1.3 collective-permute-start.4
  33.0 11.4 %copy.327 = f32[2,3,16,8,128]{1,0,4,3,2:T(2,128)} copy(f32[2,3,16,8,128]{4,3,2,0,1:T(8,128)S(1)} %multiply_add_fusion.2) | data formatting | bytes 786432 | tf_op jit(solution)/shard_map/add | solution.py:123
  44.5 1.3 collective-permute-start.5
  46.0 6.9 %gather_fusion = f32[16,2,3]{2,1,0:T(2,128)} fusion(f32[2,3,16384]{1,0,2:T(2,128)} %bitcast.334, s32[1024]{0:T(1024)S(1)} %pad_clamp_fusion), kind=kCustom, calls=%fused_computation.clone | custom fusion | bytes 832 | tf_op jit(solution)/shard_map/jit(_take)/gather | solution.py:124
  53.7 4.0 %collective-permute-start.6 = (f32[2,2,1,8,128]{4,3,0,2,1:T(8,128)S(1)}, f32[2,2,1,8,128]{4,3,0,2,1:T(8,128)S(1)}, u32[]{:S(2)}, u32[]{:S(2)}) collective-permute-start(f32[2,2,1,8,128]{4,3,0,2,1:T(8,128)S(1)} %slice_bitcast_fusion.44), channel_id=1, source_target_pairs={{0,16},{16,32},{32,48},{48,64},{64,80},{80,96},{96,112},{1,17},{17... | collective-permute-start | bytes 49160 | tf_op jit(solution)/shard_map/ppermute | solution.py:13
  57.7 4.8 %collective-permute-start.7 = (f32[2,2,16,1,128]{4,3,2,0,1:T(1,128)S(1)}, f32[2,2,16,1,128]{4,3,2,0,1:T(1,128)S(1)}, u32[]{:S(2)}, u32[]{:S(2)}) collective-permute-start(f32[2,2,16,1,128]{4,3,2,0,1:T(1,128)S(1)} %slice.658), channel_id=1, source_target_pairs={{0,1},{1,2},{2,3},{3,4},{4,5},{5,6},{6,7},{7,8},{8,9},{9,10},{10,1... | collective-permute-start | bytes 98312 | tf_op jit(solution)/shard_map/ppermute | solution.py:13
  65.3 1.3 collective-permute-start.8
  70.6 1.3 collective-permute-start.9
  71.9 1.3 collective-permute-start.12
  74.7 1.3 collective-permute-start.13
  76.0 11.4 %copy.330 = f32[2,3,16,8,128]{1,0,4,3,2:T(2,128)} copy(f32[2,3,16,8,128]{4,3,2,0,1:T(8,128)S(1)} %get-tuple-element.18) | data formatting | bytes 786432 | tf_op jit(solution)/shard_map/add | solution.py:123
  87.4 7.1 %gather_fusion.1 = f32[16,2,3]{2,1,0:T(2,128)} fusion(f32[2,3,16384]{1,0,2:T(2,128)} %bitcast.336, s32[1024]{0:T(1024)} %copy-done.18), kind=kCustom, calls=%fused_computation.1.clone | custom fusion | bytes 832 | tf_op jit(solution)/shard_map/jit(_take)/gather | solution.py:124
  96.7 1.1 fusion.59
  97.8 1.2 fusion.63
  99.1 1.2 maximum_add_fusion.2
  100.4 4.6 %collective-permute-start.10 = (f32[2,2,1,8,128]{4,3,0,2,1:T(8,128)S(1)}, f32[2,2,1,8,128]{4,3,0,2,1:T(8,128)S(1)}, u32[]{:S(2)}, u32[]{:S(2)}) collective-permute-start(f32[2,2,1,8,128]{4,3,0,2,1:T(8,128)S(1)} %slice_bitcast_fusion.38), channel_id=1, source_target_pairs={{0,16},{16,32},{32,48},{48,64},{64,80},{80,96},{96,112},{1,17},{17... | collective-permute-start | bytes 49160 | tf_op jit(solution)/shard_map/ppermute | solution.py:13
  105.7 1.1 fusion.39
  106.9 1.3 fusion.43
  109.3 5.8 %collective-permute-start.11 = (f32[2,2,16,1,128]{4,3,2,0,1:T(1,128)S(1)}, f32[2,2,16,1,128]{4,3,2,0,1:T(1,128)S(1)}, u32[]{:S(2)}, u32[]{:S(2)}) collective-permute-start(f32[2,2,16,1,128]{4,3,2,0,1:T(1,128)S(1)} %slice.680), channel_id=1, source_target_pairs={{0,1},{1,2},{2,3},{3,4},{4,5},{5,6},{6,7},{7,8},{8,9},{9,10},{10,1... | collective-permute-start | bytes 98312 | tf_op jit(solution)/shard_map/ppermute | solution.py:13
  115.2 4.1 %collective-permute-start.14 = (f32[2,2,1,8,128]{4,3,0,2,1:T(8,128)S(1)}, f32[2,2,1,8,128]{4,3,0,2,1:T(8,128)S(1)}, u32[]{:S(2)}, u32[]{:S(2)}) collective-permute-start(f32[2,2,1,8,128]{4,3,0,2,1:T(8,128)S(1)} %copy.349), channel_id=1, source_target_pairs={{0,16},{16,32},{32,48},{48,64},{64,80},{80,96},{96,112},{1,17},{17... | collective-permute-start | bytes 49160 | tf_op jit(solution)/shard_map/ppermute | solution.py:13
  119.3 4.5 %collective-permute-start.15 = (f32[2,2,16,1,128]{4,2,0,3,1:T(8,128)S(1)}, f32[2,2,16,1,128]{4,2,0,3,1:T(8,128)S(1)}, u32[]{:S(2)}, u32[]{:S(2)}) collective-permute-start(f32[2,2,16,1,128]{4,2,0,3,1:T(8,128)S(1)} %copy.351), channel_id=1, source_target_pairs={{0,1},{1,2},{2,3},{3,4},{4,5},{5,6},{6,7},{7,8},{8,9},{9,10},{10,1... | collective-permute-start | bytes 98312 | tf_op jit(solution)/shard_map/ppermute | solution.py:13
  125.2 2.5 multiply_add_fusion
  127.7 12.7 %copy.333 = f32[2,3,16,8,128]{1,0,4,3,2:T(2,128)} copy(f32[2,3,16,8,128]{4,3,2,0,1:T(8,128)} %get-tuple-element.21) | data formatting | bytes 786432 | tf_op jit(solution)/shard_map/add | solution.py:123
  140.4 6.5 %gather_fusion.2 = f32[16,2,3]{2,1,0:T(2,128)S(1)} fusion(f32[2,3,16384]{1,0,2:T(2,128)} %bitcast.335, s32[1024]{0:T(1024)} %copy-done.18), kind=kCustom, calls=%fused_computation.2.clone | custom fusion | bytes 832 | tf_op jit(solution)/shard_map/jit(_take)/gather | solution.py:124
  148.2 14.6 %all-to-all-start.2 = ((f32[2,16,2,3]{3,2,0,1:T(2,128)}), f32[2,16,2,3]{3,2,0,1:T(2,128)S(1)}, u32[]{:S(2)}, u32[]{:S(2)}) async-start(f32[2,16,2,3]{3,2,0,1:T(2,128)} %copy.335), calls=%async_computation.2 | async-start | bytes 65536 | tf_op jit(solution)/shard_map/all_to_all | solution.py:127
  163.4 6.9 %all-to-all-done.2 = f32[2,16,2,3]{3,2,0,1:T(2,128)S(1)} async-done(((f32[2,16,2,3]{3,2,0,1:T(2,128)}), f32[2,16,2,3]{3,2,0,1:T(2,128)S(1)}, u32[]{:S(2)}, u32[]{:S(2)}) %all-to-all-start.2) | async-done | bytes 800 | tf_op jit(solution)/shard_map/all_to_all | solution.py:127
  170.3 3.5 %all-to-all-start.1 = ((f32[2,16,2,3]{3,2,0,1:T(2,128)}), f32[2,16,2,3]{3,2,0,1:T(2,128)S(1)}, u32[]{:S(2)}, u32[]{:S(2)}) async-start(f32[2,16,2,3]{3,2,0,1:T(2,128)} %copy.332), calls=%async_computation.1 | async-start | bytes 65536 | tf_op jit(solution)/shard_map/all_to_all | solution.py:127
  174.4 1.3 collective-permute-start.16
  176.4 5.0 %all-to-all-done.1 = f32[2,16,2,3]{3,2,0,1:T(2,128)S(1)} async-done(((f32[2,16,2,3]{3,2,0,1:T(2,128)}), f32[2,16,2,3]{3,2,0,1:T(2,128)S(1)}, u32[]{:S(2)}, u32[]{:S(2)}) %all-to-all-start.1) | async-done | bytes 800 | tf_op jit(solution)/shard_map/all_to_all | solution.py:127
  181.4 4.1 %all-to-all-start = ((f32[2,16,2,3]{3,2,0,1:T(2,128)}), f32[2,16,2,3]{3,2,0,1:T(2,128)}, u32[]{:S(2)}, u32[]{:S(2)}) async-start(f32[2,16,2,3]{3,2,0,1:T(2,128)} %copy.329), calls=%async_computation | async-start | bytes 65536 | tf_op jit(solution)/shard_map/all_to_all | solution.py:127
  187.1 1.3 collective-permute-start.17
  190.1 3.0 %all-to-all-done = f32[2,16,2,3]{3,2,0,1:T(2,128)} async-done(((f32[2,16,2,3]{3,2,0,1:T(2,128)}), f32[2,16,2,3]{3,2,0,1:T(2,128)}, u32[]{:S(2)}, u32[]{:S(2)}) %all-to-all-start) | async-done | bytes 800 | tf_op jit(solution)/shard_map/all_to_all | solution.py:127
  193.1 1.4 copy.336
  196.1 1.1 fusion.23
  197.3 4.6 %collective-permute-start.18 = (f32[2,2,1,8,128]{4,3,0,2,1:T(8,128)S(1)}, f32[2,2,1,8,128]{4,3,0,2,1:T(8,128)S(1)}, u32[]{:S(2)}, u32[]{:S(2)}) collective-permute-start(f32[2,2,1,8,128]{4,3,0,2,1:T(8,128)S(1)} %copy.355), channel_id=1, source_target_pairs={{0,16},{16,32},{32,48},{48,64},{64,80},{80,96},{96,112},{1,17},{17... | collective-permute-start | bytes 49160 | tf_op jit(solution)/shard_map/ppermute | solution.py:13
  202.0 2.2 collective-permute-start.19
  205.4 1.4 multiply_reduce_fusion
  207.5 1.3 maximum_bitcast_fusion
  208.8 63.8 %all-reduce.25.cloned.1.call-done = f32[16,8,128]{2,1,0:T(8,128)} async-done(((f32[16,8,128]{2,1,0:T(8,128)}), f32[16,8,128]{2,1,0:T(8,128)}) %all-reduce.25.cloned.1.call-update) | async-done | bytes 65552 | tf_op jit(solution)/shard_map/psum | solution.py:144
  272.6 1.5 copy.385
  (175 shorter events, 32.5 us)
Async XLA Ops:
  8.3 10.8 %collective-permute-start = (f32[2,2,1,8,128]{4,0,3,2,1:T(2,128)S(1)}, f32[2,2,1,8,128]{4,0,3,2,1:T(2,128)S(1)}, u32[]{:S(2)}, u32[]{:S(2)}) collective-permute-start(f32[2,2,1,8,128]{4,0,3,2,1:T(2,128)S(1)} %bitcast.361), channel_id=1, source_target_pairs={{16,0},{32,16},{48,32},{64,48},{80,64},{96,80},{112,96},{17,1},{33... | collective-permute-start | bytes 49160 | tf_op jit(solution)/shard_map/ppermute | solution.py:13
  9.6 9.5 %collective-permute-start.1 = (f32[2,2,16,1,128]{4,2,0,3,1:T(8,128)S(1)}, f32[2,2,16,1,128]{4,2,0,3,1:T(8,128)S(1)}, u32[]{:S(2)}, u32[]{:S(2)}) collective-permute-start(f32[2,2,16,1,128]{4,2,0,3,1:T(8,128)S(1)} %slice.625), channel_id=1, source_target_pairs={{1,0},{2,1},{3,2},{4,3},{5,4},{6,5},{7,6},{8,7},{9,8},{10,9},{11,1... | collective-permute-start | bytes 98312 | tf_op jit(solution)/shard_map/ppermute | solution.py:13
  18.8 11.5 %copy-start.12 = (f32[2,1,16,8,128]{4,3,2,0,1:T(8,128)}, f32[2,1,16,8,128]{4,3,2,0,1:T(8,128)S(1)}, u32[]{:S(2)}) copy-start(f32[2,1,16,8,128]{4,3,2,0,1:T(8,128)S(1)} %get-tuple-element.123) | copy-start | bytes 393220
  18.8 45.0 %copy-start.1 = (f32[2,3,16,8,128]{4,3,2,1,0:T(8,128)S(1)}, f32[2,3,16,8,128]{4,3,2,1,0:T(8,128)}, u32[]{:S(2)}) copy-start(f32[2,3,16,8,128]{4,3,2,1,0:T(8,128)} %param.14) | copy-start | bytes 1179652
  18.8 34.2 %copy-start.18 = (s32[1024]{0:T(1024)}, s32[1024]{0:T(1024)S(1)}, u32[]{:S(2)}) copy-start(s32[1024]{0:T(1024)S(1)} %pad_clamp_fusion) | copy-start | bytes 12292
  20.3 8.7 %collective-permute-start.2 = (f32[2,2,1,8,128]{4,0,3,2,1:T(2,128)S(1)}, f32[2,2,1,8,128]{4,0,3,2,1:T(2,128)S(1)}, u32[]{:S(2)}, u32[]{:S(2)}) collective-permute-start(f32[2,2,1,8,128]{4,0,3,2,1:T(2,128)S(1)} %bitcast.362), channel_id=1, source_target_pairs={{0,16},{16,32},{32,48},{48,64},{64,80},{80,96},{96,112},{1,17},{17... | collective-permute-start | bytes 49160 | tf_op jit(solution)/shard_map/ppermute | solution.py:13
  25.0 5.0 %collective-permute-start.3 = (f32[2,2,16,1,128]{4,2,0,3,1:T(8,128)S(1)}, f32[2,2,16,1,128]{4,2,0,3,1:T(8,128)S(1)}, u32[]{:S(2)}, u32[]{:S(2)}) collective-permute-start(f32[2,2,16,1,128]{4,2,0,3,1:T(8,128)S(1)} %slice.636), channel_id=1, source_target_pairs={{0,1},{1,2},{2,3},{3,4},{4,5},{5,6},{6,7},{7,8},{8,9},{9,10},{10,1... | collective-permute-start | bytes 98312 | tf_op jit(solution)/shard_map/ppermute | solution.py:13
  31.6 21.4 %collective-permute-start.4 = (f32[2,2,1,8,128]{4,2,0,3,1:T(1,128)S(1)}, f32[2,2,1,8,128]{4,2,0,3,1:T(1,128)S(1)}, u32[]{:S(2)}, u32[]{:S(2)}) collective-permute-start(f32[2,2,1,8,128]{4,2,0,3,1:T(1,128)S(1)} %slice.643), channel_id=1, source_target_pairs={{16,0},{32,16},{48,32},{64,48},{80,64},{96,80},{112,96},{17,1},{33... | collective-permute-start | bytes 49160 | tf_op jit(solution)/shard_map/ppermute | solution.py:13
  44.5 8.5 %collective-permute-start.5 = (f32[2,2,16,1,128]{4,2,0,3,1:T(8,128)S(1)}, f32[2,2,16,1,128]{4,2,0,3,1:T(8,128)S(1)}, u32[]{:S(2)}, u32[]{:S(2)}) collective-permute-start(f32[2,2,16,1,128]{4,2,0,3,1:T(8,128)S(1)} %slice.647), channel_id=1, source_target_pairs={{1,0},{2,1},{3,2},{4,3},{5,4},{6,5},{7,6},{8,7},{9,8},{10,9},{11,1... | collective-permute-start | bytes 98312 | tf_op jit(solution)/shard_map/ppermute | solution.py:13
  53.2 10.6 %copy-start.6 = (f32[2,1,16,8,128]{4,3,2,0,1:T(8,128)}, f32[2,1,16,8,128]{4,3,2,0,1:T(8,128)S(1)}, u32[]{:S(2)}) copy-start(f32[2,1,16,8,128]{4,3,2,0,1:T(8,128)S(1)} %copy.285) | copy-start | bytes 393220
  53.3 10.4 %copy-start.7 = (f32[2,1,16,8,128]{4,3,2,0,1:T(8,128)}, f32[2,1,16,8,128]{4,3,2,0,1:T(8,128)S(1)}, u32[]{:S(2)}) copy-start(f32[2,1,16,8,128]{4,3,2,0,1:T(8,128)S(1)} %fusion.102) | copy-start | bytes 393220
  53.7 8.9 %collective-permute-start.6 = (f32[2,2,1,8,128]{4,3,0,2,1:T(8,128)S(1)}, f32[2,2,1,8,128]{4,3,0,2,1:T(8,128)S(1)}, u32[]{:S(2)}, u32[]{:S(2)}) collective-permute-start(f32[2,2,1,8,128]{4,3,0,2,1:T(8,128)S(1)} %slice_bitcast_fusion.44), channel_id=1, source_target_pairs={{0,16},{16,32},{32,48},{48,64},{64,80},{80,96},{96,112},{1,17},{17... | collective-permute-start | bytes 49160 | tf_op jit(solution)/shard_map/ppermute | solution.py:13
  57.7 5.8 %collective-permute-start.7 = (f32[2,2,16,1,128]{4,3,2,0,1:T(1,128)S(1)}, f32[2,2,16,1,128]{4,3,2,0,1:T(1,128)S(1)}, u32[]{:S(2)}, u32[]{:S(2)}) collective-permute-start(f32[2,2,16,1,128]{4,3,2,0,1:T(1,128)S(1)} %slice.658), channel_id=1, source_target_pairs={{0,1},{1,2},{2,3},{3,4},{4,5},{5,6},{6,7},{7,8},{8,9},{9,10},{10,1... | collective-permute-start | bytes 98312 | tf_op jit(solution)/shard_map/ppermute | solution.py:13
  63.7 61.5 %copy-start.2 = (f32[2,1,16,8,128]{4,3,2,0,1:T(8,128)}, f32[2,1,16,8,128]{4,3,2,0,1:T(8,128)S(1)}, u32[]{:S(2)}) copy-start(f32[2,1,16,8,128]{4,3,2,0,1:T(8,128)S(1)} %get-tuple-element.33) | copy-start | bytes 393220
  63.7 61.5 %copy-start.4 = (f32[2,1,16,8,128]{4,3,2,0,1:T(8,128)}, f32[2,1,16,8,128]{4,3,2,0,1:T(8,128)S(1)}, u32[]{:S(2)}) copy-start(f32[2,1,16,8,128]{4,3,2,0,1:T(8,128)S(1)} %get-tuple-element.34) | copy-start | bytes 393220
  64.6 10.1 %copy-start.10 = (f32[2,16,8,128]{3,2,1,0:T(8,128)}, f32[2,16,8,128]{3,2,1,0:T(8,128)S(1)}, u32[]{:S(2)}) copy-start(f32[2,16,8,128]{3,2,1,0:T(8,128)S(1)} %get-tuple-element.46) | copy-start | bytes 393220
  64.6 11.4 %copy-start.11 = (f32[2,16,8,128]{3,2,1,0:T(8,128)}, f32[2,16,8,128]{3,2,1,0:T(8,128)S(1)}, u32[]{:S(2)}) copy-start(f32[2,16,8,128]{3,2,1,0:T(8,128)S(1)} %get-tuple-element.47) | copy-start | bytes 393220
  65.3 29.2 %collective-permute-start.8 = (f32[2,2,1,8,128]{4,3,0,2,1:T(8,128)}, f32[2,2,1,8,128]{4,3,0,2,1:T(8,128)}, u32[]{:S(2)}, u32[]{:S(2)}) collective-permute-start(f32[2,2,1,8,128]{4,3,0,2,1:T(8,128)} %slice_bitcast_fusion.41), channel_id=1, source_target_pairs={{16,0},{32,16},{48,32},{64,48},{80,64},{96,80},{112,96},{17,1},{33... | collective-permute-start | bytes 49160 | tf_op jit(solution)/shard_map/ppermute | solution.py:13
  67.2 6.0 %copy-start.8 = (f32[2,16,8,128]{3,2,1,0:T(8,128)}, f32[2,16,8,128]{3,2,1,0:T(8,128)S(1)}, u32[]{:S(2)}) copy-start(f32[2,16,8,128]{3,2,1,0:T(8,128)S(1)} %get-tuple-element.71) | copy-start | bytes 393220
  67.2 6.7 %copy-start.9 = (f32[2,16,8,128]{3,2,1,0:T(8,128)}, f32[2,16,8,128]{3,2,1,0:T(8,128)S(1)}, u32[]{:S(2)}) copy-start(f32[2,16,8,128]{3,2,1,0:T(8,128)S(1)} %get-tuple-element.72) | copy-start | bytes 393220
  70.6 25.3 %collective-permute-start.9 = (f32[2,2,16,1,128]{4,3,2,0,1:T(1,128)}, f32[2,2,16,1,128]{4,3,2,0,1:T(1,128)}, u32[]{:S(2)}, u32[]{:S(2)}) collective-permute-start(f32[2,2,16,1,128]{4,3,2,0,1:T(1,128)} %slice.669), channel_id=1, source_target_pairs={{1,0},{2,1},{3,2},{4,3},{5,4},{6,5},{7,6},{8,7},{9,8},{10,9},{11,1... | collective-permute-start | bytes 98312 | tf_op jit(solution)/shard_map/ppermute | solution.py:13
  71.9 23.3 %collective-permute-start.12 = (f32[2,2,1,8,128]{4,3,0,2,1:T(8,128)}, f32[2,2,1,8,128]{4,3,0,2,1:T(8,128)}, u32[]{:S(2)}, u32[]{:S(2)}) collective-permute-start(f32[2,2,1,8,128]{4,3,0,2,1:T(8,128)} %slice_bitcast_fusion.35), channel_id=1, source_target_pairs={{16,0},{32,16},{48,32},{64,48},{80,64},{96,80},{112,96},{17,1},{33... | collective-permute-start | bytes 49160 | tf_op jit(solution)/shard_map/ppermute | solution.py:13
  74.7 30.2 %collective-permute-start.13 = (f32[2,2,16,1,128]{4,3,2,0,1:T(1,128)}, f32[2,2,16,1,128]{4,3,2,0,1:T(1,128)}, u32[]{:S(2)}, u32[]{:S(2)}) collective-permute-start(f32[2,2,16,1,128]{4,3,2,0,1:T(1,128)} %slice.691), channel_id=1, source_target_pairs={{1,0},{2,1},{3,2},{4,3},{5,4},{6,5},{7,6},{8,7},{9,8},{10,9},{11,1... | collective-permute-start | bytes 98312 | tf_op jit(solution)/shard_map/ppermute | solution.py:13
  100.4 23.5 %collective-permute-start.10 = (f32[2,2,1,8,128]{4,3,0,2,1:T(8,128)S(1)}, f32[2,2,1,8,128]{4,3,0,2,1:T(8,128)S(1)}, u32[]{:S(2)}, u32[]{:S(2)}) collective-permute-start(f32[2,2,1,8,128]{4,3,0,2,1:T(8,128)S(1)} %slice_bitcast_fusion.38), channel_id=1, source_target_pairs={{0,16},{16,32},{32,48},{48,64},{64,80},{80,96},{96,112},{1,17},{17... | collective-permute-start | bytes 49160 | tf_op jit(solution)/shard_map/ppermute | solution.py:13
  106.9 98.5 %copy-start = (f32[2,3,16,8,128]{4,3,2,1,0:T(8,128)S(1)}, f32[2,3,16,8,128]{4,3,2,1,0:T(8,128)}, u32[]{:S(2)}) copy-start(f32[2,3,16,8,128]{4,3,2,1,0:T(8,128)} %param.12) | copy-start | bytes 1179652
  109.3 14.6 %collective-permute-start.11 = (f32[2,2,16,1,128]{4,3,2,0,1:T(1,128)S(1)}, f32[2,2,16,1,128]{4,3,2,0,1:T(1,128)S(1)}, u32[]{:S(2)}, u32[]{:S(2)}) collective-permute-start(f32[2,2,16,1,128]{4,3,2,0,1:T(1,128)S(1)} %slice.680), channel_id=1, source_target_pairs={{0,1},{1,2},{2,3},{3,4},{4,5},{5,6},{6,7},{7,8},{8,9},{9,10},{10,1... | collective-permute-start | bytes 98312 | tf_op jit(solution)/shard_map/ppermute | solution.py:13
  115.2 8.7 %collective-permute-start.14 = (f32[2,2,1,8,128]{4,3,0,2,1:T(8,128)S(1)}, f32[2,2,1,8,128]{4,3,0,2,1:T(8,128)S(1)}, u32[]{:S(2)}, u32[]{:S(2)}) collective-permute-start(f32[2,2,1,8,128]{4,3,0,2,1:T(8,128)S(1)} %copy.349), channel_id=1, source_target_pairs={{0,16},{16,32},{32,48},{48,64},{64,80},{80,96},{96,112},{1,17},{17... | collective-permute-start | bytes 49160 | tf_op jit(solution)/shard_map/ppermute | solution.py:13
  119.3 5.6 %collective-permute-start.15 = (f32[2,2,16,1,128]{4,2,0,3,1:T(8,128)S(1)}, f32[2,2,16,1,128]{4,2,0,3,1:T(8,128)S(1)}, u32[]{:S(2)}, u32[]{:S(2)}) collective-permute-start(f32[2,2,16,1,128]{4,2,0,3,1:T(8,128)S(1)} %copy.351), channel_id=1, source_target_pairs={{0,1},{1,2},{2,3},{3,4},{4,5},{5,6},{6,7},{7,8},{8,9},{9,10},{10,1... | collective-permute-start | bytes 98312 | tf_op jit(solution)/shard_map/ppermute | solution.py:13
  127.7 19.2 %copy-start.16 = (f32[16,2,3]{2,1,0:T(2,128)S(1)}, f32[16,2,3]{2,1,0:T(2,128)}, u32[]{:S(2)}) copy-start(f32[16,2,3]{2,1,0:T(2,128)} %gather_fusion) | copy-start | bytes 1156
  127.7 19.2 %copy-start.17 = (f32[16,2,3]{2,1,0:T(2,128)S(1)}, f32[16,2,3]{2,1,0:T(2,128)}, u32[]{:S(2)}) copy-start(f32[16,2,3]{2,1,0:T(2,128)} %gather_fusion.1) | copy-start | bytes 1156
  127.7 19.2 %copy-start.19 = (pred[16]{0:T(512)(128)(4,1)S(1)}, pred[16]{0:T(512)(128)(4,1)}, u32[]{:S(2)}) copy-start(pred[16]{0:T(512)(128)(4,1)} %compare_and_fusion) | copy-start | bytes 52
  127.7 77.7 %copy-start.3 = (f32[2,1,16,8,128]{4,3,2,0,1:T(8,128)S(1)}, f32[2,1,16,8,128]{4,3,2,0,1:T(8,128)}, u32[]{:S(2)}) copy-start(f32[2,1,16,8,128]{4,3,2,0,1:T(8,128)} %copy-done.2) | copy-start | bytes 393220
  127.7 77.7 %copy-start.5 = (f32[2,1,16,8,128]{4,3,2,0,1:T(8,128)S(1)}, f32[2,1,16,8,128]{4,3,2,0,1:T(8,128)}, u32[]{:S(2)}) copy-start(f32[2,1,16,8,128]{4,3,2,0,1:T(8,128)} %copy-done.4) | copy-start | bytes 393220
  127.7 79.1 %copy-start.13 = (f32[16,8,128]{2,1,0:T(8,128)S(1)}, f32[16,8,128]{2,1,0:T(8,128)}, u32[]{:S(2)}) copy-start(f32[16,8,128]{2,1,0:T(8,128)} %get-tuple-element.22) | copy-start | bytes 196612
  148.2 22.2 %all-to-all-start.2 = ((f32[2,16,2,3]{3,2,0,1:T(2,128)}), f32[2,16,2,3]{3,2,0,1:T(2,128)S(1)}, u32[]{:S(2)}, u32[]{:S(2)}) async-start(f32[2,16,2,3]{3,2,0,1:T(2,128)} %copy.335), calls=%async_computation.2 | async-start | bytes 65536 | tf_op jit(solution)/shard_map/all_to_all | solution.py:127
  170.3 15.2 %copy-start.14 = (f32[2,16,2,3]{3,2,0,1:T(2,128)}, f32[2,16,2,3]{3,2,0,1:T(2,128)S(1)}, u32[]{:S(2)}) copy-start(f32[2,16,2,3]{3,2,0,1:T(2,128)S(1)} %all-to-all-done.2) | copy-start | bytes 2308
  170.3 11.1 %all-to-all-start.1 = ((f32[2,16,2,3]{3,2,0,1:T(2,128)}), f32[2,16,2,3]{3,2,0,1:T(2,128)S(1)}, u32[]{:S(2)}, u32[]{:S(2)}) async-start(f32[2,16,2,3]{3,2,0,1:T(2,128)} %copy.332), calls=%async_computation.1 | async-start | bytes 65536 | tf_op jit(solution)/shard_map/all_to_all | solution.py:127
  174.4 20.1 %collective-permute-start.16 = (f32[2,2,1,8,128]{4,3,0,2,1:T(8,128)}, f32[2,2,1,8,128]{4,3,0,2,1:T(8,128)}, u32[]{:S(2)}, u32[]{:S(2)}) collective-permute-start(f32[2,2,1,8,128]{4,3,0,2,1:T(8,128)} %slice_bitcast_fusion.32), channel_id=1, source_target_pairs={{16,0},{32,16},{48,32},{64,48},{80,64},{96,80},{112,96},{17,1},{33... | collective-permute-start | bytes 49160 | tf_op jit(solution)/shard_map/ppermute | solution.py:13
  181.4 4.1 %copy-start.15 = (f32[2,16,2,3]{3,2,0,1:T(2,128)}, f32[2,16,2,3]{3,2,0,1:T(2,128)S(1)}, u32[]{:S(2)}) copy-start(f32[2,16,2,3]{3,2,0,1:T(2,128)S(1)} %all-to-all-done.1) | copy-start | bytes 2308
  181.4 11.7 %all-to-all-start = ((f32[2,16,2,3]{3,2,0,1:T(2,128)}), f32[2,16,2,3]{3,2,0,1:T(2,128)}, u32[]{:S(2)}, u32[]{:S(2)}) async-start(f32[2,16,2,3]{3,2,0,1:T(2,128)} %copy.329), calls=%async_computation | async-start | bytes 65536 | tf_op jit(solution)/shard_map/all_to_all | solution.py:127
  185.6 87.0 %all-reduce.25.cloned.1.call-start = ((), (), s32[]{:S(2)}) async-start(), calls=%async_computation.3 | async-start | bytes 131072 | tf_op jit(solution)/shard_map/psum | solution.py:144
  187.1 8.2 %collective-permute-start.17 = (f32[2,2,16,1,128]{4,3,2,0,1:T(1,128)}, f32[2,2,16,1,128]{4,3,2,0,1:T(1,128)}, u32[]{:S(2)}, u32[]{:S(2)}) collective-permute-start(f32[2,2,16,1,128]{4,3,2,0,1:T(1,128)} %slice.713), channel_id=1, source_target_pairs={{1,0},{2,1},{3,2},{4,3},{5,4},{6,5},{7,6},{8,7},{9,8},{10,9},{11,1... | collective-permute-start | bytes 98312 | tf_op jit(solution)/shard_map/ppermute | solution.py:13
  197.3 6.9 %collective-permute-start.18 = (f32[2,2,1,8,128]{4,3,0,2,1:T(8,128)S(1)}, f32[2,2,1,8,128]{4,3,0,2,1:T(8,128)S(1)}, u32[]{:S(2)}, u32[]{:S(2)}) collective-permute-start(f32[2,2,1,8,128]{4,3,0,2,1:T(8,128)S(1)} %copy.355), channel_id=1, source_target_pairs={{0,16},{16,32},{32,48},{48,64},{64,80},{80,96},{96,112},{1,17},{17... | collective-permute-start | bytes 49160 | tf_op jit(solution)/shard_map/ppermute | solution.py:13
  202.0 3.2 %collective-permute-start.19 = (f32[2,2,16,1,128]{4,3,2,1,0:T(1,128)S(1)}, f32[2,2,16,1,128]{4,3,2,1,0:T(1,128)S(1)}, u32[]{:S(2)}, u32[]{:S(2)}) collective-permute-start(f32[2,2,16,1,128]{4,3,2,1,0:T(1,128)S(1)} %slice.724), channel_id=1, source_target_pairs={{0,1},{1,2},{2,3},{3,4},{4,5},{5,6},{6,7},{7,8},{8,9},{9,10},{10,1... | collective-permute-start | bytes 98312 | tf_op jit(solution)/shard_map/ppermute | solution.py:13
Sparse Core Ops, SparseCore 0:
  207.6 64.9 all-reduce.24
where the time goes:
time: 284 us; the launch traced here: 281 us
  waiting for transfers between devices  82.6 us (29%)
  local copies, waits for them, and re-layouts  78.5 us (28%)
  starting transfers between devices  78.4 us (28%)
  other arithmetic  26.5 us (9%)
  between operations  15 us (5%)
    psum x1, waiting for transfers between devices, per_device(): total = lax.psum(local, 'src')  63.8 us
    ppermute x20, starting transfers between devices, passed_along(): return lax.ppermute(block, axis, route)  56.2 us
    add x3, local copies, waits for them, and re-layouts, per_device(): e_field = decay_use * e_field + gain_use * drive  35.4 us
    all_to_all x3, starting transfers between devices, per_device(): lax.all_to_all(jnp.transpose(placed, (0, 2, 3, 1)), 'lat', split_axis=1,...  22.2 us
    gather x3, local copies, waits for them, and re-layouts, per_device(): sampled = jnp.take(e_field.reshape(groups, 3, -1), cells, axis=2)  20.5 us
    all_to_all x3, waiting for transfers between devices, per_device(): lax.all_to_all(jnp.transpose(placed, (0, 2, 3, 1)), 'lat', split_axis=1,...  14.9 us
    squeeze x27, local copies, waits for them, and re-layouts, component(): return field[..., k, :, :, :]  6.66 us
    another operation x10, other arithmetic, curl_upper(): return jnp.stack([yz - zy, zx - xz, xy - yx], axis=-4)  6.36 us
  transfers between devices with their start and end apart: 24, of which 8 were waited for; matrix products, arithmetic and copies ran while one was open for 25% of the time, Pallas kernels for 0%

commit v1 on v0

v1 whole, which is shorter than its diff:
```python
import functools

import jax
import jax.numpy as jnp
from jax import lax
from jax.experimental import pallas as pl
from jax.experimental.pallas import tpu as pltpu
from jax.sharding import PartitionSpec as P

CC = 0.5
KK = 0.5
ROWS = 24
F32 = jnp.float32
UP = ((0, 3), (3, 2), (5, 2), (7, 1), (8, 2))
DN = ((0, 3), (3, 3), (6, 2), (8, 2), (10, 2))
UP_ROWS = 9
DN_ROWS = 11


def shifted(block, axis, distance):
    n = lax.axis_size(axis)
    route = [(i, i + distance) for i in range(n) if 0 <= i + distance < n]
    return lax.ppermute(block, axis, route)


def lanes():
    return lax.broadcasted_iota(jnp.int32, (ROWS, 128), 1)


def zrow():
    r = lax.broadcasted_iota(jnp.int32, (ROWS, 128), 0)
    return jnp.where(r < 20, r, r - ROWS)


def yp(f):
    return jnp.where(lanes() == 127, 0.0, pltpu.roll(f, 127, 1))


def ym(f):
    return jnp.where(lanes() == 0, 0.0, pltpu.roll(f, 1, 1))


def zp(f):
    return pltpu.roll(f, ROWS - 1, 0)


def zm(f):
    return pltpu.roll(f, 1, 0)


def dpy(f):
    return yp(f) - f


def dpz(f):
    return zp(f) - f


def dmy(f):
    return f - ym(f)


def dmz(f):
    return f - zm(f)


def curl_p(f, nxt):
    fx, fy, fz = f
    return (dpy(fz) - dpz(fy), dpz(fx) - (nxt[2] - fz), (nxt[1] - fy) - dpy(fx))


def curl_m(f, prv):
    fx, fy, fz = f
    return (dmy(fz) - dmz(fy), dmz(fx) - (fz - prv[2]), (fy - prv[1]) - dmy(fx))


def slope(conductivity):
    return 1.0 / (1.0 + KK * conductivity)


def coefs(conductivity, keep):
    inv = slope(conductivity)
    a = jnp.where(keep, (1.0 - KK * conductivity) * inv, 0.0)
    b = jnp.where(keep, CC * inv, 0.0)
    return a, b


def first_row_mask(depth_at):
    return jnp.where((zrow() < 0) & (depth_at == 0), 0.0, 1.0)


def last_row_keep(depth_at, depth_n):
    return jnp.logical_not((zrow() > 15) & (depth_at == depth_n - 1))


def pack_kernel(e, h, le, lh, cond, up, dn, sems):
    copies = []

    def move(src, dst):
        c = pltpu.make_async_copy(src, dst, sems.at[len(copies)])
        c.start()
        copies.append(c)

    for field, ref in enumerate((e, h, le, lh)):
        at, n = UP[field]
        move(ref.at[:, :, pl.ds(0, n * 8)], up.at[:, :, pl.ds(at * 8, n * 8)])
        at, n = DN[field]
        move(ref.at[:, :, pl.ds((16 - n) * 8, n * 8)], dn.at[:, :, pl.ds(at * 8, n * 8)])
    for row in range(2):
        move(cond.at[pl.ds(row * 8, 8)], up.at[0, row, pl.ds((UP_ROWS - 1) * 8, 8)])
        move(cond.at[pl.ds((14 + row) * 8, 8)], dn.at[0, row, pl.ds((DN_ROWS - 1) * 8, 8)])
    for c in copies:
        c.wait()


def pack(e, h, le, lh, cond):
    g = e.shape[0]
    return pl.pallas_call(
        pack_kernel,
        out_shape=(
            jax.ShapeDtypeStruct((g, 3, UP_ROWS * 8, 128), F32),
            jax.ShapeDtypeStruct((g, 3, DN_ROWS * 8, 128), F32),
        ),
        in_specs=[pl.BlockSpec(memory_space=pl.ANY)] * 5,
        out_specs=(pl.BlockSpec(memory_space=pltpu.VMEM),) * 2,
        scratch_shapes=[pltpu.SemaphoreType.DMA((12,))],
        name="pack",
    )(e, h, le, lh, cond)


def halo_tile(up, dn, lead, x, field):
    r = lax.broadcasted_iota(jnp.int32, (8, 128), 0)
    at, _ = UP[field]
    s = min(at, UP_ROWS - 8)
    hi = up[(*lead, pl.ds(s * 8 + x, 8, stride=8), slice(None))]
    if at != s:
        hi = pltpu.roll(hi, (8 - (at - s)) % 8, 0)
    at, n = DN[field]
    s = min(at, DN_ROWS - 8)
    lo = dn[(*lead, pl.ds(s * 8 + x, 8, stride=8), slice(None))]
    turn = (8 - n - (at - s)) % 8
    if turn:
        lo = pltpu.roll(lo, turn, 0)
    return jnp.where(r < 4, hi, lo)


def planes_kernel(
    depth_n, lat_n, e, h, le, lh, cond, up, dn, amp, tow, te, th, tle, tlh, ta, tb, to_lo, to_hi
):
    groups = e.shape[0]
    depth_at = lax.axis_index("depth")
    lat_at = lax.axis_index("lat")
    for g in range(groups):

        def body(c, carry, g=g):
            for field, (src, dst) in enumerate(((e, te), (h, th), (le, tle), (lh, tlh))):
                for x in range(8):
                    dst[g, c, x, 0:8] = src[g, c, pl.ds(x, 8, stride=8), :]
                    dst[g, c, x, 8:16] = src[g, c, pl.ds(64 + x, 8, stride=8), :]
                    dst[g, c, x, 16:24] = halo_tile(up, dn, (g, c), x, field)
            return carry

        lax.fori_loop(0, 3, body, 0)
    keep = last_row_keep(depth_at, depth_n)
    r8 = lax.broadcasted_iota(jnp.int32, (8, 128), 0)
    u0 = up[0, 0, pl.ds((UP_ROWS - 1) * 8, 8), :]
    u1 = up[0, 1, pl.ds((UP_ROWS - 1) * 8, 8), :]
    d0 = dn[0, 0, pl.ds((DN_ROWS - 1) * 8, 8), :]
    d1 = dn[0, 1, pl.ds((DN_ROWS - 1) * 8, 8), :]
    for x in range(8):
        halo = jnp.where(r8 == 0, u0[x : x + 1], 1.0)
        halo = jnp.where(r8 == 1, u1[x : x + 1], halo)
        halo = jnp.where(r8 == 6, d0[x : x + 1], halo)
        halo = jnp.where(r8 == 7, d1[x : x + 1], halo)
        whole = jnp.concatenate(
            [cond[pl.ds(x, 8, stride=8), :], cond[pl.ds(64 + x, 8, stride=8), :], halo], axis=0
        )
        a, b = coefs(whole, keep)
        ta[x] = a
        tb[x] = b
        if x == 0:
            to_lo[groups * 11] = whole
        if x == 7:
            to_hi[groups * 13] = whole
    row_mask = first_row_mask(depth_at)
    z, lane = zrow(), lanes()

    def forward_planes(g, carry):
        s = -CC * row_mask
        cell = tow[g]
        lz = cell // (1024 * lat_n) - depth_at * 16
        lx = cell // 128 % (8 * lat_n) - lat_at * 8
        point = jnp.where((z == lz) & (lane == cell % 128), amp[g, 0], 0.0)

        def e0(x):
            return tuple(te[g, c, x] for c in range(3))

        def h0(x):
            return tuple(th[g, c, x] for c in range(3))

        def step_h(x):
            return tuple(f + s * k for f, k in zip(h0(x), curl_p(e0(x), e0(x + 1))))

        def put(ref, k, value):
            ref[g * (11 if ref is to_lo else 13) + k] = value

        a0, b0, a1, b1 = ta[0], tb[0], ta[1], tb[1]
        f0, f1 = e0(0), e0(1)
        h1 = step_h(0)
        put(to_lo, 0, f0[1])
        put(to_lo, 1, f0[2])
        put(to_lo, 2, a0 * f0[1] + b0 * (dmz(h1[0]) - h1[2]))
        put(to_lo, 3, a0 * f0[2] + b0 * (h1[1] - dmy(h1[0])))
        put(to_lo, 4, h1[0])
        hit = jnp.where(lx == 0, point, 0.0)
        ex = a0 * f0[0] + b0 * (dmy(h1[2]) - dmz(h1[1]) - hit)
        k1 = step_h(1)
        ey1 = a1 * f1[1] + b1 * (dmz(k1[0]) - k1[2] + h1[2])
        ez1 = a1 * f1[2] + b1 * (k1[1] - h1[1] - dmy(k1[0]))
        put(to_lo, 5, h1[1] + s * (dpz(ex) - ez1))
        put(to_lo, 6, h1[2] + s * (ey1 - dpy(ex)))
        a7, b7, a6, b6 = ta[7], tb[7], ta[6], tb[6]
        f7, f6 = e0(7), e0(6)
        g7 = h0(7)
        put(to_hi, 0, g7[1] + s * (dpz(f7[0]) + f7[2]))
        put(to_hi, 1, g7[2] - s * (f7[1] + dpy(f7[0])))
        put(to_hi, 2, f7[0])
        hx7 = g7[0] + s * (dpy(f7[2]) - dpz(f7[1]))
        h6 = step_h(6)
        put(to_hi, 3, a7 * f7[1] + b7 * (dmz(hx7) + h6[2]))
        put(to_hi, 4, a7 * f7[2] - b7 * (h6[1] + dmy(hx7)))
        put(to_hi, 5, hx7)
        h5 = step_h(5)
        m6 = curl_m(h6, h5)
        hit = jnp.where(lx == 6, point, 0.0)
        ex6 = a6 * f6[0] + b6 * (m6[0] - hit)
        ey6 = a6 * f6[1] + b6 * m6[1]
        ez6 = a6 * f6[2] + b6 * m6[2]
        put(to_hi, 6, h6[1] + s * (dpz(ex6) + ez6))
        put(to_hi, 7, h6[2] - s * (ey6 + dpy(ex6)))
        s = row_mask

        def l0(x):
            return tuple(tle[g, c, x] for c in range(3))

        def w0(x):
            return tuple(tb[x] * f for f in l0(x))

        def m0(x):
            return tuple(tlh[g, c, x] for c in range(3))

        def step_m(x):
            return tuple(f + s * k for f, k in zip(m0(x), curl_p(w0(x), w0(x + 1))))

        q0, v0 = l0(0), w0(0)
        m1 = step_m(0)
        put(to_lo, 7, v0[1])
        put(to_lo, 8, v0[2])
        put(to_lo, 9, a0 * q0[1] - CC * (dmz(m1[0]) - m1[2]))
        put(to_lo, 10, a0 * q0[2] - CC * (m1[1] - dmy(m1[0])))
        q7, v7, n7 = l0(7), w0(7), m0(7)
        put(to_hi, 8, n7[1] + s * (dpz(v7[0]) + v7[2]))
        put(to_hi, 9, n7[2] - s * (v7[1] + dpy(v7[0])))
        put(to_hi, 10, q7[0])
        mx7 = n7[0] + s * (dpy(v7[2]) - dpz(v7[1]))
        m6 = step_m(6)
        put(to_hi, 11, a7 * q7[1] - CC * (dmz(mx7) + m6[2]))
        put(to_hi, 12, a7 * q7[2] + CC * (m6[1] + dmy(mx7)))
        return carry

    lax.fori_loop(0, groups, forward_planes, 0)


def planes(e, h, le, lh, cond, up, dn, amp, tow, depth_n, lat_n):
    g = e.shape[0]
    vm = pl.BlockSpec(memory_space=pltpu.VMEM)
    sm = pl.BlockSpec(memory_space=pltpu.SMEM)
    field = jax.ShapeDtypeStruct((g, 3, 8, ROWS, 128), F32)
    coef = jax.ShapeDtypeStruct((8, ROWS, 128), F32)
    return pl.pallas_call(
        functools.partial(planes_kernel, depth_n, lat_n),
        out_shape=(
            field,
            field,
            field,
            field,
            coef,
            coef,
            jax.ShapeDtypeStruct((g * 11 + 1, ROWS, 128), F32),
            jax.ShapeDtypeStruct((g * 13 + 1, ROWS, 128), F32),
        ),
        in_specs=[vm] * 7 + [sm] * 2,
        out_specs=(vm,) * 8,
        compiler_params=pltpu.CompilerParams(vmem_limit_bytes=40 * 1024 * 1024),
        name="planes",
    )(e, h, le, lh, cond, up, dn, amp, tow)


def march_kernel(
    depth_n,
    lat_n,
    te,
    th,
    tle,
    tlh,
    ta,
    tb,
    cond,
    lo,
    hi,
    amp,
    tow,
    rcell,
    rowner,
    grad,
    send,
    ee,
    hh,
    ww,
    mm,
    l1,
    l2,
    acc,
    samp,
    count,
):
    groups = te.shape[0]
    depth_at = lax.axis_index("depth")
    lat_at = lax.axis_index("lat")
    row_mask = first_row_mask(depth_at)
    z, lane = zrow(), lanes()
    keep = last_row_keep(depth_at, depth_n)
    a8, b8 = coefs(hi[groups * 11], keep & (lat_at < lat_n - 1))
    al, bl = coefs(lo[groups * 13], keep)
    left = jnp.where(lat_at == 0, 0.0, 1.0)
    receivers = rcell.shape[0]

    def get(ref, g, x):
        return tuple(ref[g, c, x] for c in range(3))

    def put(ref, g, x, value):
        for c in range(3):
            ref[g, c, x] = value[c]

    def update_h(g, s, w, m):
        def body(x, carry):
            k = curl_p(get(w, g, x), get(w, g, x + 1))
            for c in range(3):
                m[g, c, x + 1] = m[g, c, x + 1] + s * k[c]
            return carry

        lax.fori_loop(0, 8, body, 0)

    def copy_in(g, carry):
        for c in range(3):
            for x in range(8):
                ee[g, c, x] = te[g, c, x]
                hh[g, c, x + 1] = th[g, c, x]
                mm[g, c, x + 1] = tlh[g, c, x]
                ww[g, c, x] = tb[x] * tle[g, c, x]
        return carry

    lax.fori_loop(0, groups, copy_in, 0)
    acc[...] = jnp.zeros_like(acc)

    def adjoint(g, carry):
        s = row_mask
        p, n = g * 11 + 7, g * 13 + 8
        ww[g, 1, 8] = hi[p]
        ww[g, 2, 8] = hi[p + 1]
        update_h(g, s, ww, mm)
        my = left * (lo[n] - s * ww[g, 2, 0])
        mz = left * (lo[n + 1] + s * ww[g, 1, 0])
        mm[g, 1, 0] = my
        mm[g, 2, 0] = mz

        def first(x, c0):
            k = curl_m(get(mm, g, x + 1), (None, mm[g, 1, x], mm[g, 2, x]))
            for c in range(3):
                new = ta[x] * tle[g, c, x] - CC * k[c]
                l1[g, c, x] = new
                ww[g, c, x] = tb[x] * new
            return c0

        lax.fori_loop(0, 8, first, 0)
        ww[g, 1, 8] = b8 * (hi[p + 2] - CC * mm[g, 2, 8])
        ww[g, 2, 8] = b8 * (hi[p + 3] + CC * mm[g, 1, 8])
        wx = bl * (al * lo[n + 2] - CC * (dmy(mz) - dmz(my)))
        wy = bl * (lo[n + 3] + CC * mz)
        wz = bl * (lo[n + 4] - CC * my)
        mm[g, 1, 0] = left * (my + s * (dpz(wx) - (ww[g, 2, 0] - wz)))
        mm[g, 2, 0] = left * (mz + s * ((ww[g, 1, 0] - wy) - dpy(wx)))
        update_h(g, s, ww, mm)

        def second(x, c0):
            k = curl_m(get(mm, g, x + 1), (None, mm[g, 1, x], mm[g, 2, x]))
            for c in range(3):
                l2[g, c, x] = ta[x] * l1[g, c, x] - CC * k[c]
            return c0

        lax.fori_loop(0, 8, second, 0)
        return carry

    lax.fori_loop(0, groups, adjoint, 0)

    def forward(g, carry):
        s = -CC * row_mask
        p, n = g * 11, g * 13
        cell = tow[g]
        lz = cell // (1024 * lat_n) - depth_at * 16
        lx = cell // 128 % (8 * lat_n) - lat_at * 8
        point = jnp.where((z == lz) & (lane == cell % 128), 1.0, 0.0)

        def update_e(step, weight):
            def body(x, c0):
                old = get(ee, g, x)
                k = curl_m(get(hh, g, x + 1), (None, hh[g, 1, x], hh[g, 2, x]))
                k = (k[0] - jnp.where(lx == x, amp[g, step], 0.0) * point, k[1], k[2])
                a, b = ta[x], tb[x]
                total = None
                for c in range(3):
                    t = (-2.0 * KK * old[c][0:16] - CC * KK * k[c][0:16]) * weight[g, c, x, 0:16]
                    total = t if total is None else total + t
                    ee[g, c, x] = a * old[c] + b * k[c]
                acc[x] += total
                return c0

            lax.fori_loop(0, 8, body, 0)

        def sample(step):
            def body(r, c0):
                cell_r = rcell[r]
                zr, xr, yr = cell_r // 1024, cell_r // 128 % 8, cell_r % 128
                one = lax.broadcasted_iota(jnp.int32, (1, 128), 1)
                for c in range(3):
                    row = ee[g, c, xr, pl.ds(zr, 1), :]
                    samp[r, pl.ds(g * 9 + 3 * step + c, 1), :] = jnp.where(one == yr, row, 0.0)
                return c0

            lax.fori_loop(0, receivers, body, 0)

        ee[g, 1, 8] = hi[p]
        ee[g, 2, 8] = hi[p + 1]
        hy = left * (lo[n] - s * ee[g, 2, 0])
        hz = left * (lo[n + 1] + s * ee[g, 1, 0])
        hh[g, 1, 0] = hy
        hh[g, 2, 0] = hz
        update_h(g, s, ee, hh)
        update_e(0, l2)
        sample(0)
        ey8 = hi[p + 2] + b8 * hh[g, 2, 8]
        ez8 = hi[p + 3] - b8 * hh[g, 1, 8]
        ee[g, 1, 8] = ey8
        ee[g, 2, 8] = ez8
        hit = jnp.where(lx == -1, amp[g, 0], 0.0) * point
        ex = al * lo[n + 2] + bl * (dmy(hz) - dmz(hy) - hit)
        ey = lo[n + 3] - bl * hz
        ez = lo[n + 4] + bl * hy
        hy2 = left * (hy + s * (dpz(ex) - (ee[g, 2, 0] - ez)))
        hz2 = left * (hz + s * ((ee[g, 1, 0] - ey) - dpy(ex)))
        hh[g, 1, 0] = hy2
        hh[g, 2, 0] = hz2
        update_h(g, s, ee, hh)
        update_e(1, l1)
        sample(1)
        gx = hi[p + 4] + s * (dpy(ez8) - dpz(ey8))
        gy = hi[p + 5] + s * ez8
        gz = hi[p + 6] - s * ey8
        ee[g, 1, 8] = a8 * ey8 + b8 * (dmz(gx) - gz + hh[g, 2, 8])
        ee[g, 2, 8] = a8 * ez8 + b8 * (gy - hh[g, 1, 8] - dmy(gx))
        hx2 = lo[n + 5] + s * (dpy(ez) - dpz(ey))
        hit = jnp.where(lx == -1, amp[g, 1], 0.0) * point
        hyf = lo[n + 6] - s * ez
        hzf = lo[n + 7] + s * ey
        ex2 = al * ex + bl * (dmy(hz2) - dmz(hy2) - hit)
        ey2 = al * ey + bl * (dmz(hx2) - hz2 + hzf)
        ez2 = al * ez + bl * (hy2 - hyf - dmy(hx2))
        hh[g, 1, 0] = left * (hy2 + s * (dpz(ex2) - (ee[g, 2, 0] - ez2)))
        hh[g, 2, 0] = left * (hz2 + s * ((ee[g, 1, 0] - ey2) - dpy(ex2)))
        update_h(g, s, ee, hh)
        update_e(2, tle)
        sample(2)
        return carry

    lax.fori_loop(0, groups, forward, 0)
    for x in range(8):
        for half in range(2):
            c = cond[pl.ds(half * 64 + x, 8, stride=8), :]
            inv = slope(c)
            grad[pl.ds(half * 64 + x, 8, stride=8), :] = acc[x, half * 8 : half * 8 + 8] * inv * inv
    send[...] = jnp.zeros_like(send)
    for o in range(send.shape[0]):
        count[o] = 0
    r24 = lax.broadcasted_iota(jnp.int32, (ROWS, 128), 0)

    def place(r, c0):
        o = rowner[r]
        slot = count[o]
        count[o] = slot + 1
        values = jnp.sum(samp[r], axis=-1, keepdims=True)
        used = (r24 == lane) & (r24 < groups * 9)
        row = jnp.sum(jnp.where(used, values, 0.0), axis=0, keepdims=True)
        send[o, pl.ds(slot, 1), :] = row
        return c0

    lax.fori_loop(0, receivers, place, 0)


def march(te, th, tle, tlh, ta, tb, cond, lo, hi, amp, tow, rcell, rowner, depth_n, lat_n):
    g = te.shape[0]
    vm = pl.BlockSpec(memory_space=pltpu.VMEM)
    sm = pl.BlockSpec(memory_space=pltpu.SMEM)
    return pl.pallas_call(
        functools.partial(march_kernel, depth_n, lat_n),
        out_shape=(
            jax.ShapeDtypeStruct((128, 128), F32),
            jax.ShapeDtypeStruct((lat_n, 8, 128), F32),
        ),
        in_specs=[vm] * 9 + [sm] * 4,
        out_specs=(vm,) * 2,
        scratch_shapes=[pltpu.VMEM((g, 3, 9, ROWS, 128), F32)] * 4
        + [pltpu.VMEM((g, 3, 8, ROWS, 128), F32)] * 2
        + [
            pltpu.VMEM((8, 16, 128), F32),
            pltpu.VMEM((rcell.shape[0], ROWS, 128), F32),
            pltpu.SMEM((lat_n,), jnp.int32),
        ],
        compiler_params=pltpu.CompilerParams(vmem_limit_bytes=40 * 1024 * 1024),
        name="march",
    )(te, th, tle, tlh, ta, tb, cond, lo, hi, amp, tow, rcell, rowner)


def src_sum(value):
    n = lax.axis_size("src")
    step = 1
    while step < n:
        value = value + lax.ppermute(value, "src", [(i, i ^ step) for i in range(n)])
        step *= 2
    return value


def per_device(
    conductivity, e_start, h_start, e_weight, h_weight, source_amp, tow_cell, rec_cell, rec_owner
):
    groups = e_start.shape[0]
    depth_n, lat_n = lax.axis_size("depth"), lax.axis_size("lat")

    def flat(f):
        return f.reshape(groups, 3, 128, 128)

    e, h, le, lh = flat(e_start), flat(h_start), flat(e_weight), flat(h_weight)
    cond = conductivity.reshape(128, 128)
    up, dn = pack(e, h, le, lh, cond)
    up = shifted(up, "depth", -1)
    dn = shifted(dn, "depth", 1)
    te, th, tle, tlh, ta, tb, to_lo, to_hi = planes(
        e, h, le, lh, cond, up, dn, source_amp, tow_cell, depth_n, lat_n
    )
    hi = shifted(to_lo, "lat", -1)
    lo = shifted(to_hi, "lat", 1)
    grad, send = march(
        te,
        th,
        tle,
        tlh,
        ta,
        tb,
        cond,
        lo,
        hi,
        source_amp,
        tow_cell,
        rec_cell.reshape(-1),
        rec_owner.reshape(-1),
        depth_n,
        lat_n,
    )
    got = lax.all_to_all(send, "lat", split_axis=0, concat_axis=0, tiled=True)
    total = src_sum(grad).reshape(16, 8, 128)
    lines = got[:, 0:2, 0 : groups * 9].reshape(lat_n, 2, groups, 9)
    lines = jnp.transpose(lines, (2, 0, 1, 3)).reshape(groups, 1, 1, lat_n, 2, 9)
    return (total, lines)


def solution(mesh):
    placed = (
        P("depth", "lat", None),
        P("src", None, "depth", "lat", None),
        P("src", None, "depth", "lat", None),
        P("src", None, "depth", "lat", None),
        P("src", None, "depth", "lat", None),
        P("src", None),
        P("src"),
        P("depth", "lat", None),
        P("depth", "lat", None, None),
    )
    return jax.shard_map(
        per_device,
        mesh=mesh,
        in_specs=placed,
        out_specs=(P("depth", "lat", None), P("src", "depth", "lat", None, None, None)),
        check_vma=False,
    )
```

time: 284 us -> 79.7 us (0.28)
  the two profiles are of different devices: /device:TPU:1 before, /device:TPU:28 now
where the time goes in v1:
time: 79.7 us; the launch traced here: 79.3 us
  starting transfers between devices  29.2 us (37%)
  waiting for transfers between devices  25.5 us (32%)
  Pallas kernels  21.8 us (27%)
  local copies, waits for them, and re-layouts  1.41 us (2%)
  between operations  0.82 us (1%)
    ppermute x4, waiting for transfers between devices, shifted(): return lax.ppermute(block, axis, route)  18.9 us
    pallas_call x1, Pallas kernels, march(): pl.pallas_call(functools.partial(march_kernel, depth_n, lat_n), out_shape...  18.3 us
    all_to_all x1, starting transfers between devices, per_device(): got = lax.all_to_all(send, 'lat', split_axis=0, concat_axis=0, tiled=True)  13.8 us
    ppermute x4, starting transfers between devices, shifted(): return lax.ppermute(block, axis, route)  11 us
    all_to_all x1, waiting for transfers between devices, per_device(): got = lax.all_to_all(send, 'lat', split_axis=0, concat_axis=0, tiled=True)  6.6 us
    ppermute x2, starting transfers between devices, src_sum(): lax.ppermute(value, 'src', [(i, i ^ step) for i in range(n)])  4.32 us
    pallas_call x1, Pallas kernels, pack(): pl.pallas_call(pack_kernel, out_shape=(jax.ShapeDtypeStruct((g, 3, UP_ROW...  1.99 us
  transfers between devices with their start and end apart: 7, of which 4 were waited for; matrix products, arithmetic and copies ran while one was open for 1% of the time, Pallas kernels for 0%

profile of v1, /device:TPU:28, one launch (start us, length us, event | category | flops | bytes accessed | tf_op | source)
XLA Modules:
  0.0 79.3 jit_solution(14925563341619185895)
XLA Ops:
  0.6 0.0 copy-start
  0.6 0.0 copy-start.1
  0.7 0.0 copy-start.2
  0.7 0.0 copy-start.3
  0.7 0.0 copy-start.4
  0.7 2.0 %pack.1 = (f32[2,3,72,128]{3,2,1,0:T(8,128)}, f32[2,3,88,128]{3,2,1,0:T(8,128)}) custom-call(f32[2,3,128,128]{3,2,1,0:T(8,128)} %bitcast.16, f32[2,3,128,128]{3,2,1,0:T(8,128)} %bitcast.18, f32[2,3,128,128]{3,2,1,0:T(8,128)} %bitcast.20, f32[2,3,128,128]{3,2,1,0:T(8,128)} %bitcast.22, f32[128,128]{1,0:T(8,128)} %bitcast.24), custom_call_target="tpu_custom_call" | custom-call | tf_op jit(solution)/shard_map/pack/pallas_call | solution.py:118
  2.7 0.0 copy-start.5
  2.7 0.0 copy-start.6
  2.7 4.7 %collective-permute-start.1 = (f32[2,3,88,128]{3,2,1,0:T(8,128)}, f32[2,3,88,128]{3,2,1,0:T(8,128)S(1)}, u32[]{:S(2)}, u32[]{:S(2)}) collective-permute-start(f32[2,3,88,128]{3,2,1,0:T(8,128)} %get-tuple-element.15), channel_id=1, source_target_pairs={{0,16},{16,32},{32,48},{48,64},{64,80},{80,96},{96,112},{1,17},{17... | collective-permute-start | bytes 811016 | tf_op jit(solution)/shard_map/ppermute | solution.py:23
  7.4 1.9 %collective-permute-start = (f32[2,3,72,128]{3,2,1,0:T(8,128)}, f32[2,3,72,128]{3,2,1,0:T(8,128)S(1)}, u32[]{:S(2)}, u32[]{:S(2)}) collective-permute-start(f32[2,3,72,128]{3,2,1,0:T(8,128)} %get-tuple-element.14), channel_id=1, source_target_pairs={{16,0},{32,16},{48,32},{64,48},{80,64},{96,80},{112,96},{17,1},{33... | collective-permute-start | bytes 663560 | tf_op jit(solution)/shard_map/ppermute | solution.py:23
  9.3 8.3 %collective-permute-done.up = f32[2,3,72,128]{3,2,1,0:T(8,128)S(1)} collective-permute-done((f32[2,3,72,128]{3,2,1,0:T(8,128)}, f32[2,3,72,128]{3,2,1,0:T(8,128)S(1)}, u32[]{:S(2)}, u32[]{:S(2)}) %collective-permute-start) | collective-permute-done | bytes 221216 | tf_op jit(solution)/shard_map/ppermute | solution.py:23
  17.6 0.0 collective-permute-done.1.dn
  17.6 0.0 copy-done
  17.6 0.0 copy-done.1
  17.6 0.0 copy-done.2
  17.6 0.0 copy-done.3
  17.6 0.0 copy-done.4
  17.6 0.0 copy-done.5
  17.7 0.0 copy-done.6
  17.7 1.6 %planes.1 = (f32[2,3,8,24,128]{4,3,2,1,0:T(8,128)S(1)}, f32[2,3,8,24,128]{4,3,2,1,0:T(8,128)S(1)}, f32[2,3,8,24,128]{4,3,2,1,0:T(8,128)S(1)}, f32[2,3,8,24,128]{...) custom-call(f32[2,3,128,128]{3,2,1,0:T(8,128)S(1)} %bitcast.17, ...), custom_call_target="tpu_custom_call" | custom-call | tf_op jit(solution)/shard_map/planes/pallas_call | solution.py:280
  19.2 3.1 %collective-permute-start.2 = (f32[27,24,128]{2,1,0:T(8,128)S(1)}, f32[27,24,128]{2,1,0:T(8,128)S(1)}, u32[]{:S(2)}, u32[]{:S(2)}) collective-permute-start(f32[27,24,128]{2,1,0:T(8,128)S(1)} %get-tuple-element.22), channel_id=1, source_target_pairs={{0,1},{1,2},{2,3},{3,4},{4,5},{5,6},{6,7},{7,8},{8,9},{9,10},{10,1... | collective-permute-start | bytes 995336 | tf_op jit(solution)/shard_map/ppermute | solution.py:23
  22.4 1.3 %collective-permute-start.3 = (f32[23,24,128]{2,1,0:T(8,128)S(1)}, f32[23,24,128]{2,1,0:T(8,128)S(1)}, u32[]{:S(2)}, u32[]{:S(2)}) collective-permute-start(f32[23,24,128]{2,1,0:T(8,128)S(1)} %get-tuple-element.23), channel_id=1, source_target_pairs={{1,0},{2,1},{3,2},{4,3},{5,4},{6,5},{7,6},{8,7},{9,8},{10,9},{11,1... | collective-permute-start | bytes 847880 | tf_op jit(solution)/shard_map/ppermute | solution.py:23
  23.7 8.5 %collective-permute-done.3.hi = f32[23,24,128]{2,1,0:T(8,128)S(1)} collective-permute-done((f32[23,24,128]{2,1,0:T(8,128)S(1)}, f32[23,24,128]{2,1,0:T(8,128)S(1)}, u32[]{:S(2)}, u32[]{:S(2)}) %collective-permute-start.3) | collective-permute-done | bytes 282656 | tf_op jit(solution)/shard_map/ppermute | solution.py:23
  32.2 2.1 %collective-permute-done.2.lo = f32[27,24,128]{2,1,0:T(8,128)S(1)} collective-permute-done((f32[27,24,128]{2,1,0:T(8,128)S(1)}, f32[27,24,128]{2,1,0:T(8,128)S(1)}, u32[]{:S(2)}, u32[]{:S(2)}) %collective-permute-start.2) | collective-permute-done | bytes 331808 | tf_op jit(solution)/shard_map/ppermute | solution.py:23
  34.3 0.0 copy-start.7
  34.3 0.0 copy-start.8
  34.3 0.7 copy-done.7
  34.9 0.0 copy-done.8
  34.9 18.3 %march.1 = (f32[128,128]{1,0:T(8,128)S(1)}, f32[16,8,128]{2,1,0:T(8,128)}) custom-call(f32[2,3,8,24,128]{4,3,2,1,0:T(8,128)S(1)} %get-tuple-element.16.te, f32[2,3,8,24,128]{4,3,2,1,0:T(8,128)S(1)} %get-tuple-element.17.th, f32[2,3,8,24,128]{4,3,2,1,0:T(8,128)S(1)} %get-tuple-element.18.tle, f32[2,3,8,24,128]{4,3,2,1,0:T(8,128)S(1)} %get-tuple-element.19.tlh, ...), custom_call_target="tpu_custom_call" | custom-call | tf_op jit(solution)/shard_map/march/pallas_call | solution.py:513
  53.2 1.9 %collective-permute-start.4 = (f32[128,128]{1,0:T(8,128)S(1)}, f32[128,128]{1,0:T(8,128)S(1)}, u32[]{:S(2)}, u32[]{:S(2)}) collective-permute-start(f32[128,128]{1,0:T(8,128)S(1)} %get-tuple-element.24), channel_id=1, source_target_pairs={{0,128},{128,0},{256,384},{384,256},{1,129},{129,1},{257,385},{385... | collective-permute-start | bytes 196616 | tf_op jit(solution)/shard_map/ppermute | solution.py:537
  55.1 13.8 %all-to-all-start = ((f32[16,8,128]{2,1,0:T(8,128)}), f32[16,8,128]{2,1,0:T(8,128)S(1)}, u32[]{:S(2)}, u32[]{:S(2)}) async-start(f32[16,8,128]{2,1,0:T(8,128)} %get-tuple-element.25), calls=%async_computation | async-start | bytes 131072 | tf_op jit(solution)/shard_map/all_to_all | solution.py:578
  68.9 0.0 collective-permute-done.4
  69.0 2.4 %collective-permute-start.5 = (f32[128,128]{1,0:T(8,128)S(1)}, f32[128,128]{1,0:T(8,128)S(1)}, u32[]{:S(2)}, u32[]{:S(2)}) collective-permute-start(f32[128,128]{1,0:T(8,128)S(1)} %add.6), channel_id=1, source_target_pairs={{0,256},{128,384},{256,0},{384,128},{1,257},{129,385},{257,1},{385... | collective-permute-start | bytes 196616 | tf_op jit(solution)/shard_map/ppermute | solution.py:537
  71.4 6.6 %all-to-all-done = f32[16,8,128]{2,1,0:T(8,128)S(1)} async-done(((f32[16,8,128]{2,1,0:T(8,128)}), f32[16,8,128]{2,1,0:T(8,128)S(1)}, u32[]{:S(2)}, u32[]{:S(2)}) %all-to-all-start) | async-done | bytes 65568 | tf_op jit(solution)/shard_map/all_to_all | solution.py:578
  78.0 0.7 copy.12
  78.7 0.0 collective-permute-done.5
  78.7 0.6 add_bitcast_fusion
  (2 shorter events, 0.0 us)
Async XLA Ops:
  0.6 17.0 %copy-start = (f32[2,3,16,8,128]{4,3,2,1,0:T(8,128)S(1)}, f32[2,3,16,8,128]{4,3,2,1,0:T(8,128)}, u32[]{:S(2)}) copy-start(f32[2,3,16,8,128]{4,3,2,1,0:T(8,128)} %param.10) | copy-start | bytes 1179652
  0.6 17.0 %copy-start.1 = (f32[2,3,16,8,128]{4,3,2,1,0:T(8,128)S(1)}, f32[2,3,16,8,128]{4,3,2,1,0:T(8,128)}, u32[]{:S(2)}) copy-start(f32[2,3,16,8,128]{4,3,2,1,0:T(8,128)} %param.11) | copy-start | bytes 1179652
  0.7 17.0 %copy-start.2 = (f32[2,3,16,8,128]{4,3,2,1,0:T(8,128)S(1)}, f32[2,3,16,8,128]{4,3,2,1,0:T(8,128)}, u32[]{:S(2)}) copy-start(f32[2,3,16,8,128]{4,3,2,1,0:T(8,128)} %param.12) | copy-start | bytes 1179652
  0.7 17.0 %copy-start.3 = (f32[2,3,16,8,128]{4,3,2,1,0:T(8,128)S(1)}, f32[2,3,16,8,128]{4,3,2,1,0:T(8,128)}, u32[]{:S(2)}) copy-start(f32[2,3,16,8,128]{4,3,2,1,0:T(8,128)} %param.13) | copy-start | bytes 1179652
  0.7 17.0 %copy-start.4 = (f32[16,8,128]{2,1,0:T(8,128)S(1)}, f32[16,8,128]{2,1,0:T(8,128)}, u32[]{:S(2)}) copy-start(f32[16,8,128]{2,1,0:T(8,128)} %param.9) | copy-start | bytes 196612
  2.7 15.0 %copy-start.5 = (f32[2,3]{1,0:T(2,128)S(1)}, f32[2,3]{1,0:T(2,128)}, u32[]{:S(2)}) copy-start(f32[2,3]{1,0:T(2,128)} %amp.3) | copy-start | bytes 76
  2.7 15.0 %copy-start.6 = (s32[2]{0:T(128)S(1)}, s32[2]{0:T(128)}, u32[]{:S(2)}) copy-start(s32[2]{0:T(128)} %tow.3) | copy-start | bytes 28
  2.7 14.9 %collective-permute-start.1 = (f32[2,3,88,128]{3,2,1,0:T(8,128)}, f32[2,3,88,128]{3,2,1,0:T(8,128)S(1)}, u32[]{:S(2)}, u32[]{:S(2)}) collective-permute-start(f32[2,3,88,128]{3,2,1,0:T(8,128)} %get-tuple-element.15), channel_id=1, source_target_pairs={{0,16},{16,32},{32,48},{48,64},{64,80},{80,96},{96,112},{1,17},{17... | collective-permute-start | bytes 811016 | tf_op jit(solution)/shard_map/ppermute | solution.py:23
  7.4 10.2 %collective-permute-start = (f32[2,3,72,128]{3,2,1,0:T(8,128)}, f32[2,3,72,128]{3,2,1,0:T(8,128)S(1)}, u32[]{:S(2)}, u32[]{:S(2)}) collective-permute-start(f32[2,3,72,128]{3,2,1,0:T(8,128)} %get-tuple-element.14), channel_id=1, source_target_pairs={{16,0},{32,16},{48,32},{64,48},{80,64},{96,80},{112,96},{17,1},{33... | collective-permute-start | bytes 663560 | tf_op jit(solution)/shard_map/ppermute | solution.py:23
  19.2 15.0 %collective-permute-start.2 = (f32[27,24,128]{2,1,0:T(8,128)S(1)}, f32[27,24,128]{2,1,0:T(8,128)S(1)}, u32[]{:S(2)}, u32[]{:S(2)}) collective-permute-start(f32[27,24,128]{2,1,0:T(8,128)S(1)} %get-tuple-element.22), channel_id=1, source_target_pairs={{0,1},{1,2},{2,3},{3,4},{4,5},{5,6},{6,7},{7,8},{8,9},{9,10},{10,1... | collective-permute-start | bytes 995336 | tf_op jit(solution)/shard_map/ppermute | solution.py:23
  22.4 9.8 %collective-permute-start.3 = (f32[23,24,128]{2,1,0:T(8,128)S(1)}, f32[23,24,128]{2,1,0:T(8,128)S(1)}, u32[]{:S(2)}, u32[]{:S(2)}) collective-permute-start(f32[23,24,128]{2,1,0:T(8,128)S(1)} %get-tuple-element.23), channel_id=1, source_target_pairs={{1,0},{2,1},{3,2},{4,3},{5,4},{6,5},{7,6},{8,7},{9,8},{10,9},{11,1... | collective-permute-start | bytes 847880 | tf_op jit(solution)/shard_map/ppermute | solution.py:23
  34.3 0.7 copy-start.7
  34.3 0.7 copy-start.8
  53.2 15.7 %collective-permute-start.4 = (f32[128,128]{1,0:T(8,128)S(1)}, f32[128,128]{1,0:T(8,128)S(1)}, u32[]{:S(2)}, u32[]{:S(2)}) collective-permute-start(f32[128,128]{1,0:T(8,128)S(1)} %get-tuple-element.24), channel_id=1, source_target_pairs={{0,128},{128,0},{256,384},{384,256},{1,129},{129,1},{257,385},{385... | collective-permute-start | bytes 196616 | tf_op jit(solution)/shard_map/ppermute | solution.py:537
  55.1 22.9 %all-to-all-start = ((f32[16,8,128]{2,1,0:T(8,128)}), f32[16,8,128]{2,1,0:T(8,128)S(1)}, u32[]{:S(2)}, u32[]{:S(2)}) async-start(f32[16,8,128]{2,1,0:T(8,128)} %get-tuple-element.25), calls=%async_computation | async-start | bytes 131072 | tf_op jit(solution)/shard_map/all_to_all | solution.py:578
  69.0 9.7 %collective-permute-start.5 = (f32[128,128]{1,0:T(8,128)S(1)}, f32[128,128]{1,0:T(8,128)S(1)}, u32[]{:S(2)}, u32[]{:S(2)}) collective-permute-start(f32[128,128]{1,0:T(8,128)S(1)} %add.6), channel_id=1, source_target_pairs={{0,256},{128,384},{256,0},{384,128},{1,257},{129,385},{257,1},{385... | collective-permute-start | bytes 196616 | tf_op jit(solution)/shard_map/ppermute | solution.py:537

commit v2 on v1

v2 whole, which is shorter than its diff:
```python
import functools

import jax
import jax.numpy as jnp
from jax import lax
from jax.experimental import pallas as pl
from jax.experimental.pallas import tpu as pltpu
from jax.sharding import PartitionSpec as P

CC = 0.5
KK = 0.5
ROWS = 24
F32 = jnp.float32
UP = ((0, 3), (3, 2), (5, 2), (7, 1), (8, 2))
DN = ((0, 3), (3, 3), (6, 2), (8, 2), (10, 2))
UP_ROWS = 9
DN_ROWS = 11


def shifted(block, axis, distance):
    n = lax.axis_size(axis)
    route = [(i, i + distance) for i in range(n) if 0 <= i + distance < n]
    return lax.ppermute(block, axis, route)


def swapped(block, axis, first):
    n = lax.axis_size(axis)
    lower = range(first, n - 1, 2)
    return lax.ppermute(block, axis, [p for i in lower for p in ((i, i + 1), (i + 1, i))])


def lanes():
    return lax.broadcasted_iota(jnp.int32, (ROWS, 128), 1)


def zrow():
    r = lax.broadcasted_iota(jnp.int32, (ROWS, 128), 0)
    return jnp.where(r < 20, r, r - ROWS)


def yp(f):
    return jnp.where(lanes() == 127, 0.0, pltpu.roll(f, 127, 1))


def ym(f):
    return jnp.where(lanes() == 0, 0.0, pltpu.roll(f, 1, 1))


def zp(f):
    return pltpu.roll(f, ROWS - 1, 0)


def zm(f):
    return pltpu.roll(f, 1, 0)


def dpy(f):
    return yp(f) - f


def dpz(f):
    return zp(f) - f


def dmy(f):
    return f - ym(f)


def dmz(f):
    return f - zm(f)


def curl_p(f, nxt):
    fx, fy, fz = f
    return (dpy(fz) - dpz(fy), dpz(fx) - (nxt[2] - fz), (nxt[1] - fy) - dpy(fx))


def curl_m(f, prv):
    fx, fy, fz = f
    return (dmy(fz) - dmz(fy), dmz(fx) - (fz - prv[2]), (fy - prv[1]) - dmy(fx))


def coefs(conductivity, keep):
    inv = 1.0 / (1.0 + KK * conductivity)
    a = jnp.where(keep, (1.0 - KK * conductivity) * inv, 0.0)
    b = jnp.where(keep, CC * inv, 0.0)
    return a, b


def first_row_mask(depth_at):
    return jnp.where((zrow() < 0) & (depth_at == 0), 0.0, 1.0)


def last_row_keep(depth_at, depth_n):
    return jnp.logical_not((zrow() > 15) & (depth_at == depth_n - 1))


def pack_kernel(e, h, le, lh, cond, one, two, sems):
    even = lax.axis_index("depth") % 2 == 0

    def fill(up, dn):
        copies = []

        def move(src, dst):
            c = pltpu.make_async_copy(src, dst, sems.at[len(copies)])
            c.start()
            copies.append(c)

        for field, ref in enumerate((e, h, le, lh)):
            at, n = UP[field]
            move(ref.at[:, :, pl.ds(0, n * 8)], up.at[:, :, pl.ds(at * 8, n * 8)])
            at, n = DN[field]
            move(ref.at[:, :, pl.ds((16 - n) * 8, n * 8)], dn.at[:, :, pl.ds(at * 8, n * 8)])
        for row in range(2):
            move(cond.at[pl.ds(row * 8, 8)], up.at[0, row, pl.ds((UP_ROWS - 1) * 8, 8)])
            move(cond.at[pl.ds((14 + row) * 8, 8)], dn.at[0, row, pl.ds((DN_ROWS - 1) * 8, 8)])
        for c in copies:
            c.wait()

    @pl.when(even)
    def _():
        fill(two, one)

    @pl.when(jnp.logical_not(even))
    def _():
        fill(one, two)


def pack(e, h, le, lh, cond):
    message = jax.ShapeDtypeStruct((e.shape[0], 3, DN_ROWS * 8, 128), F32)
    return pl.pallas_call(
        pack_kernel,
        out_shape=(message, message),
        in_specs=[pl.BlockSpec(memory_space=pl.ANY)] * 5,
        out_specs=(pl.BlockSpec(memory_space=pltpu.VMEM),) * 2,
        scratch_shapes=[pltpu.SemaphoreType.DMA((12,))],
        name="pack",
    )(e, h, le, lh, cond)


TO_LO = ((3, 17),) * 2 + ((2, 16),) * 2 + ((2, 15),) + ((1, 15),) * 2 + ((2, 16),) * 2 + ((1, 15),) * 2
TO_HI = (
    ((3, 17),) * 2
    + ((2, 17),)
    + ((2, 16),) * 2
    + ((2, 15),)
    + ((1, 15),) * 2
    + ((2, 16),) * 2
    + ((1, 16),)
    + ((1, 15),) * 2
)


def offset(table, k):
    return sum(lo + hi + 1 for lo, hi in table[:k])


def chunk(table):
    return -(-(offset(table, len(table)) + 12) // 8) * 8


def put_plane(ref, table, g, k, value):
    lo, hi = table[k]
    at = offset(table, k)
    ref[g, at : at + hi + 1] = value[0 : hi + 1]
    ref[g, at + hi + 1 : at + hi + 1 + lo] = value[ROWS - lo : ROWS]


def get_plane(ref, table, g, k):
    lo, hi = table[k]
    at = offset(table, k)
    end = at + lo + hi + 1
    rest = ref[g, end - 8 : end]
    if hi > 15:
        r = lax.broadcasted_iota(jnp.int32, (8, 128), 0)
        rest = jnp.where(r < 4, ref[g, at + 16 : at + 24], rest)
    return jnp.concatenate([ref[g, at : at + 16], rest], axis=0)


def put_conductivity(ref, table, value):
    at = offset(table, len(table))
    ref[0, at : at + 8] = value[0:8]
    ref[1, at : at + 8] = value[8:16]
    ref[1, at + 8 : at + 10] = value[16:18]
    ref[1, at + 10 : at + 12] = value[22:24]


def get_conductivity(ref, table):
    at = offset(table, len(table))
    r = lax.broadcasted_iota(jnp.int32, (8, 128), 0)
    rest = ref[1, at + 4 : at + 12]
    rest = jnp.where(r < 4, pltpu.roll(rest, 4, 0), rest)
    return jnp.concatenate([ref[0, at : at + 8], ref[1, at : at + 8], rest], axis=0)


def halo_tile(up, dn, lead, x, field):
    r = lax.broadcasted_iota(jnp.int32, (8, 128), 0)
    at, _ = UP[field]
    s = min(at, UP_ROWS - 8)
    hi = up[(*lead, pl.ds(s * 8 + x, 8, stride=8), slice(None))]
    if at != s:
        hi = pltpu.roll(hi, (8 - (at - s)) % 8, 0)
    at, n = DN[field]
    s = min(at, DN_ROWS - 8)
    lo = dn[(*lead, pl.ds(s * 8 + x, 8, stride=8), slice(None))]
    turn = (8 - n - (at - s)) % 8
    if turn:
        lo = pltpu.roll(lo, turn, 0)
    return jnp.where(r < 4, hi, lo)


def own_kernel(e, h, le, lh, cond, te, th, tle, tlh, tc, be, bh, ble, blh, bc, sems):
    pairs = ((e, be), (h, bh), (le, ble), (lh, blh), (cond, bc))
    copies = [pltpu.make_async_copy(src, dst, sems.at[k]) for k, (src, dst) in enumerate(pairs)]
    for c in copies:
        c.start()
    for k, (src, dst) in enumerate(((be, te), (bh, th), (ble, tle), (blh, tlh))):
        copies[k].wait()

        def body(g, carry, src=src, dst=dst):
            for c in range(3):
                for x in range(8):
                    dst[g, c, x, 0:8] = src[g, c, pl.ds(x, 8, stride=8), :]
                    dst[g, c, x, 8:16] = src[g, c, pl.ds(64 + x, 8, stride=8), :]
            return carry

        lax.fori_loop(0, e.shape[0], body, 0)
    copies[4].wait()
    for x in range(8):
        tc[x, 0:8] = bc[pl.ds(x, 8, stride=8), :]
        tc[x, 8:16] = bc[pl.ds(64 + x, 8, stride=8), :]


def own_planes(e, h, le, lh, cond):
    g = e.shape[0]
    vm = pl.BlockSpec(memory_space=pltpu.VMEM)
    field = jax.ShapeDtypeStruct((g, 3, 8, ROWS, 128), F32)
    return pl.pallas_call(
        own_kernel,
        out_shape=(field,) * 4 + (jax.ShapeDtypeStruct((8, 16, 128), F32),),
        in_specs=[pl.BlockSpec(memory_space=pltpu.HBM)] * 5,
        out_specs=(vm,) * 5,
        scratch_shapes=[pltpu.VMEM((g, 3, 128, 128), F32)] * 4
        + [pltpu.VMEM((128, 128), F32), pltpu.SemaphoreType.DMA((5,))],
        cost_estimate=pl.CostEstimate(flops=5_000_000, bytes_accessed=8_000_000, transcendentals=0),
        compiler_params=pltpu.CompilerParams(vmem_limit_bytes=24 * 1024 * 1024),
        name="own",
    )(e, h, le, lh, cond)


def planes_kernel(
    depth_n,
    lat_n,
    ie,
    ih,
    ile,
    ilh,
    tc,
    one,
    two,
    amp,
    tow,
    te,
    th,
    tle,
    tlh,
    ta,
    tb,
    to_lo,
    to_hi,
):
    groups = te.shape[0]
    depth_at = lax.axis_index("depth")
    lat_at = lax.axis_index("lat")

    even = depth_at % 2 == 0

    def halos(up, dn):
        def halo(g, carry):
            for c in range(3):
                for field, dst in enumerate((te, th, tle, tlh)):
                    for x in range(8):
                        dst[g, c, x, 16:24] = halo_tile(up, dn, (g, c), x, field)
            return carry

        lax.fori_loop(0, groups, halo, 0)

    @pl.when(even)
    def _():
        halos(one, two)

    @pl.when(jnp.logical_not(even))
    def _():
        halos(two, one)

    keep = last_row_keep(depth_at, depth_n)
    r8 = lax.broadcasted_iota(jnp.int32, (8, 128), 0)

    def edge(first, second, row, at):
        rows = pl.ds((at - 1) * 8, 8)
        return jnp.where(even, first[0, row, rows, :], second[0, row, rows, :])

    u0, u1 = (edge(one, two, row, UP_ROWS) for row in range(2))
    d0, d1 = (edge(two, one, row, DN_ROWS) for row in range(2))
    for x in range(8):
        rest = jnp.where(r8 == 0, u0[x : x + 1], 1.0)
        rest = jnp.where(r8 == 1, u1[x : x + 1], rest)
        rest = jnp.where(r8 == 6, d0[x : x + 1], rest)
        rest = jnp.where(r8 == 7, d1[x : x + 1], rest)
        whole = jnp.concatenate([tc[x], rest], axis=0)
        a, b = coefs(whole, keep)
        ta[x] = a
        tb[x] = b
        if x == 0:
            put_conductivity(to_lo, TO_LO, whole)
        if x == 7:
            put_conductivity(to_hi, TO_HI, whole)
    row_mask = first_row_mask(depth_at)
    z, lane = zrow(), lanes()

    def forward_planes(g, carry):
        s = -CC * row_mask
        cell = tow[g]
        lz = cell // (1024 * lat_n) - depth_at * 16
        lx = cell // 128 % (8 * lat_n) - lat_at * 8
        point = jnp.where((z == lz) & (lane == cell % 128), amp[g, 0], 0.0)

        def e0(x):
            return tuple(te[g, c, x] for c in range(3))

        def h0(x):
            return tuple(th[g, c, x] for c in range(3))

        def step_h(x):
            return tuple(f + s * k for f, k in zip(h0(x), curl_p(e0(x), e0(x + 1))))

        def put(ref, k, value):
            put_plane(ref, TO_LO if ref is to_lo else TO_HI, g, k, value)

        a0, b0, a1, b1 = ta[0], tb[0], ta[1], tb[1]
        f0, f1 = e0(0), e0(1)
        h1 = step_h(0)
        put(to_lo, 0, f0[1])
        put(to_lo, 1, f0[2])
        put(to_lo, 2, a0 * f0[1] + b0 * (dmz(h1[0]) - h1[2]))
        put(to_lo, 3, a0 * f0[2] + b0 * (h1[1] - dmy(h1[0])))
        put(to_lo, 4, h1[0])
        hit = jnp.where(lx == 0, point, 0.0)
        ex = a0 * f0[0] + b0 * (dmy(h1[2]) - dmz(h1[1]) - hit)
        k1 = step_h(1)
        ey1 = a1 * f1[1] + b1 * (dmz(k1[0]) - k1[2] + h1[2])
        ez1 = a1 * f1[2] + b1 * (k1[1] - h1[1] - dmy(k1[0]))
        put(to_lo, 5, h1[1] + s * (dpz(ex) - ez1))
        put(to_lo, 6, h1[2] + s * (ey1 - dpy(ex)))
        a7, b7, a6, b6 = ta[7], tb[7], ta[6], tb[6]
        f7, f6 = e0(7), e0(6)
        g7 = h0(7)
        put(to_hi, 0, g7[1] + s * (dpz(f7[0]) + f7[2]))
        put(to_hi, 1, g7[2] - s * (f7[1] + dpy(f7[0])))
        put(to_hi, 2, f7[0])
        hx7 = g7[0] + s * (dpy(f7[2]) - dpz(f7[1]))
        h6 = step_h(6)
        put(to_hi, 3, a7 * f7[1] + b7 * (dmz(hx7) + h6[2]))
        put(to_hi, 4, a7 * f7[2] - b7 * (h6[1] + dmy(hx7)))
        put(to_hi, 5, hx7)
        h5 = step_h(5)
        m6 = curl_m(h6, h5)
        hit = jnp.where(lx == 6, point, 0.0)
        ex6 = a6 * f6[0] + b6 * (m6[0] - hit)
        ey6 = a6 * f6[1] + b6 * m6[1]
        ez6 = a6 * f6[2] + b6 * m6[2]
        put(to_hi, 6, h6[1] + s * (dpz(ex6) + ez6))
        put(to_hi, 7, h6[2] - s * (ey6 + dpy(ex6)))
        s = row_mask

        def l0(x):
            return tuple(tle[g, c, x] for c in range(3))

        def w0(x):
            return tuple(tb[x] * f for f in l0(x))

        def m0(x):
            return tuple(tlh[g, c, x] for c in range(3))

        def step_m(x):
            return tuple(f + s * k for f, k in zip(m0(x), curl_p(w0(x), w0(x + 1))))

        q0, v0 = l0(0), w0(0)
        m1 = step_m(0)
        put(to_lo, 7, v0[1])
        put(to_lo, 8, v0[2])
        put(to_lo, 9, a0 * q0[1] - CC * (dmz(m1[0]) - m1[2]))
        put(to_lo, 10, a0 * q0[2] - CC * (m1[1] - dmy(m1[0])))
        q7, v7, n7 = l0(7), w0(7), m0(7)
        put(to_hi, 8, n7[1] + s * (dpz(v7[0]) + v7[2]))
        put(to_hi, 9, n7[2] - s * (v7[1] + dpy(v7[0])))
        put(to_hi, 10, q7[0])
        mx7 = n7[0] + s * (dpy(v7[2]) - dpz(v7[1]))
        m6 = step_m(6)
        put(to_hi, 11, a7 * q7[1] - CC * (dmz(mx7) + m6[2]))
        put(to_hi, 12, a7 * q7[2] + CC * (m6[1] + dmy(mx7)))
        return carry

    lax.fori_loop(0, groups, forward_planes, 0)


def planes(own, one, two, amp, tow, depth_n, lat_n):
    g = one.shape[0]
    vm = pl.BlockSpec(memory_space=pltpu.VMEM)
    sm = pl.BlockSpec(memory_space=pltpu.SMEM)
    field = jax.ShapeDtypeStruct((g, 3, 8, ROWS, 128), F32)
    coef = jax.ShapeDtypeStruct((8, ROWS, 128), F32)
    return pl.pallas_call(
        functools.partial(planes_kernel, depth_n, lat_n),
        out_shape=(
            field,
            field,
            field,
            field,
            coef,
            coef,
            jax.ShapeDtypeStruct((g, chunk(TO_LO), 128), F32),
            jax.ShapeDtypeStruct((g, chunk(TO_HI), 128), F32),
        ),
        in_specs=[vm] * 7 + [sm] * 2,
        out_specs=(vm,) * 8,
        input_output_aliases={0: 0, 1: 1, 2: 2, 3: 3},
        compiler_params=pltpu.CompilerParams(vmem_limit_bytes=24 * 1024 * 1024),
        name="planes",
    )(*own, one, two, amp, tow)


SLOTS = 24
STRIDE = 8 * ROWS


def e_at(g, n, c, x):
    return pl.ds(pl.multiple_of((g * 9 + n * 3 + c) * STRIDE + x * ROWS, 8), ROWS)


def triple(ref, g, x):
    return tuple(ref[g, c, x] for c in range(3))


def inside(n, x):
    return n + 1 <= x <= 6 - n


def weighted(old, drive, weight):
    total = None
    for c in range(3):
        t = (-2.0 * KK * old[c][0:16] - CC * KK * drive[c][0:16]) * weight[c][0:16]
        total = t if total is None else total + t
    return total


def take_samples(store, rcell, use, put):
    k = lax.broadcasted_iota(jnp.int32, (SLOTS, 128), 0)
    step = k // 3 % 3
    lane = lanes()

    def body(r, c0):
        cell = rcell[r]
        z, x, y = cell // 1024, cell // 128 % 8, cell % 128
        rows = store[pl.ds(x * ROWS + z, SLOTS, stride=STRIDE), :]
        near = (x >= step + 1) & (x <= 6 - step)
        put(r, jnp.where((lane == y) & use(near), rows, 0.0))
        return c0

    lax.fori_loop(0, rcell.shape[0], body, 0, unroll=4)


def tow_at(tow, g, depth_at, lat_at, lat_n):
    cell = tow[g]
    lz = cell // (1024 * lat_n) - depth_at * 16
    lx = cell // 128 % (8 * lat_n) - lat_at * 8
    point = jnp.where((zrow() == lz) & (lanes() == cell % 128), 1.0, 0.0)
    return lx, point


def inner_kernel(
    lat_n, te, th, tle, tlh, ta, tb, amp, tow, rcell, hh, mm, l1, l2, d0, ei, acc, samp
):
    groups = te.shape[0]
    depth_at = lax.axis_index("depth")
    lat_at = lax.axis_index("lat")
    row_mask = first_row_mask(depth_at)
    acc[...] = jnp.zeros_like(acc)

    def one_group(g, carry):
        lx, point = tow_at(tow, g, depth_at, lat_at, lat_n)
        lam = (tle, l1, l2)
        s = row_mask
        for n in range(2):
            w = {}

            def scaled(x, n=n, w=w):
                if x not in w:
                    w[x] = tuple(tb[x] * f for f in triple(lam[n], g, x))
                return w[x]

            for x in range(n, 7 - n):
                k = curl_p(scaled(x), scaled(x + 1))
                base = triple(tlh if n == 0 else mm, g, x)
                for c in range(3):
                    mm[g, c, x] = base[c] + s * k[c]
            for x in range(n + 1, 7 - n):
                k = curl_m(triple(mm, g, x), triple(mm, g, x - 1))
                old = triple(lam[n], g, x)
                for c in range(3):
                    lam[n + 1][g, c, x] = ta[x] * old[c] - CC * k[c]
        s = -CC * row_mask

        def e_of(n, x):
            if n == 0:
                return triple(te, g, x)
            return tuple(ei[e_at(g, n - 1, c, x), :] for c in range(3))

        for n in range(3):
            for x in range(n, 7 - n):
                k = curl_p(e_of(n, x), e_of(n, x + 1))
                base = triple(th if n == 0 else hh, g, x)
                for c in range(3):
                    hh[g, c, x] = base[c] + s * k[c]
            for x in range(n + 1, 7 - n):
                k = curl_m(triple(hh, g, x), triple(hh, g, x - 1))
                k = (k[0] - jnp.where(lx == x, amp[g, n], 0.0) * point, k[1], k[2])
                old = e_of(n, x)
                for c in range(3):
                    ei[e_at(g, n, c, x), :] = ta[x] * old[c] + tb[x] * k[c]
                if n == 0 and x in (1, 6):
                    for c in range(3):
                        d0[g, c, x // 6] = k[c][0:16]
                else:
                    acc[x] += weighted(old, k, triple(lam[2 - n], g, x))
        return carry

    lax.fori_loop(0, groups, one_group, 0)

    def put(r, values):
        samp[r] = values

    take_samples(ei, rcell, lambda near: near, put)


def inner(te, th, tle, tlh, ta, tb, amp, tow, rcell, lat_n):
    g, n = te.shape[0], rcell.shape[0]
    vm = pl.BlockSpec(memory_space=pltpu.VMEM)
    sm = pl.BlockSpec(memory_space=pltpu.SMEM)
    field = jax.ShapeDtypeStruct((g, 3, 8, ROWS, 128), F32)
    return pl.pallas_call(
        functools.partial(inner_kernel, lat_n),
        out_shape=(
            field,
            field,
            field,
            field,
            jax.ShapeDtypeStruct((g, 3, 2, 16, 128), F32),
            jax.ShapeDtypeStruct((SLOTS * STRIDE, 128), F32),
            jax.ShapeDtypeStruct((8, 16, 128), F32),
            jax.ShapeDtypeStruct((n, SLOTS, 128), F32),
        ),
        in_specs=[vm] * 6 + [sm] * 3,
        out_specs=(vm,) * 8,
        cost_estimate=pl.CostEstimate(flops=20_000_000, bytes_accessed=12_000_000, transcendentals=0),
        compiler_params=pltpu.CompilerParams(vmem_limit_bytes=24 * 1024 * 1024),
        name="inner",
    )(te, th, tle, tlh, ta, tb, amp, tow, rcell)


def outer_kernel(
    depth_n,
    lat_n,
    te,
    th,
    tle,
    tlh,
    ta,
    tb,
    hh,
    mm,
    l1,
    l2,
    d0,
    ei,
    acc,
    samp,
    lo,
    hi,
    amp,
    tow,
    rcell,
    rowner,
    grad,
    send,
    eo,
    ho,
    mo,
    o1,
    o2,
    total,
    count,
):
    groups = te.shape[0]
    depth_at = lax.axis_index("depth")
    lat_at = lax.axis_index("lat")
    row_mask = first_row_mask(depth_at)
    keep = last_row_keep(depth_at, depth_n)
    a8, b8 = coefs(get_conductivity(hi, TO_LO), keep & (lat_at < lat_n - 1))
    al, bl = coefs(get_conductivity(lo, TO_HI), keep)
    left = jnp.where(lat_at == 0, 0.0, 1.0)
    total[...] = acc[...]

    def lam(n, g, x):
        if n == 0:
            return triple(tle, g, x)
        near = inside(n - 1, x)
        return triple((l1 if near else o1) if n == 1 else (l2 if near else o2), g, x)

    def one_group(g, carry):
        def high(k):
            return get_plane(hi, TO_LO, g, k)

        def low(k):
            return get_plane(lo, TO_HI, g, k)

        lx, point = tow_at(tow, g, depth_at, lat_at, lat_n)
        s = row_mask
        p, q = 7, 8

        def m_of(n, x):
            return triple(mm if n <= x <= 6 - n else mo, g, x)

        def m_step(n, nxt):
            w = {8: nxt}

            def scaled(x):
                if x not in w:
                    w[x] = tuple(tb[x] * f for f in lam(n, g, x))
                return w[x]

            for x in range(8):
                if n <= x <= 6 - n:
                    continue
                k = curl_p(scaled(x), scaled(x + 1))
                base = triple(tlh, g, x) if n == 0 else m_of(n - 1, x)
                for c in range(3):
                    mo[g, c, x] = base[c] + s * k[c]

        def l_step(n, prv):
            out = (o1, o2)[n]
            for x in range(8):
                if inside(n, x):
                    continue
                k = curl_m(m_of(n, x), m_of(n, x - 1) if x else prv)
                old = lam(n, g, x)
                for c in range(3):
                    out[g, c, x] = ta[x] * old[c] - CC * k[c]

        m_step(0, (None, high(p), high(p + 1)))
        first = lam(0, g, 0)
        my = left * (low(q) - s * (tb[0] * first[2]))
        mz = left * (low(q + 1) + s * (tb[0] * first[1]))
        l_step(0, (None, my, mz))
        last = m_of(0, 7)
        m_step(1, (None, b8 * (high(p + 2) - CC * last[2]), b8 * (high(p + 3) + CC * last[1])))
        wx = bl * (al * low(q + 2) - CC * (dmy(mz) - dmz(my)))
        wy = bl * (low(q + 3) + CC * mz)
        wz = bl * (low(q + 4) - CC * my)
        first = lam(1, g, 0)
        my = left * (my + s * (dpz(wx) - (tb[0] * first[2] - wz)))
        mz = left * (mz + s * ((tb[0] * first[1] - wy) - dpy(wx)))
        l_step(1, (None, my, mz))
        s = -CC * row_mask
        p, q = 0, 0

        def e_of(n, x):
            if n == 0:
                return triple(te, g, x)
            ref = ei if inside(n - 1, x) else eo
            return tuple(ref[e_at(g, n - 1, c, x), :] for c in range(3))

        def h_of(n, x):
            return triple(hh if n <= x <= 6 - n else ho, g, x)

        def h_step(n, nxt):
            for x in range(8):
                if n <= x <= 6 - n:
                    continue
                k = curl_p(e_of(n, x), nxt if x == 7 else e_of(n, x + 1))
                base = triple(th, g, x) if n == 0 else h_of(n - 1, x)
                for c in range(3):
                    ho[g, c, x] = base[c] + s * k[c]

        def e_step(n, prv):
            for x in range(8):
                old = e_of(n, x)
                if inside(n, x):
                    if n == 0 and x in (1, 6):
                        k = tuple(d0[g, c, x // 6] for c in range(3))
                        total[x] += weighted(old, k, lam(2, g, x))
                    continue
                k = curl_m(h_of(n, x), h_of(n, x - 1) if x else prv)
                k = (k[0] - jnp.where(lx == x, amp[g, n], 0.0) * point, k[1], k[2])
                for c in range(3):
                    eo[e_at(g, n, c, x), :] = ta[x] * old[c] + tb[x] * k[c]
                total[x] += weighted(old, k, lam(2 - n, g, x))

        def drop(n):
            return jnp.where(lx == -1, amp[g, n], 0.0) * point

        h_step(0, (None, high(p), high(p + 1)))
        first = e_of(0, 0)
        hy = left * (low(q) - s * first[2])
        hz = left * (low(q + 1) + s * first[1])
        e_step(0, (None, hy, hz))
        last = h_of(0, 7)
        ey8 = high(p + 2) + b8 * last[2]
        ez8 = high(p + 3) - b8 * last[1]
        ex = al * low(q + 2) + bl * (dmy(hz) - dmz(hy) - drop(0))
        ey = low(q + 3) - bl * hz
        ez = low(q + 4) + bl * hy
        h_step(1, (None, ey8, ez8))
        first = e_of(1, 0)
        hy2 = left * (hy + s * (dpz(ex) - (first[2] - ez)))
        hz2 = left * (hz + s * ((first[1] - ey) - dpy(ex)))
        e_step(1, (None, hy2, hz2))
        last = h_of(1, 7)
        gx = high(p + 4) + s * (dpy(ez8) - dpz(ey8))
        gy = high(p + 5) + s * ez8
        gz = high(p + 6) - s * ey8
        ey9 = a8 * ey8 + b8 * (dmz(gx) - gz + last[2])
        ez9 = a8 * ez8 + b8 * (gy - last[1] - dmy(gx))
        hx2 = low(q + 5) + s * (dpy(ez) - dpz(ey))
        hyf = low(q + 6) - s * ez
        hzf = low(q + 7) + s * ey
        ex2 = al * ex + bl * (dmy(hz2) - dmz(hy2) - drop(1))
        ey2 = al * ey + bl * (dmz(hx2) - hz2 + hzf)
        ez2 = al * ez + bl * (hy2 - hyf - dmy(hx2))
        h_step(2, (None, ey9, ez9))
        first = e_of(2, 0)
        hy3 = left * (hy2 + s * (dpz(ex2) - (first[2] - ez2)))
        hz3 = left * (hz2 + s * ((first[1] - ey2) - dpy(ex2)))
        e_step(2, (None, hy3, hz3))
        return carry

    lax.fori_loop(0, groups, one_group, 0)
    for x in range(8):
        for half in range(2):
            rows = pl.ds(half * 64 + x, 8, stride=8)
            inv = tb[x, half * 8 : half * 8 + 8] * (1.0 / CC)
            grad[rows, :] = total[x, half * 8 : half * 8 + 8] * inv * inv
    send[...] = jnp.zeros_like(send)
    for o in range(send.shape[0]):
        count[o] = 0
    r24, lane = lax.broadcasted_iota(jnp.int32, (SLOTS, 128), 0), lanes()
    used = (r24 == lane) & (r24 < groups * 9)

    def put(r, values):
        o = rowner[r]
        slot = count[o]
        count[o] = slot + 1
        values = jnp.sum(samp[r] + values, axis=-1, keepdims=True)
        send[o, pl.ds(slot, 1), :] = jnp.sum(jnp.where(used, values, 0.0), axis=0, keepdims=True)

    take_samples(eo, rcell, jnp.logical_not, put)


def outer(te, th, tle, tlh, ta, tb, kept, lo, hi, amp, tow, rcell, rowner, depth_n, lat_n):
    g = te.shape[0]
    vm = pl.BlockSpec(memory_space=pltpu.VMEM)
    sm = pl.BlockSpec(memory_space=pltpu.SMEM)
    return pl.pallas_call(
        functools.partial(outer_kernel, depth_n, lat_n),
        out_shape=(
            jax.ShapeDtypeStruct((128, 128), F32),
            jax.ShapeDtypeStruct((lat_n, 8, 128), F32),
        ),
        in_specs=[vm] * 16 + [sm] * 4,
        out_specs=(vm,) * 2,
        scratch_shapes=[pltpu.VMEM((SLOTS * STRIDE, 128), F32)]
        + [pltpu.VMEM((g, 3, 8, ROWS, 128), F32)] * 4
        + [pltpu.VMEM((8, 16, 128), F32), pltpu.SMEM((lat_n,), jnp.int32)],
        cost_estimate=pl.CostEstimate(flops=10_000_000, bytes_accessed=12_000_000, transcendentals=0),
        compiler_params=pltpu.CompilerParams(vmem_limit_bytes=24 * 1024 * 1024),
        name="outer",
    )(te, th, tle, tlh, ta, tb, *kept, lo, hi, amp, tow, rcell, rowner)


def finish_kernel(mine, theirs, got, total, lines):
    total[...] = mine[...] + theirs[...]
    for slot in range(2):
        table = jnp.transpose(got[:, slot, :])
        for g in range(lines.shape[0]):
            lines[g, :, slot, :] = table[g * 9 : g * 9 + 9]


def finish(mine, theirs, got, groups):
    vm = pl.BlockSpec(memory_space=pltpu.VMEM)
    return pl.pallas_call(
        finish_kernel,
        out_shape=(
            jax.ShapeDtypeStruct(mine.shape, F32),
            jax.ShapeDtypeStruct((groups, 9, 2, got.shape[0]), F32),
        ),
        in_specs=[vm] * 3,
        out_specs=(vm,) * 2,
        compiler_params=pltpu.CompilerParams(vmem_limit_bytes=24 * 1024 * 1024),
        name="finish",
    )(mine, theirs, got)


def across(value, step):
    n = lax.axis_size("src")
    return lax.ppermute(value, "src", [(i, i ^ step) for i in range(n) if i ^ step < n])


def per_device(
    conductivity, e_start, h_start, e_weight, h_weight, source_amp, tow_cell, rec_cell, rec_owner
):
    groups = e_start.shape[0]
    depth_n, lat_n = lax.axis_size("depth"), lax.axis_size("lat")

    def flat(f):
        return f.reshape(groups, 3, 128, 128)

    e, h, le, lh = flat(e_start), flat(h_start), flat(e_weight), flat(h_weight)
    cond = conductivity.reshape(128, 128)
    one, two = pack(e, h, le, lh, cond)
    one = swapped(one, "depth", 0)
    two = swapped(two, "depth", 1)
    own = own_planes(e, h, le, lh, cond)
    te, th, tle, tlh, ta, tb, to_lo, to_hi = planes(
        own, one, two, source_amp, tow_cell, depth_n, lat_n
    )
    cells, owners = rec_cell.reshape(-1), rec_owner.reshape(-1)
    hi = shifted(to_lo, "lat", -1)
    lo = shifted(to_hi, "lat", 1)
    kept = inner(te, th, tle, tlh, ta, tb, source_amp, tow_cell, cells, lat_n)
    grad, send = outer(
        te,
        th,
        tle,
        tlh,
        ta,
        tb,
        kept,
        lo,
        hi,
        source_amp,
        tow_cell,
        cells,
        owners,
        depth_n,
        lat_n,
    )
    got = lax.all_to_all(send, "lat", split_axis=0, concat_axis=0, tiled=True)
    every = lax.all_gather(grad, "src", axis=0, tiled=False)
    total, lines = finish(every[0] + every[1], every[2] + every[3], got, groups)
    total = total.reshape(16, 8, 128)
    lines = jnp.transpose(lines.reshape(groups, 1, 1, 9, 2, lat_n), (0, 1, 2, 5, 4, 3))
    return (total, lines)


def solution(mesh):
    placed = (
        P("depth", "lat", None),
        P("src", None, "depth", "lat", None),
        P("src", None, "depth", "lat", None),
        P("src", None, "depth", "lat", None),
        P("src", None, "depth", "lat", None),
        P("src", None),
        P("src"),
        P("depth", "lat", None),
        P("depth", "lat", None, None),
    )
    return jax.shard_map(
        per_device,
        mesh=mesh,
        in_specs=placed,
        out_specs=(P("depth", "lat", None), P("src", "depth", "lat", None, None, None)),
        check_vma=False,
    )
```

time: 79.7 us -> 57.3 us (0.72)
  the two profiles are of different devices: /device:TPU:28 before, /device:TPU:32 now
where the time goes in v2:
time: 57.3 us; the launch traced here: 56.6 us
  starting transfers between devices  22.9 us (40%)
  Pallas kernels  10.5 us (18%)
  waiting for transfers between devices  10.2 us (18%)
  blocking collectives  7.45 us (13%)
  local copies, waits for them, and re-layouts  4.83 us (8%)
  between operations  0.76 us (1%)
    all_to_all x1, starting transfers between devices, per_device(): got = lax.all_to_all(send, 'lat', split_axis=0, concat_axis=0, tiled=True)  13.5 us
    all_gather x1, blocking collectives, per_device(): every = lax.all_gather(grad, 'src', axis=0, tiled=False)  7.45 us
    ppermute x2, waiting for transfers between devices, shifted(): return lax.ppermute(block, axis, route)  5.49 us
    unnamed x18, local copies, waits for them, and re-layouts  4.83 us
    ppermute x2, starting transfers between devices, swapped(): lax.ppermute(block, axis, [p for i in lower for p in ((i, i + 1), (i + 1,...  4.71 us
    ppermute x2, starting transfers between devices, shifted(): return lax.ppermute(block, axis, route)  4.7 us
    ppermute x2, waiting for transfers between devices, swapped(): lax.ppermute(block, axis, [p for i in lower for p in ((i, i + 1), (i + 1,...  3.09 us
    pallas_call x1, Pallas kernels, outer(): pl.pallas_call(functools.partial(outer_kernel, depth_n, lat_n), out_shape...  3.09 us
  transfers between devices with their start and end apart: 5, of which 4 were waited for; matrix products, arithmetic and copies ran while one was open for 0% of the time, Pallas kernels for 6%

profile of v2, /device:TPU:32, one launch (start us, length us, event | category | flops | bytes accessed | tf_op | source)
XLA Modules:
  0.0 56.6 jit_solution(16955711436737234060)
XLA Ops:
  0.6 0.0 copy-start.6
  0.6 0.0 copy-start.5
  0.6 1.9 %pack.1 = (f32[2,3,88,128]{3,2,1,0:T(8,128)}, f32[2,3,88,128]{3,2,1,0:T(8,128)}) custom-call(f32[2,3,128,128]{3,2,1,0:T(8,128)} %bitcast.13, f32[2,3,128,128]{3,2,1,0:T(8,128)} %bitcast.15, f32[2,3,128,128]{3,2,1,0:T(8,128)} %bitcast.17, f32[2,3,128,128]{3,2,1,0:T(8,128)} %bitcast.19, f32[128,128]{1,0:T(8,128)} %bitcast.21), custom_call_target="tpu_custom_call" | custom-call | tf_op jit(solution)/shard_map/pack/pallas_call | solution.py:131
  2.6 0.0 copy-start.7
  2.6 2.6 %collective-permute-start = (f32[2,3,88,128]{3,2,1,0:T(8,128)}, f32[2,3,88,128]{3,2,1,0:T(8,128)S(1)}, u32[]{:S(2)}, u32[]{:S(2)}) collective-permute-start(f32[2,3,88,128]{3,2,1,0:T(8,128)} %get-tuple-element.34), channel_id=1, source_target_pairs={{0,16},{16,0},{32,48},{48,32},{64,80},{80,64},{96,112},{112,96},{1... | collective-permute-start | bytes 811016 | tf_op jit(solution)/shard_map/ppermute | solution.py:29
  5.2 2.1 %collective-permute-start.1 = (f32[2,3,88,128]{3,2,1,0:T(8,128)}, f32[2,3,88,128]{3,2,1,0:T(8,128)S(1)}, u32[]{:S(2)}, u32[]{:S(2)}) collective-permute-start(f32[2,3,88,128]{3,2,1,0:T(8,128)} %get-tuple-element.35), channel_id=1, source_target_pairs={{16,32},{32,16},{48,64},{64,48},{80,96},{96,80},{17,33},{33,17},{4... | collective-permute-start | bytes 811016 | tf_op jit(solution)/shard_map/ppermute | solution.py:29
  7.3 0.0 copy-start
  7.3 1.0 %copy-done = f32[2,3,16,8,128]{4,3,2,1,0:T(8,128)S(1)} copy-done((f32[2,3,16,8,128]{4,3,2,1,0:T(8,128)S(1)}, f32[2,3,16,8,128]{4,3,2,1,0:T(8,128)}, u32[]{:S(2)}) %copy-start) | copy-done | bytes 393240
  8.3 0.0 copy-start.1
  8.3 1.0 %copy-done.1 = f32[2,3,16,8,128]{4,3,2,1,0:T(8,128)S(1)} copy-done((f32[2,3,16,8,128]{4,3,2,1,0:T(8,128)S(1)}, f32[2,3,16,8,128]{4,3,2,1,0:T(8,128)}, u32[]{:S(2)}) %copy-start.1) | copy-done | bytes 393240
  9.3 0.0 copy-start.2
  9.3 1.0 %copy-done.2 = f32[2,3,16,8,128]{4,3,2,1,0:T(8,128)S(1)} copy-done((f32[2,3,16,8,128]{4,3,2,1,0:T(8,128)S(1)}, f32[2,3,16,8,128]{4,3,2,1,0:T(8,128)}, u32[]{:S(2)}) %copy-start.2) | copy-done | bytes 393240
  10.3 0.0 copy-start.3
  10.3 1.0 %copy-done.3 = f32[2,3,16,8,128]{4,3,2,1,0:T(8,128)S(1)} copy-done((f32[2,3,16,8,128]{4,3,2,1,0:T(8,128)S(1)}, f32[2,3,16,8,128]{4,3,2,1,0:T(8,128)}, u32[]{:S(2)}) %copy-start.3) | copy-done | bytes 393240
  11.3 0.0 copy-start.4
  11.3 0.8 %copy-done.4 = f32[16,8,128]{2,1,0:T(8,128)S(1)} copy-done((f32[16,8,128]{2,1,0:T(8,128)S(1)}, f32[16,8,128]{2,1,0:T(8,128)}, u32[]{:S(2)}) %copy-start.4) | copy-done | bytes 65560
  12.2 1.2 %own.1 = (f32[2,3,8,24,128]{4,3,2,1,0:T(8,128)S(1)}, f32[2,3,8,24,128]{4,3,2,1,0:T(8,128)S(1)}, f32[2,3,8,24,128]{4,3,2,1,0:T(8,128)S(1)}, f32[2,3,8,24,128]{4,3,2,1,0:T(8,128)S(1)}, f32[8,16,128]{2,1,0:T(8,128)S(1)}) custom-call(f32[2,3,128,128]{3,2,1,0:T(8,128)S(1)} %bitcast.14, f32[2,3,128,128]{3,2,1,0:T(8,128)S(1)} %bitcast.16, ...), custom_call_target="tpu_custom_call" | custom-call | flops 5000000 | bytes 8000000 | tf_op jit(solution)/shard_map/own/pallas_call | solution.py:238
  13.4 0.0 collective-permute-done.one
  13.4 3.1 %collective-permute-done.1.two = f32[2,3,88,128]{3,2,1,0:T(8,128)S(1)} collective-permute-done((f32[2,3,88,128]{3,2,1,0:T(8,128)}, f32[2,3,88,128]{3,2,1,0:T(8,128)S(1)}, u32[]{:S(2)}, u32[]{:S(2)}) %collective-permute-start.1) | collective-permute-done | bytes 270368 | tf_op jit(solution)/shard_map/ppermute | solution.py:29
  16.5 0.0 copy-done.6
  16.5 0.0 copy-done.5
  16.5 0.0 copy-start.8
  16.5 1.3 %planes.1 = (f32[2,3,8,24,128]{4,3,2,1,0:T(8,128)S(1)}, f32[2,3,8,24,128]{4,3,2,1,0:T(8,128)S(1)}, f32[2,3,8,24,128]{4,3,2,1,0:T(8,128)S(1)}, f32[2,3,8,24,128]{...) custom-call(f32[2,3,8,24,128]{4,3,2,1,0:T(8,128)S(1)} %get-tuple-ele, ...), custom_call_target="tpu_custom_call", output_to_operand_aliasing={{0}: (0, {}), {1}: (1, {}), {2}: (2, {}), {3}: (3, {})} | custom-call | tf_op jit(solution)/shard_map/planes/pallas_call | solution.py:413
  17.8 3.4 %collective-permute-start.2 = (f32[2,256,128]{2,1,0:T(8,128)S(1)}, f32[2,256,128]{2,1,0:T(8,128)S(1)}, u32[]{:S(2)}, u32[]{:S(2)}) collective-permute-start(f32[2,256,128]{2,1,0:T(8,128)S(1)} %get-tuple-element.50), channel_id=1, source_target_pairs={{0,1},{1,2},{2,3},{3,4},{4,5},{5,6},{6,7},{7,8},{8,9},{9,10},{10,1... | collective-permute-start | bytes 786440 | tf_op jit(solution)/shard_map/ppermute | solution.py:23
  21.2 1.3 %collective-permute-start.3 = (f32[2,216,128]{2,1,0:T(8,128)S(1)}, f32[2,216,128]{2,1,0:T(8,128)S(1)}, u32[]{:S(2)}, u32[]{:S(2)}) collective-permute-start(f32[2,216,128]{2,1,0:T(8,128)S(1)} %get-tuple-element.51), channel_id=1, source_target_pairs={{1,0},{2,1},{3,2},{4,3},{5,4},{6,5},{7,6},{8,7},{9,8},{10,9},{11,1... | collective-permute-start | bytes 663560 | tf_op jit(solution)/shard_map/ppermute | solution.py:23
  22.5 0.0 copy-done.7
  22.5 2.3 %inner.1 = (f32[2,3,8,24,128]{4,3,2,1,0:T(8,128)S(1)}, f32[2,3,8,24,128]{4,3,2,1,0:T(8,128)S(1)}, f32[2,3,8,24,128]{4,3,2,1,0:T(8,128)S(1)}, f32[2,3,8,24,128]{4...) custom-call(f32[2,3,8,24,128]{4,3,2,1,0:T(8,128)S(1)} %get-tuple-ele, ...), custom_call_target="tpu_custom_call" | custom-call | flops 20000000 | bytes 12000000 | tf_op jit(solution)/shard_map/inner/pallas_call | solution.py:551
  24.8 4.6 %collective-permute-done.3.hi = f32[2,216,128]{2,1,0:T(8,128)S(1)} collective-permute-done((f32[2,216,128]{2,1,0:T(8,128)S(1)}, f32[2,216,128]{2,1,0:T(8,128)S(1)}, u32[]{:S(2)}, u32[]{:S(2)}) %collective-permute-start.3) | collective-permute-done | bytes 221216 | tf_op jit(solution)/shard_map/ppermute | solution.py:23
  29.4 0.9 %collective-permute-done.2.lo = f32[2,256,128]{2,1,0:T(8,128)S(1)} collective-permute-done((f32[2,256,128]{2,1,0:T(8,128)S(1)}, f32[2,256,128]{2,1,0:T(8,128)S(1)}, u32[]{:S(2)}, u32[]{:S(2)}) %collective-permute-start.2) | collective-permute-done | bytes 262176 | tf_op jit(solution)/shard_map/ppermute | solution.py:23
  30.3 0.0 copy-done.8
  30.3 3.1 %outer.1 = (f32[128,128]{1,0:T(8,128)S(1)}, f32[16,8,128]{2,1,0:T(8,128)}) custom-call(f32[2,3,8,24,128]{4,3,2,1,0:T(8,128)S(1)} %get-tuple-element.36.te, f32[2,3,8,24,128]{4,3,2,1,0:T(8,128)S(1)} %get-tuple-element.37.th, f32[2,3,8,24,128]{4,3,2,1,0:T(8,128)S(1)} %get-tuple-element.38.tle, f32[2,3,8,24,128]{4,3,2,1,0:T(8,128)S(1)} %get-tuple-element.39.tlh, ...), custom_call_target="tpu_custom_call" | custom-call | flops 10000000 | bytes 12000000 | tf_op jit(solution)/shard_map/outer/pallas_call | solution.py:773
  33.4 13.5 %all-to-all-start = ((f32[16,8,128]{2,1,0:T(8,128)}), f32[16,8,128]{2,1,0:T(8,128)S(1)}, u32[]{:S(2)}, u32[]{:S(2)}) async-start(f32[16,8,128]{2,1,0:T(8,128)} %get-tuple-element.53), calls=%async_computation | async-start | bytes 131072 | tf_op jit(solution)/shard_map/all_to_all | solution.py:857
  46.8 7.5 %all-gather = f32[512,128]{1,0:T(8,128)S(1)} all-gather(f32[128,128]{1,0:T(8,128)S(1)} %get-tuple-element.52), channel_id=2, replica_groups=mesh['src'=4,'depth'=8,'lat'=16] {'src'}, dimensions={0}, use_global_device_ids=true | all-gather | bytes 327680 | tf_op jit(solution)/shard_map/all_gather | solution.py:858
  54.3 1.6 %all-to-all-done.got = f32[16,8,128]{2,1,0:T(8,128)S(1)} async-done(((f32[16,8,128]{2,1,0:T(8,128)}), f32[16,8,128]{2,1,0:T(8,128)S(1)}, u32[]{:S(2)}, u32[]{:S(2)}) %all-to-all-start) | async-done | bytes 65568 | tf_op jit(solution)/shard_map/all_to_all | solution.py:857
  55.9 0.7 %finish.1 = (f32[128,128]{1,0:T(8,128)}, f32[2,9,2,16]{3,2,1,0:T(2,128)}) custom-call(f32[128,128]{1,0:T(8,128)S(1)} %get-tuple-element.59.mine, f32[128,128]{1,0:T(8,128)S(1)} %get-tuple-element.58.theirs, f32[16,8,128]{2,1,0:T(8,128)S(1)} %all-to-all-done.got), custom_call_target="tpu_custom_call" | custom-call | tf_op jit(solution)/shard_map/finish/pallas_call | solution.py:800
  (1 shorter events, 0.0 us)
Async XLA Ops:
  0.6 15.8 %copy-start.6 = (s32[2]{0:T(128)S(1)}, s32[2]{0:T(128)}, u32[]{:S(2)}) copy-start(s32[2]{0:T(128)} %tow.5) | copy-start | bytes 28
  0.6 15.8 %copy-start.5 = (f32[2,3]{1,0:T(2,128)S(1)}, f32[2,3]{1,0:T(2,128)}, u32[]{:S(2)}) copy-start(f32[2,3]{1,0:T(2,128)} %amp.5) | copy-start | bytes 76
  2.6 19.9 %copy-start.7 = (s32[1,1,16]{2,1,0:T(1,128)S(1)}, s32[1,1,16]{2,1,0:T(1,128)}, u32[]{:S(2)}) copy-start(s32[1,1,16]{2,1,0:T(1,128)} %param.16) | copy-start | bytes 196
  2.6 10.8 %collective-permute-start = (f32[2,3,88,128]{3,2,1,0:T(8,128)}, f32[2,3,88,128]{3,2,1,0:T(8,128)S(1)}, u32[]{:S(2)}, u32[]{:S(2)}) collective-permute-start(f32[2,3,88,128]{3,2,1,0:T(8,128)} %get-tuple-element.34), channel_id=1, source_target_pairs={{0,16},{16,0},{32,48},{48,32},{64,80},{80,64},{96,112},{112,96},{1... | collective-permute-start | bytes 811016 | tf_op jit(solution)/shard_map/ppermute | solution.py:29
  5.2 11.3 %collective-permute-start.1 = (f32[2,3,88,128]{3,2,1,0:T(8,128)}, f32[2,3,88,128]{3,2,1,0:T(8,128)S(1)}, u32[]{:S(2)}, u32[]{:S(2)}) collective-permute-start(f32[2,3,88,128]{3,2,1,0:T(8,128)} %get-tuple-element.35), channel_id=1, source_target_pairs={{16,32},{32,16},{48,64},{64,48},{80,96},{96,80},{17,33},{33,17},{4... | collective-permute-start | bytes 811016 | tf_op jit(solution)/shard_map/ppermute | solution.py:29
  7.3 1.0 %copy-start = (f32[2,3,16,8,128]{4,3,2,1,0:T(8,128)S(1)}, f32[2,3,16,8,128]{4,3,2,1,0:T(8,128)}, u32[]{:S(2)}) copy-start(f32[2,3,16,8,128]{4,3,2,1,0:T(8,128)} %param.10) | copy-start | bytes 1179652
  8.3 1.0 %copy-start.1 = (f32[2,3,16,8,128]{4,3,2,1,0:T(8,128)S(1)}, f32[2,3,16,8,128]{4,3,2,1,0:T(8,128)}, u32[]{:S(2)}) copy-start(f32[2,3,16,8,128]{4,3,2,1,0:T(8,128)} %param.11) | copy-start | bytes 1179652
  9.3 1.0 %copy-start.2 = (f32[2,3,16,8,128]{4,3,2,1,0:T(8,128)S(1)}, f32[2,3,16,8,128]{4,3,2,1,0:T(8,128)}, u32[]{:S(2)}) copy-start(f32[2,3,16,8,128]{4,3,2,1,0:T(8,128)} %param.12) | copy-start | bytes 1179652
  10.3 1.0 %copy-start.3 = (f32[2,3,16,8,128]{4,3,2,1,0:T(8,128)S(1)}, f32[2,3,16,8,128]{4,3,2,1,0:T(8,128)}, u32[]{:S(2)}) copy-start(f32[2,3,16,8,128]{4,3,2,1,0:T(8,128)} %param.13) | copy-start | bytes 1179652
  11.3 0.8 %copy-start.4 = (f32[16,8,128]{2,1,0:T(8,128)S(1)}, f32[16,8,128]{2,1,0:T(8,128)}, u32[]{:S(2)}) copy-start(f32[16,8,128]{2,1,0:T(8,128)} %param.9) | copy-start | bytes 196612
  16.5 13.8 %copy-start.8 = (s32[1,1,16,1]{2,3,1,0:T(1,128)S(1)}, s32[1,1,16,1]{2,3,1,0:T(1,128)}, u32[]{:S(2)}) copy-start(s32[1,1,16,1]{2,3,1,0:T(1,128)} %param.17) | copy-start | bytes 196
  17.8 12.5 %collective-permute-start.2 = (f32[2,256,128]{2,1,0:T(8,128)S(1)}, f32[2,256,128]{2,1,0:T(8,128)S(1)}, u32[]{:S(2)}, u32[]{:S(2)}) collective-permute-start(f32[2,256,128]{2,1,0:T(8,128)S(1)} %get-tuple-element.50), channel_id=1, source_target_pairs={{0,1},{1,2},{2,3},{3,4},{4,5},{5,6},{6,7},{7,8},{8,9},{9,10},{10,1... | collective-permute-start | bytes 786440 | tf_op jit(solution)/shard_map/ppermute | solution.py:23
  21.2 8.2 %collective-permute-start.3 = (f32[2,216,128]{2,1,0:T(8,128)S(1)}, f32[2,216,128]{2,1,0:T(8,128)S(1)}, u32[]{:S(2)}, u32[]{:S(2)}) collective-permute-start(f32[2,216,128]{2,1,0:T(8,128)S(1)} %get-tuple-element.51), channel_id=1, source_target_pairs={{1,0},{2,1},{3,2},{4,3},{5,4},{6,5},{7,6},{8,7},{9,8},{10,9},{11,1... | collective-permute-start | bytes 663560 | tf_op jit(solution)/shard_map/ppermute | solution.py:23
  33.4 22.5 %all-to-all-start = ((f32[16,8,128]{2,1,0:T(8,128)}), f32[16,8,128]{2,1,0:T(8,128)S(1)}, u32[]{:S(2)}, u32[]{:S(2)}) async-start(f32[16,8,128]{2,1,0:T(8,128)} %get-tuple-element.53), calls=%async_computation | async-start | bytes 131072 | tf_op jit(solution)/shard_map/all_to_all | solution.py:857

commit v3 on v2

--- a/solution.py
+++ b/solution.py
@@ -134,6 +134,7 @@
         in_specs=[pl.BlockSpec(memory_space=pl.ANY)] * 5,
         out_specs=(pl.BlockSpec(memory_space=pltpu.VMEM),) * 2,
         scratch_shapes=[pltpu.SemaphoreType.DMA((12,))],
+        compiler_params=pltpu.CompilerParams(vmem_limit_bytes=25165824),
         name="pack",
     )(e, h, le, lh, cond)
 
@@ -238,7 +239,7 @@
     return pl.pallas_call(
         own_kernel,
         out_shape=(field,) * 4 + (jax.ShapeDtypeStruct((8, 16, 128), F32),),
-        in_specs=[pl.BlockSpec(memory_space=pltpu.HBM)] * 5,
+        in_specs=[pl.BlockSpec(memory_space=pl.ANY)] * 5,
         out_specs=(vm,) * 5,
         scratch_shapes=[pltpu.VMEM((g, 3, 128, 128), F32)] * 4
         + [pltpu.VMEM((128, 128), F32), pltpu.SemaphoreType.DMA((5,))],
@@ -401,7 +402,7 @@
         put(to_hi, 12, a7 * q7[2] + CC * (m6[1] + dmy(mx7)))
         return carry
 
-    lax.fori_loop(0, groups, forward_planes, 0)
+    lax.fori_loop(0, groups, forward_planes, 0, unroll=True)
 
 
 def planes(own, one, two, amp, tow, depth_n, lat_n):
@@ -467,7 +468,7 @@
         put(r, jnp.where((lane == y) & use(near), rows, 0.0))
         return c0
 
-    lax.fori_loop(0, rcell.shape[0], body, 0, unroll=4)
+    lax.fori_loop(0, rcell.shape[0], body, 0, unroll=True)
 
 
 def tow_at(tow, g, depth_at, lat_at, lat_n):
@@ -535,7 +536,7 @@
                     acc[x] += weighted(old, k, triple(lam[2 - n], g, x))
         return carry
 
-    lax.fori_loop(0, groups, one_group, 0)
+    lax.fori_loop(0, groups, one_group, 0, unroll=True)
 
     def put(r, values):
         samp[r] = values
@@ -744,7 +745,7 @@
         e_step(2, (None, hy3, hz3))
         return carry
 
-    lax.fori_loop(0, groups, one_group, 0)
+    lax.fori_loop(0, groups, one_group, 0, unroll=True)
     for x in range(8):
         for half in range(2):
             rows = pl.ds(half * 64 + x, 8, stride=8)
@@ -774,7 +775,7 @@
         functools.partial(outer_kernel, depth_n, lat_n),
         out_shape=(
             jax.ShapeDtypeStruct((128, 128), F32),
-            jax.ShapeDtypeStruct((lat_n, 8, 128), F32),
+            jax.ShapeDtypeStruct((lat_n, 2, 128), F32),
         ),
         in_specs=[vm] * 16 + [sm] * 4,
         out_specs=(vm,) * 2,
@@ -826,10 +827,13 @@
 
     e, h, le, lh = flat(e_start), flat(h_start), flat(e_weight), flat(h_weight)
     cond = conductivity.reshape(128, 128)
-    one, two = pack(e, h, le, lh, cond)
+    fields = [
+        pltpu.with_memory_space_constraint(f, pltpu.HBM) for f in (e, h, le, lh, cond)
+    ]
+    one, two = pack(*fields)
     one = swapped(one, "depth", 0)
     two = swapped(two, "depth", 1)
-    own = own_planes(e, h, le, lh, cond)
+    own = own_planes(*fields)
     te, th, tle, tlh, ta, tb, to_lo, to_hi = planes(
         own, one, two, source_amp, tow_cell, depth_n, lat_n
     )

time: 57.3 us -> 54.8 us (0.956)
  the two profiles are of different devices: /device:TPU:32 before, /device:TPU:36 now
where the time goes in v3:
time: 54.8 us; the launch traced here: 54.5 us
  starting transfers between devices  23.5 us (43%)
  waiting for transfers between devices  13.7 us (25%)
  Pallas kernels  9.27 us (17%)
  blocking collectives  7.31 us (13%)
  between operations  0.73 us (1%)
    all_to_all x1, starting transfers between devices, per_device(): got = lax.all_to_all(send, 'lat', split_axis=0, concat_axis=0, tiled=True)  14.4 us
    ppermute x2, waiting for transfers between devices, swapped(): lax.ppermute(block, axis, [p for i in lower for p in ((i, i + 1), (i + 1,...  7.43 us
    all_gather x1, blocking collectives, per_device(): every = lax.all_gather(grad, 'src', axis=0, tiled=False)  7.31 us
    ppermute x2, waiting for transfers between devices, shifted(): return lax.ppermute(block, axis, route)  5.01 us
    ppermute x2, starting transfers between devices, swapped(): lax.ppermute(block, axis, [p for i in lower for p in ((i, i + 1), (i + 1,...  4.72 us
    ppermute x2, starting transfers between devices, shifted(): return lax.ppermute(block, axis, route)  4.41 us
    pallas_call x1, Pallas kernels, outer(): pl.pallas_call(functools.partial(outer_kernel, depth_n, lat_n), out_shape...  2.69 us
    pallas_call x1, Pallas kernels, inner(): pl.pallas_call(functools.partial(inner_kernel, lat_n), out_shape=(field,...  2.16 us
  transfers between devices with their start and end apart: 5, of which 4 were waited for; matrix products, arithmetic and copies ran while one was open for 0% of the time, Pallas kernels for 7%

profile of v3, /device:TPU:36, one launch (start us, length us, event | category | flops | bytes accessed | tf_op | source)
XLA Modules:
  0.0 54.5 jit_solution(18192854610087452166)
XLA Ops:
  0.6 0.0 copy-start.1
  0.6 0.0 copy-start
  0.6 1.1 %pack.1 = (f32[2,3,88,128]{3,2,1,0:T(8,128)S(1)}, f32[2,3,88,128]{3,2,1,0:T(8,128)S(1)}) custom-call(f32[2,3,128,128]{3,2,1,0:T(8,128)} %bitcast.16, f32[2,3,128,128]{3,2,1,0:T(8,128)} %bitcast.18, f32[2,3,128,128]{3,2,1,0:T(8,128)} %bitcast.20, f32[2,3,128,128]{3,2,1,0:T(8,128)} %bitcast.22, f32[128,128]{1,0:T(8,128)} %bitcast.24), custom_call_target="tpu_custom_call" | custom-call | tf_op jit(solution)/shard_map/pack/pallas_call | solution.py:131
  1.8 0.0 copy-start.2
  1.8 2.6 %collective-permute-start = (f32[2,3,88,128]{3,2,1,0:T(8,128)S(1)}, f32[2,3,88,128]{3,2,1,0:T(8,128)S(1)}, u32[]{:S(2)}, u32[]{:S(2)}) collective-permute-start(f32[2,3,88,128]{3,2,1,0:T(8,128)S(1)} %get-tuple-element.34), channel_id=1, source_target_pairs={{0,16},{16,0},{32,48},{48,32},{64,80},{80,64},{96,112},{112,96},{1... | collective-permute-start | bytes 811016 | tf_op jit(solution)/shard_map/ppermute | solution.py:29
  4.4 2.1 %collective-permute-start.1 = (f32[2,3,88,128]{3,2,1,0:T(8,128)S(1)}, f32[2,3,88,128]{3,2,1,0:T(8,128)S(1)}, u32[]{:S(2)}, u32[]{:S(2)}) collective-permute-start(f32[2,3,88,128]{3,2,1,0:T(8,128)S(1)} %get-tuple-element.35), channel_id=1, source_target_pairs={{16,32},{32,16},{48,64},{64,48},{80,96},{96,80},{17,33},{33,17},{4... | collective-permute-start | bytes 811016 | tf_op jit(solution)/shard_map/ppermute | solution.py:29
  6.5 1.5 %own.1 = (f32[2,3,8,24,128]{4,3,2,1,0:T(8,128)S(1)}, f32[2,3,8,24,128]{4,3,2,1,0:T(8,128)S(1)}, f32[2,3,8,24,128]{4,3,2,1,0:T(8,128)S(1)}, f32[2,3,8,24,128]{4,3,2,1,0:T(8,128)S(1)}, f32[8,16,128]{2,1,0:T(8,128)S(1)}) custom-call(f32[2,3,128,128]{3,2,1,0:T(8,128)} %bitcast.17, f32[2,3,128,128]{3,2,1,0:T(8,128)} %bitcast.19, f32[2,3,128,128]{3,2,1,0:T(8,128)} %bitcast.21, ...), custom_call_target="tpu_custom_call" | custom-call | flops 5000000 | bytes 8000000 | tf_op jit(solution)/shard_map/own/pallas_call | solution.py:239
  8.0 3.9 %collective-permute-done.one = f32[2,3,88,128]{3,2,1,0:T(8,128)S(1)} collective-permute-done((f32[2,3,88,128]{3,2,1,0:T(8,128)S(1)}, f32[2,3,88,128]{3,2,1,0:T(8,128)S(1)}, u32[]{:S(2)}, u32[]{:S(2)}) %collective-permute-start) | collective-permute-done | bytes 270368 | tf_op jit(solution)/shard_map/ppermute | solution.py:29
  11.9 3.5 %collective-permute-done.1.two = f32[2,3,88,128]{3,2,1,0:T(8,128)S(1)} collective-permute-done((f32[2,3,88,128]{3,2,1,0:T(8,128)S(1)}, f32[2,3,88,128]{3,2,1,0:T(8,128)S(1)}, u32[]{:S(2)}, u32[]{:S(2)}) %collective-permute-start.1) | collective-permute-done | bytes 270368 | tf_op jit(solution)/shard_map/ppermute | solution.py:29
  15.5 0.0 copy-done.1
  15.5 0.0 copy-done
  15.5 0.0 copy-start.3
  15.5 1.1 %planes.1 = (f32[2,3,8,24,128]{4,3,2,1,0:T(8,128)S(1)}, f32[2,3,8,24,128]{4,3,2,1,0:T(8,128)S(1)}, f32[2,3,8,24,128]{4,3,2,1,0:T(8,128)S(1)}, f32[2,3,8,24,128]{...) custom-call(f32[2,3,8,24,128]{4,3,2,1,0:T(8,128)S(1)} %get-tuple-ele, ...), custom_call_target="tpu_custom_call", output_to_operand_aliasing={{0}: (0, {}), {1}: (1, {}), {2}: (2, {}), {3}: (3, {})} | custom-call | tf_op jit(solution)/shard_map/planes/pallas_call | solution.py:414
  16.6 3.1 %collective-permute-start.2 = (f32[2,256,128]{2,1,0:T(8,128)S(1)}, f32[2,256,128]{2,1,0:T(8,128)S(1)}, u32[]{:S(2)}, u32[]{:S(2)}) collective-permute-start(f32[2,256,128]{2,1,0:T(8,128)S(1)} %get-tuple-element.50), channel_id=1, source_target_pairs={{0,1},{1,2},{2,3},{3,4},{4,5},{5,6},{6,7},{7,8},{8,9},{9,10},{10,1... | collective-permute-start | bytes 786440 | tf_op jit(solution)/shard_map/ppermute | solution.py:23
  19.7 1.3 %collective-permute-start.3 = (f32[2,216,128]{2,1,0:T(8,128)S(1)}, f32[2,216,128]{2,1,0:T(8,128)S(1)}, u32[]{:S(2)}, u32[]{:S(2)}) collective-permute-start(f32[2,216,128]{2,1,0:T(8,128)S(1)} %get-tuple-element.51), channel_id=1, source_target_pairs={{1,0},{2,1},{3,2},{4,3},{5,4},{6,5},{7,6},{8,7},{9,8},{10,9},{11,1... | collective-permute-start | bytes 663560 | tf_op jit(solution)/shard_map/ppermute | solution.py:23
  21.0 0.0 copy-done.2
  21.0 2.2 %inner.1 = (f32[2,3,8,24,128]{4,3,2,1,0:T(8,128)S(1)}, f32[2,3,8,24,128]{4,3,2,1,0:T(8,128)S(1)}, f32[2,3,8,24,128]{4,3,2,1,0:T(8,128)S(1)}, f32[2,3,8,24,128]{4...) custom-call(f32[2,3,8,24,128]{4,3,2,1,0:T(8,128)S(1)} %get-tuple-ele, ...), custom_call_target="tpu_custom_call" | custom-call | flops 20000000 | bytes 12000000 | tf_op jit(solution)/shard_map/inner/pallas_call | solution.py:552
  23.2 5.0 %collective-permute-done.3.hi = f32[2,216,128]{2,1,0:T(8,128)S(1)} collective-permute-done((f32[2,216,128]{2,1,0:T(8,128)S(1)}, f32[2,216,128]{2,1,0:T(8,128)S(1)}, u32[]{:S(2)}, u32[]{:S(2)}) %collective-permute-start.3) | collective-permute-done | bytes 221216 | tf_op jit(solution)/shard_map/ppermute | solution.py:23
  28.2 0.0 collective-permute-done.2.lo
  28.2 0.0 copy-done.3
  28.2 2.7 %outer.1 = (f32[128,128]{1,0:T(8,128)S(1)}, f32[16,2,128]{2,1,0:T(2,128)}) custom-call(f32[2,3,8,24,128]{4,3,2,1,0:T(8,128)S(1)} %get-tuple-element.36.te, f32[2,3,8,24,128]{4,3,2,1,0:T(8,128)S(1)} %get-tuple-element.37.th, f32[2,3,8,24,128]{4,3,2,1,0:T(8,128)S(1)} %get-tuple-element.38.tle, f32[2,3,8,24,128]{4,3,2,1,0:T(8,128)S(1)} %get-tuple-element.39.tlh, ...), custom_call_target="tpu_custom_call" | custom-call | flops 10000000 | bytes 12000000 | tf_op jit(solution)/shard_map/outer/pallas_call | solution.py:774
  30.9 14.4 %all-to-all-start = ((f32[16,2,128]{2,1,0:T(2,128)}), f32[16,2,128]{2,1,0:T(2,128)S(1)}, u32[]{:S(2)}, u32[]{:S(2)}) async-start(f32[16,2,128]{2,1,0:T(2,128)} %get-tuple-element.53), calls=%async_computation | async-start | bytes 32768 | tf_op jit(solution)/shard_map/all_to_all | solution.py:861
  45.3 7.3 %all-gather = f32[512,128]{1,0:T(8,128)S(1)} all-gather(f32[128,128]{1,0:T(8,128)S(1)} %get-tuple-element.52), channel_id=2, replica_groups=mesh['src'=4,'depth'=8,'lat'=16] {'src'}, dimensions={0}, use_global_device_ids=true | all-gather | bytes 327680 | tf_op jit(solution)/shard_map/all_gather | solution.py:862
  52.6 1.2 %all-to-all-done.got = f32[16,2,128]{2,1,0:T(2,128)S(1)} async-done(((f32[16,2,128]{2,1,0:T(2,128)}), f32[16,2,128]{2,1,0:T(2,128)S(1)}, u32[]{:S(2)}, u32[]{:S(2)}) %all-to-all-start) | async-done | bytes 16416 | tf_op jit(solution)/shard_map/all_to_all | solution.py:861
  53.8 0.7 %finish.1 = (f32[128,128]{1,0:T(8,128)}, f32[2,9,2,16]{3,2,1,0:T(2,128)}) custom-call(f32[128,128]{1,0:T(8,128)S(1)} %get-tuple-element.59.mine, f32[128,128]{1,0:T(8,128)S(1)} %get-tuple-element.58.theirs, f32[16,2,128]{2,1,0:T(2,128)S(1)} %all-to-all-done.got), custom_call_target="tpu_custom_call" | custom-call | tf_op jit(solution)/shard_map/finish/pallas_call | solution.py:801
  (1 shorter events, 0.0 us)
Async XLA Ops:
  0.6 14.8 %copy-start.1 = (s32[2]{0:T(128)S(1)}, s32[2]{0:T(128)}, u32[]{:S(2)}) copy-start(s32[2]{0:T(128)} %tow.5) | copy-start | bytes 28
  0.6 14.8 %copy-start = (f32[2,3]{1,0:T(2,128)S(1)}, f32[2,3]{1,0:T(2,128)}, u32[]{:S(2)}) copy-start(f32[2,3]{1,0:T(2,128)} %amp.5) | copy-start | bytes 76
  1.8 19.2 %copy-start.2 = (s32[1,1,16]{2,1,0:T(1,128)S(1)}, s32[1,1,16]{2,1,0:T(1,128)}, u32[]{:S(2)}) copy-start(s32[1,1,16]{2,1,0:T(1,128)} %param.16) | copy-start | bytes 196
  1.8 10.1 %collective-permute-start = (f32[2,3,88,128]{3,2,1,0:T(8,128)S(1)}, f32[2,3,88,128]{3,2,1,0:T(8,128)S(1)}, u32[]{:S(2)}, u32[]{:S(2)}) collective-permute-start(f32[2,3,88,128]{3,2,1,0:T(8,128)S(1)} %get-tuple-element.34), channel_id=1, source_target_pairs={{0,16},{16,0},{32,48},{48,32},{64,80},{80,64},{96,112},{112,96},{1... | collective-permute-start | bytes 811016 | tf_op jit(solution)/shard_map/ppermute | solution.py:29
  4.4 11.0 %collective-permute-start.1 = (f32[2,3,88,128]{3,2,1,0:T(8,128)S(1)}, f32[2,3,88,128]{3,2,1,0:T(8,128)S(1)}, u32[]{:S(2)}, u32[]{:S(2)}) collective-permute-start(f32[2,3,88,128]{3,2,1,0:T(8,128)S(1)} %get-tuple-element.35), channel_id=1, source_target_pairs={{16,32},{32,16},{48,64},{64,48},{80,96},{96,80},{17,33},{33,17},{4... | collective-permute-start | bytes 811016 | tf_op jit(solution)/shard_map/ppermute | solution.py:29
  15.5 12.7 %copy-start.3 = (s32[1,1,16,1]{2,3,1,0:T(1,128)S(1)}, s32[1,1,16,1]{2,3,1,0:T(1,128)}, u32[]{:S(2)}) copy-start(s32[1,1,16,1]{2,3,1,0:T(1,128)} %param.17) | copy-start | bytes 196
  16.6 11.6 %collective-permute-start.2 = (f32[2,256,128]{2,1,0:T(8,128)S(1)}, f32[2,256,128]{2,1,0:T(8,128)S(1)}, u32[]{:S(2)}, u32[]{:S(2)}) collective-permute-start(f32[2,256,128]{2,1,0:T(8,128)S(1)} %get-tuple-element.50), channel_id=1, source_target_pairs={{0,1},{1,2},{2,3},{3,4},{4,5},{5,6},{6,7},{7,8},{8,9},{9,10},{10,1... | collective-permute-start | bytes 786440 | tf_op jit(solution)/shard_map/ppermute | solution.py:23
  19.7 8.5 %collective-permute-start.3 = (f32[2,216,128]{2,1,0:T(8,128)S(1)}, f32[2,216,128]{2,1,0:T(8,128)S(1)}, u32[]{:S(2)}, u32[]{:S(2)}) collective-permute-start(f32[2,216,128]{2,1,0:T(8,128)S(1)} %get-tuple-element.51), channel_id=1, source_target_pairs={{1,0},{2,1},{3,2},{4,3},{5,4},{6,5},{7,6},{8,7},{9,8},{10,9},{11,1... | collective-permute-start | bytes 663560 | tf_op jit(solution)/shard_map/ppermute | solution.py:23
  30.9 22.9 %all-to-all-start = ((f32[16,2,128]{2,1,0:T(2,128)}), f32[16,2,128]{2,1,0:T(2,128)S(1)}, u32[]{:S(2)}, u32[]{:S(2)}) async-start(f32[16,2,128]{2,1,0:T(2,128)} %get-tuple-element.53), calls=%async_computation | async-start | bytes 32768 | tf_op jit(solution)/shard_map/all_to_all | solution.py:861

commit v4 on v3

--- a/solution.py
+++ b/solution.py
@@ -139,17 +139,8 @@
     )(e, h, le, lh, cond)
 
 
-TO_LO = ((3, 17),) * 2 + ((2, 16),) * 2 + ((2, 15),) + ((1, 15),) * 2 + ((2, 16),) * 2 + ((1, 15),) * 2
-TO_HI = (
-    ((3, 17),) * 2
-    + ((2, 17),)
-    + ((2, 16),) * 2
-    + ((2, 15),)
-    + ((1, 15),) * 2
-    + ((2, 16),) * 2
-    + ((1, 16),)
-    + ((1, 15),) * 2
-)
+TO_LO = ((3, 17),) * 2 + (((2, 16),) * 2 + ((1, 15),) * 2) * 2
+TO_HI = ((2, 17),) * 2 + (((1, 16),) * 2 + ((0, 15),) * 2) * 2
 
 
 def offset(table, k):
@@ -164,7 +155,8 @@
     lo, hi = table[k]
     at = offset(table, k)
     ref[g, at : at + hi + 1] = value[0 : hi + 1]
-    ref[g, at + hi + 1 : at + hi + 1 + lo] = value[ROWS - lo : ROWS]
+    if lo:
+        ref[g, at + hi + 1 : at + hi + 1 + lo] = value[ROWS - lo : ROWS]
 
 
 def get_plane(ref, table, g, k):
@@ -324,7 +316,7 @@
         cell = tow[g]
         lz = cell // (1024 * lat_n) - depth_at * 16
         lx = cell // 128 % (8 * lat_n) - lat_at * 8
-        point = jnp.where((z == lz) & (lane == cell % 128), amp[g, 0], 0.0)
+        point = jnp.where((z == lz) & (lane == cell % 128), 1.0, 0.0)
 
         def e0(x):
             return tuple(te[g, c, x] for c in range(3))
@@ -338,40 +330,45 @@
         def put(ref, k, value):
             put_plane(ref, TO_LO if ref is to_lo else TO_HI, g, k, value)
 
+        def hit(x, n):
+            return jnp.where(lx == x, amp[g, n], 0.0) * point
+
+        zero = (None, 0.0, 0.0)
         a0, b0, a1, b1 = ta[0], tb[0], ta[1], tb[1]
         f0, f1 = e0(0), e0(1)
-        h1 = step_h(0)
+        h1, k1 = step_h(0), step_h(1)
         put(to_lo, 0, f0[1])
         put(to_lo, 1, f0[2])
-        put(to_lo, 2, a0 * f0[1] + b0 * (dmz(h1[0]) - h1[2]))
-        put(to_lo, 3, a0 * f0[2] + b0 * (h1[1] - dmy(h1[0])))
-        put(to_lo, 4, h1[0])
-        hit = jnp.where(lx == 0, point, 0.0)
-        ex = a0 * f0[0] + b0 * (dmy(h1[2]) - dmz(h1[1]) - hit)
-        k1 = step_h(1)
-        ey1 = a1 * f1[1] + b1 * (dmz(k1[0]) - k1[2] + h1[2])
-        ez1 = a1 * f1[2] + b1 * (k1[1] - h1[1] - dmy(k1[0]))
-        put(to_lo, 5, h1[1] + s * (dpz(ex) - ez1))
-        put(to_lo, 6, h1[2] + s * (ey1 - dpy(ex)))
+        m = curl_m(h1, zero)
+        e1 = (a0 * f0[0] + b0 * (m[0] - hit(0, 0)), a0 * f0[1] + b0 * m[1], a0 * f0[2] + b0 * m[2])
+        put(to_lo, 2, e1[1])
+        put(to_lo, 3, e1[2])
+        m = curl_m(k1, h1)
+        k = curl_p(e1, (None, a1 * f1[1] + b1 * m[1], a1 * f1[2] + b1 * m[2]))
+        h2 = tuple(h1[c] + s * k[c] for c in range(3))
+        m = curl_m(h2, zero)
+        put(to_lo, 4, a0 * e1[1] + b0 * m[1])
+        put(to_lo, 5, a0 * e1[2] + b0 * m[2])
         a7, b7, a6, b6 = ta[7], tb[7], ta[6], tb[6]
         f7, f6 = e0(7), e0(6)
-        g7 = h0(7)
-        put(to_hi, 0, g7[1] + s * (dpz(f7[0]) + f7[2]))
-        put(to_hi, 1, g7[2] - s * (f7[1] + dpy(f7[0])))
-        put(to_hi, 2, f7[0])
-        hx7 = g7[0] + s * (dpy(f7[2]) - dpz(f7[1]))
-        h6 = step_h(6)
-        put(to_hi, 3, a7 * f7[1] + b7 * (dmz(hx7) + h6[2]))
-        put(to_hi, 4, a7 * f7[2] - b7 * (h6[1] + dmy(hx7)))
-        put(to_hi, 5, hx7)
-        h5 = step_h(5)
-        m6 = curl_m(h6, h5)
-        hit = jnp.where(lx == 6, point, 0.0)
-        ex6 = a6 * f6[0] + b6 * (m6[0] - hit)
-        ey6 = a6 * f6[1] + b6 * m6[1]
-        ez6 = a6 * f6[2] + b6 * m6[2]
-        put(to_hi, 6, h6[1] + s * (dpz(ex6) + ez6))
-        put(to_hi, 7, h6[2] - s * (ey6 + dpy(ex6)))
+        k = curl_p(f7, zero)
+        h7 = tuple(f + s * t for f, t in zip(h0(7), k))
+        put(to_hi, 0, h7[1])
+        put(to_hi, 1, h7[2])
+        h6, h5 = step_h(6), step_h(5)
+        m7, m6 = curl_m(h7, h6), curl_m(h6, h5)
+        e7 = (a7 * f7[0] + b7 * (m7[0] - hit(7, 0)), a7 * f7[1] + b7 * m7[1], a7 * f7[2] + b7 * m7[2])
+        e6 = (a6 * f6[0] + b6 * (m6[0] - hit(6, 0)), a6 * f6[1] + b6 * m6[1], a6 * f6[2] + b6 * m6[2])
+        k7, k6 = curl_p(e7, zero), curl_p(e6, e7)
+        h7 = tuple(h7[c] + s * k7[c] for c in range(3))
+        h6 = tuple(h6[c] + s * k6[c] for c in range(3))
+        put(to_hi, 2, h7[1])
+        put(to_hi, 3, h7[2])
+        m7 = curl_m(h7, h6)
+        e7 = (a7 * e7[0] + b7 * (m7[0] - hit(7, 1)), a7 * e7[1] + b7 * m7[1], a7 * e7[2] + b7 * m7[2])
+        k7 = curl_p(e7, zero)
+        put(to_hi, 4, h7[1] + s * k7[1])
+        put(to_hi, 5, h7[2] + s * k7[2])
         s = row_mask
 
         def l0(x):
@@ -387,19 +384,20 @@
             return tuple(f + s * k for f, k in zip(m0(x), curl_p(w0(x), w0(x + 1))))
 
         q0, v0 = l0(0), w0(0)
-        m1 = step_m(0)
-        put(to_lo, 7, v0[1])
-        put(to_lo, 8, v0[2])
-        put(to_lo, 9, a0 * q0[1] - CC * (dmz(m1[0]) - m1[2]))
-        put(to_lo, 10, a0 * q0[2] - CC * (m1[1] - dmy(m1[0])))
-        q7, v7, n7 = l0(7), w0(7), m0(7)
-        put(to_hi, 8, n7[1] + s * (dpz(v7[0]) + v7[2]))
-        put(to_hi, 9, n7[2] - s * (v7[1] + dpy(v7[0])))
-        put(to_hi, 10, q7[0])
-        mx7 = n7[0] + s * (dpy(v7[2]) - dpz(v7[1]))
-        m6 = step_m(6)
-        put(to_hi, 11, a7 * q7[1] - CC * (dmz(mx7) + m6[2]))
-        put(to_hi, 12, a7 * q7[2] + CC * (m6[1] + dmy(mx7)))
+        put(to_lo, 6, v0[1])
+        put(to_lo, 7, v0[2])
+        m = curl_m(step_m(0), zero)
+        put(to_lo, 8, a0 * q0[1] - CC * m[1])
+        put(to_lo, 9, a0 * q0[2] - CC * m[2])
+        q7 = l0(7)
+        k7 = curl_p(w0(7), zero)
+        n7 = tuple(f + s * t for f, t in zip(m0(7), k7))
+        put(to_hi, 6, n7[1])
+        put(to_hi, 7, n7[2])
+        m = curl_m(n7, step_m(6))
+        k7 = curl_p(tuple(b7 * (a7 * q7[c] - CC * m[c]) for c in range(3)), zero)
+        put(to_hi, 8, n7[1] + s * k7[1])
+        put(to_hi, 9, n7[2] + s * k7[2])
         return carry
 
     lax.fori_loop(0, groups, forward_planes, 0, unroll=True)
@@ -627,7 +625,6 @@
 
         lx, point = tow_at(tow, g, depth_at, lat_at, lat_n)
         s = row_mask
-        p, q = 7, 8
 
         def m_of(n, x):
             return triple(mm if n <= x <= 6 - n else mo, g, x)
@@ -658,22 +655,18 @@
                 for c in range(3):
                     out[g, c, x] = ta[x] * old[c] - CC * k[c]
 
-        m_step(0, (None, high(p), high(p + 1)))
+        m_step(0, (None, high(6), high(7)))
         first = lam(0, g, 0)
-        my = left * (low(q) - s * (tb[0] * first[2]))
-        mz = left * (low(q + 1) + s * (tb[0] * first[1]))
-        l_step(0, (None, my, mz))
+        dy, dz = -s * (tb[0] * first[2]), s * (tb[0] * first[1])
+        l_step(0, (None, left * (low(6) + dy), left * (low(7) + dz)))
         last = m_of(0, 7)
-        m_step(1, (None, b8 * (high(p + 2) - CC * last[2]), b8 * (high(p + 3) + CC * last[1])))
-        wx = bl * (al * low(q + 2) - CC * (dmy(mz) - dmz(my)))
-        wy = bl * (low(q + 3) + CC * mz)
-        wz = bl * (low(q + 4) - CC * my)
+        m_step(1, (None, b8 * (high(8) - CC * last[2]), b8 * (high(9) + CC * last[1])))
+        wx, wy, wz = -CC * bl * (dmy(dz) - dmz(dy)), CC * bl * dz, -CC * bl * dy
         first = lam(1, g, 0)
-        my = left * (my + s * (dpz(wx) - (tb[0] * first[2] - wz)))
-        mz = left * (mz + s * ((tb[0] * first[1] - wy) - dpy(wx)))
-        l_step(1, (None, my, mz))
+        dy = dy + s * (dpz(wx) - (tb[0] * first[2] - wz))
+        dz = dz + s * ((tb[0] * first[1] - wy) - dpy(wx))
+        l_step(1, (None, left * (low(8) + dy), left * (low(9) + dz)))
         s = -CC * row_mask
-        p, q = 0, 0
 
         def e_of(n, x):
             if n == 0:
@@ -707,42 +700,38 @@
                     eo[e_at(g, n, c, x), :] = ta[x] * old[c] + tb[x] * k[c]
                 total[x] += weighted(old, k, lam(2 - n, g, x))
 
-        def drop(n):
-            return jnp.where(lx == -1, amp[g, n], 0.0) * point
-
-        h_step(0, (None, high(p), high(p + 1)))
+        h_step(0, (None, high(0), high(1)))
         first = e_of(0, 0)
-        hy = left * (low(q) - s * first[2])
-        hz = left * (low(q + 1) + s * first[1])
-        e_step(0, (None, hy, hz))
+        dy, dz = -s * first[2], s * first[1]
+        e_step(0, (None, left * (low(0) + dy), left * (low(1) + dz)))
         last = h_of(0, 7)
-        ey8 = high(p + 2) + b8 * last[2]
-        ez8 = high(p + 3) - b8 * last[1]
-        ex = al * low(q + 2) + bl * (dmy(hz) - dmz(hy) - drop(0))
-        ey = low(q + 3) - bl * hz
-        ez = low(q + 4) + bl * hy
-        h_step(1, (None, ey8, ez8))
+        uy, uz = b8 * last[2], -b8 * last[1]
+        h_step(1, (None, high(2) + uy, high(3) + uz))
+        ex, ey, ez = bl * (dmy(dz) - dmz(dy)), -bl * dz, bl * dy
         first = e_of(1, 0)
-        hy2 = left * (hy + s * (dpz(ex) - (first[2] - ez)))
-        hz2 = left * (hz + s * ((first[1] - ey) - dpy(ex)))
-        e_step(1, (None, hy2, hz2))
+        dy = dy + s * (dpz(ex) - (first[2] - ez))
+        dz = dz + s * ((first[1] - ey) - dpy(ex))
+        e_step(1, (None, left * (low(2) + dy), left * (low(3) + dz)))
         last = h_of(1, 7)
-        gx = high(p + 4) + s * (dpy(ez8) - dpz(ey8))
-        gy = high(p + 5) + s * ez8
-        gz = high(p + 6) - s * ey8
-        ey9 = a8 * ey8 + b8 * (dmz(gx) - gz + last[2])
-        ez9 = a8 * ez8 + b8 * (gy - last[1] - dmy(gx))
-        hx2 = low(q + 5) + s * (dpy(ez) - dpz(ey))
-        hyf = low(q + 6) - s * ez
-        hzf = low(q + 7) + s * ey
-        ex2 = al * ex + bl * (dmy(hz2) - dmz(hy2) - drop(1))
-        ey2 = al * ey + bl * (dmz(hx2) - hz2 + hzf)
-        ez2 = al * ez + bl * (hy2 - hyf - dmy(hx2))
-        h_step(2, (None, ey9, ez9))
+        gx, gy, gz = s * (dpy(uz) - dpz(uy)), s * uz, -s * uy
+        h_step(
+            2,
+            (
+                None,
+                high(4) + a8 * uy + b8 * (dmz(gx) - gz + last[2]),
+                high(5) + a8 * uz + b8 * (gy - last[1] - dmy(gx)),
+            ),
+        )
+        hx, hy, hz = s * (dpy(ez) - dpz(ey)), -s * ez, s * ey
+        ex, ey, ez = (
+            al * ex + bl * (dmy(dz) - dmz(dy)),
+            al * ey + bl * (dmz(hx) - dz + hz),
+            al * ez + bl * (dy - hy - dmy(hx)),
+        )
         first = e_of(2, 0)
-        hy3 = left * (hy2 + s * (dpz(ex2) - (first[2] - ez2)))
-        hz3 = left * (hz2 + s * ((first[1] - ey2) - dpy(ex2)))
-        e_step(2, (None, hy3, hz3))
+        dy = dy + s * (dpz(ex) - (first[2] - ez))
+        dz = dz + s * ((first[1] - ey) - dpy(ex))
+        e_step(2, (None, left * (low(4) + dy), left * (low(5) + dz)))
         return carry
 
     lax.fori_loop(0, groups, one_group, 0, unroll=True)

time: 54.8 us -> 52.9 us (0.965)
  the two profiles are of different devices: /device:TPU:36 before, /device:TPU:32 now
where the time goes in v4:
time: 52.9 us; the launch traced here: 52.6 us
  starting transfers between devices  22.9 us (43%)
  waiting for transfers between devices  12.2 us (23%)
  Pallas kernels  9.38 us (18%)
  blocking collectives  7.32 us (14%)
  between operations  0.73 us (1%)
    all_to_all x1, starting transfers between devices, per_device(): got = lax.all_to_all(send, 'lat', split_axis=0, concat_axis=0, tiled=True)  12.3 us
    ppermute x2, waiting for transfers between devices, swapped(): lax.ppermute(block, axis, [p for i in lower for p in ((i, i + 1), (i + 1,...  7.43 us
    all_gather x1, blocking collectives, per_device(): every = lax.all_gather(grad, 'src', axis=0, tiled=False)  7.32 us
    ppermute x2, starting transfers between devices, shifted(): return lax.ppermute(block, axis, route)  5.84 us
    ppermute x2, starting transfers between devices, swapped(): lax.ppermute(block, axis, [p for i in lower for p in ((i, i + 1), (i + 1,...  4.72 us
    ppermute x2, waiting for transfers between devices, shifted(): return lax.ppermute(block, axis, route)  3.6 us
    pallas_call x1, Pallas kernels, outer(): pl.pallas_call(functools.partial(outer_kernel, depth_n, lat_n), out_shape...  2.67 us
    pallas_call x1, Pallas kernels, inner(): pl.pallas_call(functools.partial(inner_kernel, lat_n), out_shape=(field,...  2.16 us
  transfers between devices with their start and end apart: 5, of which 4 were waited for; matrix products, arithmetic and copies ran while one was open for 0% of the time, Pallas kernels for 7%

profile of v4, /device:TPU:32, one launch (start us, length us, event | category | flops | bytes accessed | tf_op | source)
XLA Modules:
  0.0 52.6 jit_solution(12802271867691915145)
XLA Ops:
  0.6 0.0 copy-start.1
  0.6 0.0 copy-start
  0.6 1.1 %pack.1 = (f32[2,3,88,128]{3,2,1,0:T(8,128)S(1)}, f32[2,3,88,128]{3,2,1,0:T(8,128)S(1)}) custom-call(f32[2,3,128,128]{3,2,1,0:T(8,128)} %bitcast.16, f32[2,3,128,128]{3,2,1,0:T(8,128)} %bitcast.18, f32[2,3,128,128]{3,2,1,0:T(8,128)} %bitcast.20, f32[2,3,128,128]{3,2,1,0:T(8,128)} %bitcast.22, f32[128,128]{1,0:T(8,128)} %bitcast.24), custom_call_target="tpu_custom_call" | custom-call | tf_op jit(solution)/shard_map/pack/pallas_call | solution.py:131
  1.8 0.0 copy-start.2
  1.8 2.6 %collective-permute-start = (f32[2,3,88,128]{3,2,1,0:T(8,128)S(1)}, f32[2,3,88,128]{3,2,1,0:T(8,128)S(1)}, u32[]{:S(2)}, u32[]{:S(2)}) collective-permute-start(f32[2,3,88,128]{3,2,1,0:T(8,128)S(1)} %get-tuple-element.34), channel_id=1, source_target_pairs={{0,16},{16,0},{32,48},{48,32},{64,80},{80,64},{96,112},{112,96},{1... | collective-permute-start | bytes 811016 | tf_op jit(solution)/shard_map/ppermute | solution.py:29
  4.4 2.1 %collective-permute-start.1 = (f32[2,3,88,128]{3,2,1,0:T(8,128)S(1)}, f32[2,3,88,128]{3,2,1,0:T(8,128)S(1)}, u32[]{:S(2)}, u32[]{:S(2)}) collective-permute-start(f32[2,3,88,128]{3,2,1,0:T(8,128)S(1)} %get-tuple-element.35), channel_id=1, source_target_pairs={{16,32},{32,16},{48,64},{64,48},{80,96},{96,80},{17,33},{33,17},{4... | collective-permute-start | bytes 811016 | tf_op jit(solution)/shard_map/ppermute | solution.py:29
  6.5 1.5 %own.1 = (f32[2,3,8,24,128]{4,3,2,1,0:T(8,128)S(1)}, f32[2,3,8,24,128]{4,3,2,1,0:T(8,128)S(1)}, f32[2,3,8,24,128]{4,3,2,1,0:T(8,128)S(1)}, f32[2,3,8,24,128]{4,3,2,1,0:T(8,128)S(1)}, f32[8,16,128]{2,1,0:T(8,128)S(1)}) custom-call(f32[2,3,128,128]{3,2,1,0:T(8,128)} %bitcast.17, f32[2,3,128,128]{3,2,1,0:T(8,128)} %bitcast.19, f32[2,3,128,128]{3,2,1,0:T(8,128)} %bitcast.21, ...), custom_call_target="tpu_custom_call" | custom-call | flops 5000000 | bytes 8000000 | tf_op jit(solution)/shard_map/own/pallas_call | solution.py:231
  8.0 3.9 %collective-permute-done.one = f32[2,3,88,128]{3,2,1,0:T(8,128)S(1)} collective-permute-done((f32[2,3,88,128]{3,2,1,0:T(8,128)S(1)}, f32[2,3,88,128]{3,2,1,0:T(8,128)S(1)}, u32[]{:S(2)}, u32[]{:S(2)}) %collective-permute-start) | collective-permute-done | bytes 270368 | tf_op jit(solution)/shard_map/ppermute | solution.py:29
  11.9 3.5 %collective-permute-done.1.two = f32[2,3,88,128]{3,2,1,0:T(8,128)S(1)} collective-permute-done((f32[2,3,88,128]{3,2,1,0:T(8,128)S(1)}, f32[2,3,88,128]{3,2,1,0:T(8,128)S(1)}, u32[]{:S(2)}, u32[]{:S(2)}) %collective-permute-start.1) | collective-permute-done | bytes 270368 | tf_op jit(solution)/shard_map/ppermute | solution.py:29
  15.5 0.0 copy-done.1
  15.5 0.0 copy-done
  15.5 0.0 copy-start.3
  15.5 1.2 %planes.1 = (f32[2,3,8,24,128]{4,3,2,1,0:T(8,128)S(1)}, f32[2,3,8,24,128]{4,3,2,1,0:T(8,128)S(1)}, f32[2,3,8,24,128]{4,3,2,1,0:T(8,128)S(1)}, f32[2,3,8,24,128]{...) custom-call(f32[2,3,8,24,128]{4,3,2,1,0:T(8,128)S(1)} %get-tuple-ele, ...), custom_call_target="tpu_custom_call", output_to_operand_aliasing={{0}: (0, {}), {1}: (1, {}), {2}: (2, {}), {3}: (3, {})} | custom-call | tf_op jit(solution)/shard_map/planes/pallas_call | solution.py:412
  16.7 1.3 %collective-permute-start.3 = (f32[2,200,128]{2,1,0:T(8,128)S(1)}, f32[2,200,128]{2,1,0:T(8,128)S(1)}, u32[]{:S(2)}, u32[]{:S(2)}) collective-permute-start(f32[2,200,128]{2,1,0:T(8,128)S(1)} %get-tuple-element.51), channel_id=1, source_target_pairs={{1,0},{2,1},{3,2},{4,3},{5,4},{6,5},{7,6},{8,7},{9,8},{10,9},{11,1... | collective-permute-start | bytes 614408 | tf_op jit(solution)/shard_map/ppermute | solution.py:23
  18.0 4.6 %collective-permute-start.2 = (f32[2,192,128]{2,1,0:T(8,128)S(1)}, f32[2,192,128]{2,1,0:T(8,128)S(1)}, u32[]{:S(2)}, u32[]{:S(2)}) collective-permute-start(f32[2,192,128]{2,1,0:T(8,128)S(1)} %get-tuple-element.50), channel_id=1, source_target_pairs={{0,1},{1,2},{2,3},{3,4},{4,5},{5,6},{6,7},{7,8},{8,9},{9,10},{10,1... | collective-permute-start | bytes 589832 | tf_op jit(solution)/shard_map/ppermute | solution.py:23
  22.6 0.0 copy-done.2
  22.6 2.2 %inner.1 = (f32[2,3,8,24,128]{4,3,2,1,0:T(8,128)S(1)}, f32[2,3,8,24,128]{4,3,2,1,0:T(8,128)S(1)}, f32[2,3,8,24,128]{4,3,2,1,0:T(8,128)S(1)}, f32[2,3,8,24,128]{4...) custom-call(f32[2,3,8,24,128]{4,3,2,1,0:T(8,128)S(1)} %get-tuple-ele, ...), custom_call_target="tpu_custom_call" | custom-call | flops 20000000 | bytes 12000000 | tf_op jit(solution)/shard_map/inner/pallas_call | solution.py:550
  24.7 3.6 %collective-permute-done.2.lo = f32[2,192,128]{2,1,0:T(8,128)S(1)} collective-permute-done((f32[2,192,128]{2,1,0:T(8,128)S(1)}, f32[2,192,128]{2,1,0:T(8,128)S(1)}, u32[]{:S(2)}, u32[]{:S(2)}) %collective-permute-start.2) | collective-permute-done | bytes 196640 | tf_op jit(solution)/shard_map/ppermute | solution.py:23
  28.3 0.0 collective-permute-done.3.hi
  28.3 0.0 copy-done.3
  28.3 2.7 %outer.1 = (f32[128,128]{1,0:T(8,128)S(1)}, f32[16,2,128]{2,1,0:T(2,128)}) custom-call(f32[2,3,8,24,128]{4,3,2,1,0:T(8,128)S(1)} %get-tuple-element.36.te, f32[2,3,8,24,128]{4,3,2,1,0:T(8,128)S(1)} %get-tuple-element.37.th, f32[2,3,8,24,128]{4,3,2,1,0:T(8,128)S(1)} %get-tuple-element.38.tle, f32[2,3,8,24,128]{4,3,2,1,0:T(8,128)S(1)} %get-tuple-element.39.tlh, ...), custom_call_target="tpu_custom_call" | custom-call | flops 10000000 | bytes 12000000 | tf_op jit(solution)/shard_map/outer/pallas_call | solution.py:763
  31.0 12.3 %all-to-all-start = ((f32[16,2,128]{2,1,0:T(2,128)}), f32[16,2,128]{2,1,0:T(2,128)S(1)}, u32[]{:S(2)}, u32[]{:S(2)}) async-start(f32[16,2,128]{2,1,0:T(2,128)} %get-tuple-element.53), calls=%async_computation | async-start | bytes 32768 | tf_op jit(solution)/shard_map/all_to_all | solution.py:850
  43.3 7.3 %all-gather = f32[512,128]{1,0:T(8,128)S(1)} all-gather(f32[128,128]{1,0:T(8,128)S(1)} %get-tuple-element.52), channel_id=2, replica_groups=mesh['src'=4,'depth'=8,'lat'=16] {'src'}, dimensions={0}, use_global_device_ids=true | all-gather | bytes 327680 | tf_op jit(solution)/shard_map/all_gather | solution.py:851
  50.7 1.2 %all-to-all-done.got = f32[16,2,128]{2,1,0:T(2,128)S(1)} async-done(((f32[16,2,128]{2,1,0:T(2,128)}), f32[16,2,128]{2,1,0:T(2,128)S(1)}, u32[]{:S(2)}, u32[]{:S(2)}) %all-to-all-start) | async-done | bytes 16416 | tf_op jit(solution)/shard_map/all_to_all | solution.py:850
  51.9 0.7 %finish.1 = (f32[128,128]{1,0:T(8,128)}, f32[2,9,2,16]{3,2,1,0:T(2,128)}) custom-call(f32[128,128]{1,0:T(8,128)S(1)} %get-tuple-element.59.mine, f32[128,128]{1,0:T(8,128)S(1)} %get-tuple-element.58.theirs, f32[16,2,128]{2,1,0:T(2,128)S(1)} %all-to-all-done.got), custom_call_target="tpu_custom_call" | custom-call | tf_op jit(solution)/shard_map/finish/pallas_call | solution.py:790
  (1 shorter events, 0.0 us)
Async XLA Ops:
  0.6 14.8 %copy-start.1 = (s32[2]{0:T(128)S(1)}, s32[2]{0:T(128)}, u32[]{:S(2)}) copy-start(s32[2]{0:T(128)} %tow.5) | copy-start | bytes 28
  0.6 14.8 %copy-start = (f32[2,3]{1,0:T(2,128)S(1)}, f32[2,3]{1,0:T(2,128)}, u32[]{:S(2)}) copy-start(f32[2,3]{1,0:T(2,128)} %amp.5) | copy-start | bytes 76
  1.8 20.8 %copy-start.2 = (s32[1,1,16]{2,1,0:T(1,128)S(1)}, s32[1,1,16]{2,1,0:T(1,128)}, u32[]{:S(2)}) copy-start(s32[1,1,16]{2,1,0:T(1,128)} %param.16) | copy-start | bytes 196
  1.8 10.1 %collective-permute-start = (f32[2,3,88,128]{3,2,1,0:T(8,128)S(1)}, f32[2,3,88,128]{3,2,1,0:T(8,128)S(1)}, u32[]{:S(2)}, u32[]{:S(2)}) collective-permute-start(f32[2,3,88,128]{3,2,1,0:T(8,128)S(1)} %get-tuple-element.34), channel_id=1, source_target_pairs={{0,16},{16,0},{32,48},{48,32},{64,80},{80,64},{96,112},{112,96},{1... | collective-permute-start | bytes 811016 | tf_op jit(solution)/shard_map/ppermute | solution.py:29
  4.4 11.0 %collective-permute-start.1 = (f32[2,3,88,128]{3,2,1,0:T(8,128)S(1)}, f32[2,3,88,128]{3,2,1,0:T(8,128)S(1)}, u32[]{:S(2)}, u32[]{:S(2)}) collective-permute-start(f32[2,3,88,128]{3,2,1,0:T(8,128)S(1)} %get-tuple-element.35), channel_id=1, source_target_pairs={{16,32},{32,16},{48,64},{64,48},{80,96},{96,80},{17,33},{33,17},{4... | collective-permute-start | bytes 811016 | tf_op jit(solution)/shard_map/ppermute | solution.py:29
  15.5 12.9 %copy-start.3 = (s32[1,1,16,1]{2,3,1,0:T(1,128)S(1)}, s32[1,1,16,1]{2,3,1,0:T(1,128)}, u32[]{:S(2)}) copy-start(s32[1,1,16,1]{2,3,1,0:T(1,128)} %param.17) | copy-start | bytes 196
  16.7 11.6 %collective-permute-start.3 = (f32[2,200,128]{2,1,0:T(8,128)S(1)}, f32[2,200,128]{2,1,0:T(8,128)S(1)}, u32[]{:S(2)}, u32[]{:S(2)}) collective-permute-start(f32[2,200,128]{2,1,0:T(8,128)S(1)} %get-tuple-element.51), channel_id=1, source_target_pairs={{1,0},{2,1},{3,2},{4,3},{5,4},{6,5},{7,6},{8,7},{9,8},{10,9},{11,1... | collective-permute-start | bytes 614408 | tf_op jit(solution)/shard_map/ppermute | solution.py:23
  18.0 10.3 %collective-permute-start.2 = (f32[2,192,128]{2,1,0:T(8,128)S(1)}, f32[2,192,128]{2,1,0:T(8,128)S(1)}, u32[]{:S(2)}, u32[]{:S(2)}) collective-permute-start(f32[2,192,128]{2,1,0:T(8,128)S(1)} %get-tuple-element.50), channel_id=1, source_target_pairs={{0,1},{1,2},{2,3},{3,4},{4,5},{5,6},{6,7},{7,8},{8,9},{9,10},{10,1... | collective-permute-start | bytes 589832 | tf_op jit(solution)/shard_map/ppermute | solution.py:23
  31.0 20.9 %all-to-all-start = ((f32[16,2,128]{2,1,0:T(2,128)}), f32[16,2,128]{2,1,0:T(2,128)S(1)}, u32[]{:S(2)}, u32[]{:S(2)}) async-start(f32[16,2,128]{2,1,0:T(2,128)} %get-tuple-element.53), calls=%async_computation | async-start | bytes 32768 | tf_op jit(solution)/shard_map/all_to_all | solution.py:850

commit v5 on v4

--- a/solution.py
+++ b/solution.py
@@ -11,10 +11,9 @@
 KK = 0.5
 ROWS = 24
 F32 = jnp.float32
-UP = ((0, 3), (3, 2), (5, 2), (7, 1), (8, 2))
-DN = ((0, 3), (3, 3), (6, 2), (8, 2), (10, 2))
-UP_ROWS = 9
-DN_ROWS = 11
+UP = (0, 2, 4, 5)
+DN = (1, 4, 5, 7)
+SPAN = 8
 
 
 def shifted(block, axis, distance):
@@ -29,8 +28,8 @@
     return lax.ppermute(block, axis, [p for i in lower for p in ((i, i + 1), (i + 1, i))])
 
 
-def lanes():
-    return lax.broadcasted_iota(jnp.int32, (ROWS, 128), 1)
+def lanes(rows=ROWS):
+    return lax.broadcasted_iota(jnp.int32, (rows, 128), 1)
 
 
 def zrow():
@@ -39,7 +38,7 @@
 
 
 def yp(f):
-    return jnp.where(lanes() == 127, 0.0, pltpu.roll(f, 127, 1))
+    return jnp.where(lanes(f.shape[0]) == 127, 0.0, pltpu.roll(f, 127, 1))
 
 
 def ym(f):
@@ -91,31 +90,103 @@
     return jnp.where((zrow() < 0) & (depth_at == 0), 0.0, 1.0)
 
 
+def unstepped(*rows):
+    z = zrow()
+    done = z == rows[0]
+    for row in rows[1:]:
+        done = done | (z == row)
+    return jnp.where(done, 0.0, 1.0)
+
+
 def last_row_keep(depth_at, depth_n):
     return jnp.logical_not((zrow() > 15) & (depth_at == depth_n - 1))
 
 
-def pack_kernel(e, h, le, lh, cond, one, two, sems):
+def stepped(fields, row, base, s, xp):
+    fx, fy, fz = (fields(c, row) for c in range(3))
+    gx, gy = fields(0, row + 1), fields(1, row + 1)
+    return (
+        base(0, row) + s * (dpy(fz) - (gy - fy)),
+        base(1, row) + s * ((gx - fx) - (xp(fz) - fz)),
+        base(2, row) + s * ((xp(fy) - fy) - dpy(fx)),
+    )
+
+
+def pack_kernel(e, h, le, lh, cond, one, two, ve, vh, vl, vm, vc, sems):
     even = lax.axis_index("depth") % 2 == 0
+    copies = []
+    for ref, dst in ((e, ve), (h, vh), (le, vl), (lh, vm)):
+        n = dst.shape[2] // 16
+        for k, first in enumerate((0, 16 - n)):
+            copies.append(
+                pltpu.make_async_copy(
+                    ref.at[:, :, pl.ds(first * 8, n * 8)],
+                    dst.at[:, :, pl.ds(k * n * 8, n * 8)],
+                    sems.at[len(copies)],
+                )
+            )
+    for k, first in enumerate((0, 14)):
+        copies.append(
+            pltpu.make_async_copy(
+                cond.at[pl.ds(first * 8, 16)], vc.at[pl.ds(k * 16, 16)], sems.at[len(copies)]
+            )
+        )
+    for c in copies:
+        c.start()
+    for c in copies:
+        c.wait()
+    sub = lax.broadcasted_iota(jnp.int32, (8, 128), 0)
+
+    def xp(f):
+        return jnp.where(sub == 7, 0.0, pltpu.roll(f, 7, 0))
+
+    def tile(ref, g, c, z):
+        n = ref.shape[2] // 16
+        k = z if z < n else z - 16 + 2 * n
+        return ref[g, c, k * 8 : k * 8 + 8]
+
+    def layer(z):
+        k = z if z < 2 else z - 12
+        return vc[k * 8 : k * 8 + 8]
 
     def fill(up, dn):
-        copies = []
-
-        def move(src, dst):
-            c = pltpu.make_async_copy(src, dst, sems.at[len(copies)])
-            c.start()
-            copies.append(c)
-
-        for field, ref in enumerate((e, h, le, lh)):
-            at, n = UP[field]
-            move(ref.at[:, :, pl.ds(0, n * 8)], up.at[:, :, pl.ds(at * 8, n * 8)])
-            at, n = DN[field]
-            move(ref.at[:, :, pl.ds((16 - n) * 8, n * 8)], dn.at[:, :, pl.ds(at * 8, n * 8)])
-        for row in range(2):
-            move(cond.at[pl.ds(row * 8, 8)], up.at[0, row, pl.ds((UP_ROWS - 1) * 8, 8)])
-            move(cond.at[pl.ds((14 + row) * 8, 8)], dn.at[0, row, pl.ds((DN_ROWS - 1) * 8, 8)])
-        for c in copies:
-            c.wait()
+        for g in range(e.shape[0]):
+
+            def e_of(c, z, g=g):
+                return tile(ve, g, c, z)
+
+            def h_of(c, z, g=g):
+                return tile(vh, g, c, z)
+
+            def w_of(c, z, g=g):
+                return CC / (1.0 + KK * layer(z)) * tile(vl, g, c, z)
+
+            def m_of(c, z, g=g):
+                return tile(vm, g, c, z)
+
+            h17 = stepped(e_of, 1, h_of, -CC, xp)
+            h3 = stepped(e_of, 13, h_of, -CC, xp)
+            m16 = stepped(w_of, 0, m_of, 1.0, xp)
+            m2 = stepped(w_of, 14, m_of, 1.0, xp)
+            extra = jnp.where(sub == 0, e_of(2, 13), 0.0)
+            extra = jnp.where(sub == 1, pltpu.roll(tile(vl, g, 2, 14), 1, 0), extra)
+            for c in range(3):
+                blank = jnp.zeros((8, 128), F32)
+                ups = (e_of(c, 0), e_of(c, 1), h_of(c, 0), h17[c], tile(vl, g, c, 0), m16[c])
+                ups += (layer(0), layer(1)) if g == 0 and c == 0 else (blank, blank)
+                dns = (
+                    e_of(c, 14),
+                    e_of(c, 15),
+                    h3[c] if c < 2 else extra,
+                    h_of(c, 14),
+                    h_of(c, 15),
+                    tile(vl, g, c, 15),
+                    m2[c] if c < 2 else layer(14 + g % 2),
+                    m_of(c, 15),
+                )
+                for k in range(SPAN):
+                    up[g, c, k * 8 : k * 8 + 8] = ups[k]
+                    dn[g, c, k * 8 : k * 8 + 8] = dns[k]
 
     @pl.when(even)
     def _():
@@ -127,14 +198,16 @@
 
 
 def pack(e, h, le, lh, cond):
-    message = jax.ShapeDtypeStruct((e.shape[0], 3, DN_ROWS * 8, 128), F32)
+    g = e.shape[0]
+    message = jax.ShapeDtypeStruct((g, 3, SPAN * 8, 128), F32)
     return pl.pallas_call(
         pack_kernel,
         out_shape=(message, message),
         in_specs=[pl.BlockSpec(memory_space=pl.ANY)] * 5,
         out_specs=(pl.BlockSpec(memory_space=pltpu.VMEM),) * 2,
-        scratch_shapes=[pltpu.SemaphoreType.DMA((12,))],
-        compiler_params=pltpu.CompilerParams(vmem_limit_bytes=25165824),
+        scratch_shapes=[pltpu.VMEM((g, 3, 2 * n * 8, 128), F32) for n in (3, 3, 2, 2)]
+        + [pltpu.VMEM((32, 128), F32), pltpu.SemaphoreType.DMA((10,))],
+        compiler_params=pltpu.CompilerParams(vmem_limit_bytes=24 * 1024 * 1024),
         name="pack",
     )(e, h, le, lh, cond)
 
@@ -184,22 +257,6 @@
     rest = ref[1, at + 4 : at + 12]
     rest = jnp.where(r < 4, pltpu.roll(rest, 4, 0), rest)
     return jnp.concatenate([ref[0, at : at + 8], ref[1, at : at + 8], rest], axis=0)
-
-
-def halo_tile(up, dn, lead, x, field):
-    r = lax.broadcasted_iota(jnp.int32, (8, 128), 0)
-    at, _ = UP[field]
-    s = min(at, UP_ROWS - 8)
-    hi = up[(*lead, pl.ds(s * 8 + x, 8, stride=8), slice(None))]
-    if at != s:
-        hi = pltpu.roll(hi, (8 - (at - s)) % 8, 0)
-    at, n = DN[field]
-    s = min(at, DN_ROWS - 8)
-    lo = dn[(*lead, pl.ds(s * 8 + x, 8, stride=8), slice(None))]
-    turn = (8 - n - (at - s)) % 8
-    if turn:
-        lo = pltpu.roll(lo, turn, 0)
-    return jnp.where(r < 4, hi, lo)
 
 
 def own_kernel(e, h, le, lh, cond, te, th, tle, tlh, tc, be, bh, ble, blh, bc, sems):
@@ -268,12 +325,20 @@
 
     even = depth_at % 2 == 0
 
+    r8 = lax.broadcasted_iota(jnp.int32, (8, 128), 0)
+
     def halos(up, dn):
         def halo(g, carry):
             for c in range(3):
-                for field, dst in enumerate((te, th, tle, tlh)):
-                    for x in range(8):
-                        dst[g, c, x, 16:24] = halo_tile(up, dn, (g, c), x, field)
+                for x in range(8):
+                    hi = up[g, c, pl.ds(x, 8, stride=8), :]
+                    lo = dn[g, c, pl.ds(x, 8, stride=8), :]
+                    for field, dst in enumerate((te, th, tle, tlh)):
+                        a = pltpu.roll(hi, 8 - UP[field], 0) if UP[field] else hi
+                        b = pltpu.roll(lo, 7 - DN[field], 0) if DN[field] != 7 else lo
+                        dst[g, c, x, 16:24] = jnp.where(r8 < 4, a, b)
+            te[g, 2, 0, 21:22] = dn[g, 2, 16:17]
+            tle[g, 2, 0, 22:23] = dn[g, 2, 17:18]
             return carry
 
         lax.fori_loop(0, groups, halo, 0)
@@ -287,14 +352,13 @@
         halos(two, one)
 
     keep = last_row_keep(depth_at, depth_n)
-    r8 = lax.broadcasted_iota(jnp.int32, (8, 128), 0)
-
-    def edge(first, second, row, at):
-        rows = pl.ds((at - 1) * 8, 8)
-        return jnp.where(even, first[0, row, rows, :], second[0, row, rows, :])
-
-    u0, u1 = (edge(one, two, row, UP_ROWS) for row in range(2))
-    d0, d1 = (edge(two, one, row, DN_ROWS) for row in range(2))
+
+    def edge(first, second, g, c, slot):
+        rows = pl.ds(slot * 8, 8)
+        return jnp.where(even, first[g, c, rows, :], second[g, c, rows, :])
+
+    u0, u1 = (edge(one, two, 0, 0, 6 + k) for k in range(2))
+    d0, d1 = (edge(two, one, k, 2, 6) for k in range(2))
     for x in range(8):
         rest = jnp.where(r8 == 0, u0[x : x + 1], 1.0)
         rest = jnp.where(r8 == 1, u1[x : x + 1], rest)
@@ -311,8 +375,11 @@
     row_mask = first_row_mask(depth_at)
     z, lane = zrow(), lanes()
 
+    first_e, first_l = unstepped(17, -3), unstepped(16, -2)
+
     def forward_planes(g, carry):
         s = -CC * row_mask
+        s_first = s * first_e
         cell = tow[g]
         lz = cell // (1024 * lat_n) - depth_at * 16
         lx = cell // 128 % (8 * lat_n) - lat_at * 8
@@ -325,7 +392,7 @@
             return tuple(th[g, c, x] for c in range(3))
 
         def step_h(x):
-            return tuple(f + s * k for f, k in zip(h0(x), curl_p(e0(x), e0(x + 1))))
+            return tuple(f + s_first * k for f, k in zip(h0(x), curl_p(e0(x), e0(x + 1))))
 
         def put(ref, k, value):
             put_plane(ref, TO_LO if ref is to_lo else TO_HI, g, k, value)
@@ -352,7 +419,7 @@
         a7, b7, a6, b6 = ta[7], tb[7], ta[6], tb[6]
         f7, f6 = e0(7), e0(6)
         k = curl_p(f7, zero)
-        h7 = tuple(f + s * t for f, t in zip(h0(7), k))
+        h7 = tuple(f + s_first * t for f, t in zip(h0(7), k))
         put(to_hi, 0, h7[1])
         put(to_hi, 1, h7[2])
         h6, h5 = step_h(6), step_h(5)
@@ -370,6 +437,7 @@
         put(to_hi, 4, h7[1] + s * k7[1])
         put(to_hi, 5, h7[2] + s * k7[2])
         s = row_mask
+        m_first = s * first_l
 
         def l0(x):
             return tuple(tle[g, c, x] for c in range(3))
@@ -381,7 +449,7 @@
             return tuple(tlh[g, c, x] for c in range(3))
 
         def step_m(x):
-            return tuple(f + s * k for f, k in zip(m0(x), curl_p(w0(x), w0(x + 1))))
+            return tuple(f + m_first * k for f, k in zip(m0(x), curl_p(w0(x), w0(x + 1))))
 
         q0, v0 = l0(0), w0(0)
         put(to_lo, 6, v0[1])
@@ -391,7 +459,7 @@
         put(to_lo, 9, a0 * q0[2] - CC * m[2])
         q7 = l0(7)
         k7 = curl_p(w0(7), zero)
-        n7 = tuple(f + s * t for f, t in zip(m0(7), k7))
+        n7 = tuple(f + m_first * t for f, t in zip(m0(7), k7))
         put(to_hi, 6, n7[1])
         put(to_hi, 7, n7[2])
         m = curl_m(n7, step_m(6))
@@ -489,8 +557,8 @@
     def one_group(g, carry):
         lx, point = tow_at(tow, g, depth_at, lat_at, lat_n)
         lam = (tle, l1, l2)
-        s = row_mask
         for n in range(2):
+            s = row_mask * unstepped(16, -2) if n == 0 else row_mask
             w = {}
 
             def scaled(x, n=n, w=w):
@@ -508,14 +576,13 @@
                 old = triple(lam[n], g, x)
                 for c in range(3):
                     lam[n + 1][g, c, x] = ta[x] * old[c] - CC * k[c]
-        s = -CC * row_mask
-
         def e_of(n, x):
             if n == 0:
                 return triple(te, g, x)
             return tuple(ei[e_at(g, n - 1, c, x), :] for c in range(3))
 
         for n in range(3):
+            s = -CC * (row_mask * unstepped(17, -3) if n == 0 else row_mask)
             for x in range(n, 7 - n):
                 k = curl_p(e_of(n, x), e_of(n, x + 1))
                 base = triple(th if n == 0 else hh, g, x)
@@ -630,7 +697,7 @@
             return triple(mm if n <= x <= 6 - n else mo, g, x)
 
         def m_step(n, nxt):
-            w = {8: nxt}
+            w = {8: nxt if n else (None, 0.0, 0.0)}
 
             def scaled(x):
                 if x not in w:
@@ -642,8 +709,11 @@
                     continue
                 k = curl_p(scaled(x), scaled(x + 1))
                 base = triple(tlh, g, x) if n == 0 else m_of(n - 1, x)
+                new = tuple(base[c] + (s if n else s * unstepped(16, -2)) * k[c] for c in range(3))
+                if n == 0:
+                    new = (new[0], new[1] - s * nxt[2], new[2] + s * nxt[1])
                 for c in range(3):
-                    mo[g, c, x] = base[c] + s * k[c]
+                    mo[g, c, x] = new[c]
 
         def l_step(n, prv):
             out = (o1, o2)[n]
@@ -681,10 +751,14 @@
             for x in range(8):
                 if n <= x <= 6 - n:
                     continue
-                k = curl_p(e_of(n, x), nxt if x == 7 else e_of(n, x + 1))
+                after = (nxt if n else (None, 0.0, 0.0)) if x == 7 else e_of(n, x + 1)
+                k = curl_p(e_of(n, x), after)
                 base = triple(th, g, x) if n == 0 else h_of(n - 1, x)
+                new = tuple(base[c] + (s if n else s * unstepped(17, -3)) * k[c] for c in range(3))
+                if n == 0:
+                    new = (new[0], new[1] - s * nxt[2], new[2] + s * nxt[1])
                 for c in range(3):
-                    ho[g, c, x] = base[c] + s * k[c]
+                    ho[g, c, x] = new[c]
 
         def e_step(n, prv):
             for x in range(8):

time: 52.9 us -> 51.4 us (0.972)
  waiting for transfers between devices: 12.2 us -> 10.7 us
    ppermute x2, waiting for transfers between devices: 7.43 us -> 5.83 us  [swapped(): lax.ppermute(block, axis, [p for i in lower for p in ((i, i + 1), (i + 1,...]
where the time goes in v5:
time: 51.4 us; the launch traced here: 51 us
  starting transfers between devices  22.9 us (45%)
  waiting for transfers between devices  10.7 us (21%)
  Pallas kernels  9.41 us (18%)
  blocking collectives  7.32 us (14%)
  between operations  0.73 us (1%)
    all_to_all x1, starting transfers between devices, per_device(): got = lax.all_to_all(send, 'lat', split_axis=0, concat_axis=0, tiled=True)  12.3 us
    all_gather x1, blocking collectives, per_device(): every = lax.all_gather(grad, 'src', axis=0, tiled=False)  7.32 us
    ppermute x2, starting transfers between devices, shifted(): return lax.ppermute(block, axis, route)  5.84 us
    ppermute x2, waiting for transfers between devices, swapped(): lax.ppermute(block, axis, [p for i in lower for p in ((i, i + 1), (i + 1,...  5.83 us
    ppermute x2, starting transfers between devices, swapped(): lax.ppermute(block, axis, [p for i in lower for p in ((i, i + 1), (i + 1,...  4.72 us
    ppermute x2, waiting for transfers between devices, shifted(): return lax.ppermute(block, axis, route)  3.62 us
    pallas_call x1, Pallas kernels, outer(): pl.pallas_call(functools.partial(outer_kernel, depth_n, lat_n), out_shape...  2.68 us
    pallas_call x1, Pallas kernels, inner(): pl.pallas_call(functools.partial(inner_kernel, lat_n), out_shape=(field,...  2.15 us
  transfers between devices with their start and end apart: 5, of which 4 were waited for; matrix products, arithmetic and copies ran while one was open for 0% of the time, Pallas kernels for 7%

profile of v5, /device:TPU:32, one launch (start us, length us, event | category | flops | bytes accessed | tf_op | source)
XLA Modules:
  0.0 51.0 jit_solution(9486811658854665615)
XLA Ops:
  0.6 0.0 copy-start.1
  0.6 0.0 copy-start
  0.6 1.2 %pack.1 = (f32[2,3,64,128]{3,2,1,0:T(8,128)S(1)}, f32[2,3,64,128]{3,2,1,0:T(8,128)S(1)}) custom-call(f32[2,3,128,128]{3,2,1,0:T(8,128)} %bitcast.16, f32[2,3,128,128]{3,2,1,0:T(8,128)} %bitcast.18, f32[2,3,128,128]{3,2,1,0:T(8,128)} %bitcast.20, f32[2,3,128,128]{3,2,1,0:T(8,128)} %bitcast.22, f32[128,128]{1,0:T(8,128)} %bitcast.24), custom_call_target="tpu_custom_call" | custom-call | tf_op jit(solution)/shard_map/pack/pallas_call | solution.py:203
  1.9 0.0 copy-start.2
  1.9 2.6 %collective-permute-start = (f32[2,3,64,128]{3,2,1,0:T(8,128)S(1)}, f32[2,3,64,128]{3,2,1,0:T(8,128)S(1)}, u32[]{:S(2)}, u32[]{:S(2)}) collective-permute-start(f32[2,3,64,128]{3,2,1,0:T(8,128)S(1)} %get-tuple-element.34), channel_id=1, source_target_pairs={{0,16},{16,0},{32,48},{48,32},{64,80},{80,64},{96,112},{112,96},{1... | collective-permute-start | bytes 589832 | tf_op jit(solution)/shard_map/ppermute | solution.py:28
  4.5 2.1 %collective-permute-start.1 = (f32[2,3,64,128]{3,2,1,0:T(8,128)S(1)}, f32[2,3,64,128]{3,2,1,0:T(8,128)S(1)}, u32[]{:S(2)}, u32[]{:S(2)}) collective-permute-start(f32[2,3,64,128]{3,2,1,0:T(8,128)S(1)} %get-tuple-element.35), channel_id=1, source_target_pairs={{16,32},{32,16},{48,64},{64,48},{80,96},{96,80},{17,33},{33,17},{4... | collective-permute-start | bytes 589832 | tf_op jit(solution)/shard_map/ppermute | solution.py:28
  6.6 1.5 %own.1 = (f32[2,3,8,24,128]{4,3,2,1,0:T(8,128)S(1)}, f32[2,3,8,24,128]{4,3,2,1,0:T(8,128)S(1)}, f32[2,3,8,24,128]{4,3,2,1,0:T(8,128)S(1)}, f32[2,3,8,24,128]{4,3,2,1,0:T(8,128)S(1)}, f32[8,16,128]{2,1,0:T(8,128)S(1)}) custom-call(f32[2,3,128,128]{3,2,1,0:T(8,128)} %bitcast.17, f32[2,3,128,128]{3,2,1,0:T(8,128)} %bitcast.19, f32[2,3,128,128]{3,2,1,0:T(8,128)} %bitcast.21, ...), custom_call_target="tpu_custom_call" | custom-call | flops 5000000 | bytes 8000000 | tf_op jit(solution)/shard_map/own/pallas_call | solution.py:288
  8.1 2.3 %collective-permute-done.one = f32[2,3,64,128]{3,2,1,0:T(8,128)S(1)} collective-permute-done((f32[2,3,64,128]{3,2,1,0:T(8,128)S(1)}, f32[2,3,64,128]{3,2,1,0:T(8,128)S(1)}, u32[]{:S(2)}, u32[]{:S(2)}) %collective-permute-start) | collective-permute-done | bytes 196640 | tf_op jit(solution)/shard_map/ppermute | solution.py:28
  10.4 3.5 %collective-permute-done.1.two = f32[2,3,64,128]{3,2,1,0:T(8,128)S(1)} collective-permute-done((f32[2,3,64,128]{3,2,1,0:T(8,128)S(1)}, f32[2,3,64,128]{3,2,1,0:T(8,128)S(1)}, u32[]{:S(2)}, u32[]{:S(2)}) %collective-permute-start.1) | collective-permute-done | bytes 196640 | tf_op jit(solution)/shard_map/ppermute | solution.py:28
  13.9 0.0 copy-done.1
  13.9 0.0 copy-done
  13.9 0.0 copy-start.3
  13.9 1.2 %planes.1 = (f32[2,3,8,24,128]{4,3,2,1,0:T(8,128)S(1)}, f32[2,3,8,24,128]{4,3,2,1,0:T(8,128)S(1)}, f32[2,3,8,24,128]{4,3,2,1,0:T(8,128)S(1)}, f32[2,3,8,24,128]{...) custom-call(f32[2,3,8,24,128]{4,3,2,1,0:T(8,128)S(1)} %get-tuple-ele, ...), custom_call_target="tpu_custom_call", output_to_operand_aliasing={{0}: (0, {}), {1}: (1, {}), {2}: (2, {}), {3}: (3, {})} | custom-call | tf_op jit(solution)/shard_map/planes/pallas_call | solution.py:480
  15.1 1.3 %collective-permute-start.3 = (f32[2,200,128]{2,1,0:T(8,128)S(1)}, f32[2,200,128]{2,1,0:T(8,128)S(1)}, u32[]{:S(2)}, u32[]{:S(2)}) collective-permute-start(f32[2,200,128]{2,1,0:T(8,128)S(1)} %get-tuple-element.51), channel_id=1, source_target_pairs={{1,0},{2,1},{3,2},{4,3},{5,4},{6,5},{7,6},{8,7},{9,8},{10,9},{11,1... | collective-permute-start | bytes 614408 | tf_op jit(solution)/shard_map/ppermute | solution.py:22
  16.4 4.6 %collective-permute-start.2 = (f32[2,192,128]{2,1,0:T(8,128)S(1)}, f32[2,192,128]{2,1,0:T(8,128)S(1)}, u32[]{:S(2)}, u32[]{:S(2)}) collective-permute-start(f32[2,192,128]{2,1,0:T(8,128)S(1)} %get-tuple-element.50), channel_id=1, source_target_pairs={{0,1},{1,2},{2,3},{3,4},{4,5},{5,6},{6,7},{7,8},{8,9},{9,10},{10,1... | collective-permute-start | bytes 589832 | tf_op jit(solution)/shard_map/ppermute | solution.py:22
  21.0 0.0 copy-done.2
  21.0 2.1 %inner.1 = (f32[2,3,8,24,128]{4,3,2,1,0:T(8,128)S(1)}, f32[2,3,8,24,128]{4,3,2,1,0:T(8,128)S(1)}, f32[2,3,8,24,128]{4,3,2,1,0:T(8,128)S(1)}, f32[2,3,8,24,128]{4...) custom-call(f32[2,3,8,24,128]{4,3,2,1,0:T(8,128)S(1)} %get-tuple-ele, ...), custom_call_target="tpu_custom_call" | custom-call | flops 20000000 | bytes 12000000 | tf_op jit(solution)/shard_map/inner/pallas_call | solution.py:617
  23.2 3.6 %collective-permute-done.2.lo = f32[2,192,128]{2,1,0:T(8,128)S(1)} collective-permute-done((f32[2,192,128]{2,1,0:T(8,128)S(1)}, f32[2,192,128]{2,1,0:T(8,128)S(1)}, u32[]{:S(2)}, u32[]{:S(2)}) %collective-permute-start.2) | collective-permute-done | bytes 196640 | tf_op jit(solution)/shard_map/ppermute | solution.py:22
  26.8 0.0 collective-permute-done.3.hi
  26.8 0.0 copy-done.3
  26.8 2.7 %outer.1 = (f32[128,128]{1,0:T(8,128)S(1)}, f32[16,2,128]{2,1,0:T(2,128)}) custom-call(f32[2,3,8,24,128]{4,3,2,1,0:T(8,128)S(1)} %get-tuple-element.36.te, f32[2,3,8,24,128]{4,3,2,1,0:T(8,128)S(1)} %get-tuple-element.37.th, f32[2,3,8,24,128]{4,3,2,1,0:T(8,128)S(1)} %get-tuple-element.38.tle, f32[2,3,8,24,128]{4,3,2,1,0:T(8,128)S(1)} %get-tuple-element.39.tlh, ...), custom_call_target="tpu_custom_call" | custom-call | flops 10000000 | bytes 12000000 | tf_op jit(solution)/shard_map/outer/pallas_call | solution.py:837
  29.5 12.3 %all-to-all-start = ((f32[16,2,128]{2,1,0:T(2,128)}), f32[16,2,128]{2,1,0:T(2,128)S(1)}, u32[]{:S(2)}, u32[]{:S(2)}) async-start(f32[16,2,128]{2,1,0:T(2,128)} %get-tuple-element.53), calls=%async_computation | async-start | bytes 32768 | tf_op jit(solution)/shard_map/all_to_all | solution.py:924
  41.8 7.3 %all-gather = f32[512,128]{1,0:T(8,128)S(1)} all-gather(f32[128,128]{1,0:T(8,128)S(1)} %get-tuple-element.52), channel_id=2, replica_groups=mesh['src'=4,'depth'=8,'lat'=16] {'src'}, dimensions={0}, use_global_device_ids=true | all-gather | bytes 327680 | tf_op jit(solution)/shard_map/all_gather | solution.py:925
  49.1 1.2 %all-to-all-done.got = f32[16,2,128]{2,1,0:T(2,128)S(1)} async-done(((f32[16,2,128]{2,1,0:T(2,128)}), f32[16,2,128]{2,1,0:T(2,128)S(1)}, u32[]{:S(2)}, u32[]{:S(2)}) %all-to-all-start) | async-done | bytes 16416 | tf_op jit(solution)/shard_map/all_to_all | solution.py:924
  50.4 0.7 %finish.1 = (f32[128,128]{1,0:T(8,128)}, f32[2,9,2,16]{3,2,1,0:T(2,128)}) custom-call(f32[128,128]{1,0:T(8,128)S(1)} %get-tuple-element.59.mine, f32[128,128]{1,0:T(8,128)S(1)} %get-tuple-element.58.theirs, f32[16,2,128]{2,1,0:T(2,128)S(1)} %all-to-all-done.got), custom_call_target="tpu_custom_call" | custom-call | tf_op jit(solution)/shard_map/finish/pallas_call | solution.py:864
  (1 shorter events, 0.0 us)
Async XLA Ops:
  0.6 13.3 %copy-start.1 = (s32[2]{0:T(128)S(1)}, s32[2]{0:T(128)}, u32[]{:S(2)}) copy-start(s32[2]{0:T(128)} %tow.5) | copy-start | bytes 28
  0.6 13.3 %copy-start = (f32[2,3]{1,0:T(2,128)S(1)}, f32[2,3]{1,0:T(2,128)}, u32[]{:S(2)}) copy-start(f32[2,3]{1,0:T(2,128)} %amp.5) | copy-start | bytes 76
  1.9 19.1 %copy-start.2 = (s32[1,1,16]{2,1,0:T(1,128)S(1)}, s32[1,1,16]{2,1,0:T(1,128)}, u32[]{:S(2)}) copy-start(s32[1,1,16]{2,1,0:T(1,128)} %param.16) | copy-start | bytes 196
  1.9 8.5 %collective-permute-start = (f32[2,3,64,128]{3,2,1,0:T(8,128)S(1)}, f32[2,3,64,128]{3,2,1,0:T(8,128)S(1)}, u32[]{:S(2)}, u32[]{:S(2)}) collective-permute-start(f32[2,3,64,128]{3,2,1,0:T(8,128)S(1)} %get-tuple-element.34), channel_id=1, source_target_pairs={{0,16},{16,0},{32,48},{48,32},{64,80},{80,64},{96,112},{112,96},{1... | collective-permute-start | bytes 589832 | tf_op jit(solution)/shard_map/ppermute | solution.py:28
  4.5 9.5 %collective-permute-start.1 = (f32[2,3,64,128]{3,2,1,0:T(8,128)S(1)}, f32[2,3,64,128]{3,2,1,0:T(8,128)S(1)}, u32[]{:S(2)}, u32[]{:S(2)}) collective-permute-start(f32[2,3,64,128]{3,2,1,0:T(8,128)S(1)} %get-tuple-element.35), channel_id=1, source_target_pairs={{16,32},{32,16},{48,64},{64,48},{80,96},{96,80},{17,33},{33,17},{4... | collective-permute-start | bytes 589832 | tf_op jit(solution)/shard_map/ppermute | solution.py:28
  13.9 12.8 %copy-start.3 = (s32[1,1,16,1]{2,3,1,0:T(1,128)S(1)}, s32[1,1,16,1]{2,3,1,0:T(1,128)}, u32[]{:S(2)}) copy-start(s32[1,1,16,1]{2,3,1,0:T(1,128)} %param.17) | copy-start | bytes 196
  15.1 11.6 %collective-permute-start.3 = (f32[2,200,128]{2,1,0:T(8,128)S(1)}, f32[2,200,128]{2,1,0:T(8,128)S(1)}, u32[]{:S(2)}, u32[]{:S(2)}) collective-permute-start(f32[2,200,128]{2,1,0:T(8,128)S(1)} %get-tuple-element.51), channel_id=1, source_target_pairs={{1,0},{2,1},{3,2},{4,3},{5,4},{6,5},{7,6},{8,7},{9,8},{10,9},{11,1... | collective-permute-start | bytes 614408 | tf_op jit(solution)/shard_map/ppermute | solution.py:22
  16.4 10.3 %collective-permute-start.2 = (f32[2,192,128]{2,1,0:T(8,128)S(1)}, f32[2,192,128]{2,1,0:T(8,128)S(1)}, u32[]{:S(2)}, u32[]{:S(2)}) collective-permute-start(f32[2,192,128]{2,1,0:T(8,128)S(1)} %get-tuple-element.50), channel_id=1, source_target_pairs={{0,1},{1,2},{2,3},{3,4},{4,5},{5,6},{6,7},{7,8},{8,9},{9,10},{10,1... | collective-permute-start | bytes 589832 | tf_op jit(solution)/shard_map/ppermute | solution.py:22
  29.5 20.9 %all-to-all-start = ((f32[16,2,128]{2,1,0:T(2,128)}), f32[16,2,128]{2,1,0:T(2,128)S(1)}, u32[]{:S(2)}, u32[]{:S(2)}) async-start(f32[16,2,128]{2,1,0:T(2,128)} %get-tuple-element.53), calls=%async_computation | async-start | bytes 32768 | tf_op jit(solution)/shard_map/all_to_all | solution.py:924

commit v6 on v5

--- a/solution.py
+++ b/solution.py
@@ -81,9 +81,10 @@
 
 def coefs(conductivity, keep):
     inv = 1.0 / (1.0 + KK * conductivity)
-    a = jnp.where(keep, (1.0 - KK * conductivity) * inv, 0.0)
-    b = jnp.where(keep, CC * inv, 0.0)
-    return a, b
+    a, b = (1.0 - KK * conductivity) * inv, CC * inv
+    if keep is True:
+        return a, b
+    return jnp.where(keep, a, 0.0), jnp.where(keep, b, 0.0)
 
 
 def first_row_mask(depth_at):
@@ -259,7 +260,7 @@
     return jnp.concatenate([ref[0, at : at + 8], ref[1, at : at + 8], rest], axis=0)
 
 
-def own_kernel(e, h, le, lh, cond, te, th, tle, tlh, tc, be, bh, ble, blh, bc, sems):
+def own_kernel(e, h, le, lh, cond, te, th, tle, tlh, ta, tb, tc, be, bh, ble, blh, bc, sems):
     pairs = ((e, be), (h, bh), (le, ble), (lh, blh), (cond, bc))
     copies = [pltpu.make_async_copy(src, dst, sems.at[k]) for k, (src, dst) in enumerate(pairs)]
     for c in copies:
@@ -277,8 +278,11 @@
         lax.fori_loop(0, e.shape[0], body, 0)
     copies[4].wait()
     for x in range(8):
-        tc[x, 0:8] = bc[pl.ds(x, 8, stride=8), :]
-        tc[x, 8:16] = bc[pl.ds(64 + x, 8, stride=8), :]
+        for half in range(2):
+            value = bc[pl.ds(half * 64 + x, 8, stride=8), :]
+            at = pl.ds(half * 8, 8)
+            tc[x, at] = value
+            ta[x, at], tb[x, at] = coefs(value, True)
 
 
 def own_planes(e, h, le, lh, cond):
@@ -287,9 +291,11 @@
     field = jax.ShapeDtypeStruct((g, 3, 8, ROWS, 128), F32)
     return pl.pallas_call(
         own_kernel,
-        out_shape=(field,) * 4 + (jax.ShapeDtypeStruct((8, 16, 128), F32),),
+        out_shape=(field,) * 4
+        + (jax.ShapeDtypeStruct((8, ROWS, 128), F32),) * 2
+        + (jax.ShapeDtypeStruct((8, 16, 128), F32),),
         in_specs=[pl.BlockSpec(memory_space=pl.ANY)] * 5,
-        out_specs=(vm,) * 5,
+        out_specs=(vm,) * 7,
         scratch_shapes=[pltpu.VMEM((g, 3, 128, 128), F32)] * 4
         + [pltpu.VMEM((128, 128), F32), pltpu.SemaphoreType.DMA((5,))],
         cost_estimate=pl.CostEstimate(flops=5_000_000, bytes_accessed=8_000_000, transcendentals=0),
@@ -305,6 +311,8 @@
     ih,
     ile,
     ilh,
+    ia,
+    ib,
     tc,
     one,
     two,
@@ -364,14 +372,11 @@
         rest = jnp.where(r8 == 1, u1[x : x + 1], rest)
         rest = jnp.where(r8 == 6, d0[x : x + 1], rest)
         rest = jnp.where(r8 == 7, d1[x : x + 1], rest)
-        whole = jnp.concatenate([tc[x], rest], axis=0)
-        a, b = coefs(whole, keep)
-        ta[x] = a
-        tb[x] = b
+        ta[x, 16:24], tb[x, 16:24] = coefs(rest, keep[16:24])
         if x == 0:
-            put_conductivity(to_lo, TO_LO, whole)
+            put_conductivity(to_lo, TO_LO, jnp.concatenate([tc[x], rest], axis=0))
         if x == 7:
-            put_conductivity(to_hi, TO_HI, whole)
+            put_conductivity(to_hi, TO_HI, jnp.concatenate([tc[x], rest], axis=0))
     row_mask = first_row_mask(depth_at)
     z, lane = zrow(), lanes()
 
@@ -489,9 +494,9 @@
             jax.ShapeDtypeStruct((g, chunk(TO_LO), 128), F32),
             jax.ShapeDtypeStruct((g, chunk(TO_HI), 128), F32),
         ),
-        in_specs=[vm] * 7 + [sm] * 2,
+        in_specs=[vm] * 9 + [sm] * 2,
         out_specs=(vm,) * 8,
-        input_output_aliases={0: 0, 1: 1, 2: 2, 3: 3},
+        input_output_aliases={0: 0, 1: 1, 2: 2, 3: 3, 4: 4, 5: 5},
         compiler_params=pltpu.CompilerParams(vmem_limit_bytes=24 * 1024 * 1024),
         name="planes",
     )(*own, one, two, amp, tow)
@@ -665,7 +670,10 @@
     o1,
     o2,
     total,
+    drives,
+    staged,
     count,
+    sem,
 ):
     groups = te.shape[0]
     depth_at = lax.axis_index("depth")
@@ -683,7 +691,13 @@
         near = inside(n - 1, x)
         return triple((l1 if near else o1) if n == 1 else (l2 if near else o2), g, x)
 
-    def one_group(g, carry):
+    def e_of(n, g, x):
+        if n == 0:
+            return triple(te, g, x)
+        ref = ei if inside(n - 1, x) else eo
+        return tuple(ref[e_at(g, n - 1, c, x), :] for c in range(3))
+
+    def forward(g, carry):
         def high(k):
             return get_plane(hi, TO_LO, g, k)
 
@@ -691,58 +705,7 @@
             return get_plane(lo, TO_HI, g, k)
 
         lx, point = tow_at(tow, g, depth_at, lat_at, lat_n)
-        s = row_mask
-
-        def m_of(n, x):
-            return triple(mm if n <= x <= 6 - n else mo, g, x)
-
-        def m_step(n, nxt):
-            w = {8: nxt if n else (None, 0.0, 0.0)}
-
-            def scaled(x):
-                if x not in w:
-                    w[x] = tuple(tb[x] * f for f in lam(n, g, x))
-                return w[x]
-
-            for x in range(8):
-                if n <= x <= 6 - n:
-                    continue
-                k = curl_p(scaled(x), scaled(x + 1))
-                base = triple(tlh, g, x) if n == 0 else m_of(n - 1, x)
-                new = tuple(base[c] + (s if n else s * unstepped(16, -2)) * k[c] for c in range(3))
-                if n == 0:
-                    new = (new[0], new[1] - s * nxt[2], new[2] + s * nxt[1])
-                for c in range(3):
-                    mo[g, c, x] = new[c]
-
-        def l_step(n, prv):
-            out = (o1, o2)[n]
-            for x in range(8):
-                if inside(n, x):
-                    continue
-                k = curl_m(m_of(n, x), m_of(n, x - 1) if x else prv)
-                old = lam(n, g, x)
-                for c in range(3):
-                    out[g, c, x] = ta[x] * old[c] - CC * k[c]
-
-        m_step(0, (None, high(6), high(7)))
-        first = lam(0, g, 0)
-        dy, dz = -s * (tb[0] * first[2]), s * (tb[0] * first[1])
-        l_step(0, (None, left * (low(6) + dy), left * (low(7) + dz)))
-        last = m_of(0, 7)
-        m_step(1, (None, b8 * (high(8) - CC * last[2]), b8 * (high(9) + CC * last[1])))
-        wx, wy, wz = -CC * bl * (dmy(dz) - dmz(dy)), CC * bl * dz, -CC * bl * dy
-        first = lam(1, g, 0)
-        dy = dy + s * (dpz(wx) - (tb[0] * first[2] - wz))
-        dz = dz + s * ((tb[0] * first[1] - wy) - dpy(wx))
-        l_step(1, (None, left * (low(8) + dy), left * (low(9) + dz)))
         s = -CC * row_mask
-
-        def e_of(n, x):
-            if n == 0:
-                return triple(te, g, x)
-            ref = ei if inside(n - 1, x) else eo
-            return tuple(ref[e_at(g, n - 1, c, x), :] for c in range(3))
 
         def h_of(n, x):
             return triple(hh if n <= x <= 6 - n else ho, g, x)
@@ -751,8 +714,8 @@
             for x in range(8):
                 if n <= x <= 6 - n:
                     continue
-                after = (nxt if n else (None, 0.0, 0.0)) if x == 7 else e_of(n, x + 1)
-                k = curl_p(e_of(n, x), after)
+                after = (nxt if n else (None, 0.0, 0.0)) if x == 7 else e_of(n, g, x + 1)
+                k = curl_p(e_of(n, g, x), after)
                 base = triple(th, g, x) if n == 0 else h_of(n - 1, x)
                 new = tuple(base[c] + (s if n else s * unstepped(17, -3)) * k[c] for c in range(3))
                 if n == 0:
@@ -762,27 +725,24 @@
 
         def e_step(n, prv):
             for x in range(8):
-                old = e_of(n, x)
                 if inside(n, x):
-                    if n == 0 and x in (1, 6):
-                        k = tuple(d0[g, c, x // 6] for c in range(3))
-                        total[x] += weighted(old, k, lam(2, g, x))
                     continue
+                old = e_of(n, g, x)
                 k = curl_m(h_of(n, x), h_of(n, x - 1) if x else prv)
                 k = (k[0] - jnp.where(lx == x, amp[g, n], 0.0) * point, k[1], k[2])
                 for c in range(3):
                     eo[e_at(g, n, c, x), :] = ta[x] * old[c] + tb[x] * k[c]
-                total[x] += weighted(old, k, lam(2 - n, g, x))
+                    drives[g, n, c, x] = k[c][0:16]
 
         h_step(0, (None, high(0), high(1)))
-        first = e_of(0, 0)
+        first = e_of(0, g, 0)
         dy, dz = -s * first[2], s * first[1]
         e_step(0, (None, left * (low(0) + dy), left * (low(1) + dz)))
         last = h_of(0, 7)
         uy, uz = b8 * last[2], -b8 * last[1]
         h_step(1, (None, high(2) + uy, high(3) + uz))
         ex, ey, ez = bl * (dmy(dz) - dmz(dy)), -bl * dz, bl * dy
-        first = e_of(1, 0)
+        first = e_of(1, g, 0)
         dy = dy + s * (dpz(ex) - (first[2] - ez))
         dz = dz + s * ((first[1] - ey) - dpy(ex))
         e_step(1, (None, left * (low(2) + dy), left * (low(3) + dz)))
@@ -802,32 +762,100 @@
             al * ey + bl * (dmz(hx) - dz + hz),
             al * ez + bl * (dy - hy - dmy(hx)),
         )
-        first = e_of(2, 0)
+        first = e_of(2, g, 0)
         dy = dy + s * (dpz(ex) - (first[2] - ez))
         dz = dz + s * ((first[1] - ey) - dpy(ex))
         e_step(2, (None, left * (low(4) + dy), left * (low(5) + dz)))
         return carry
 
-    lax.fori_loop(0, groups, one_group, 0, unroll=True)
+    lax.fori_loop(0, groups, forward, 0, unroll=True)
+    staged[...] = jnp.zeros_like(staged)
+    for o in range(staged.shape[0]):
+        count[o] = 0
+    r24, lane = lax.broadcasted_iota(jnp.int32, (SLOTS, 128), 0), lanes()
+    used = (r24 == lane) & (r24 < groups * 9)
+
+    def put(r, values):
+        o = rowner[r]
+        slot = count[o]
+        count[o] = slot + 1
+        values = jnp.sum(samp[r] + values, axis=-1, keepdims=True)
+        staged[o, pl.ds(slot, 1), :] = jnp.sum(jnp.where(used, values, 0.0), axis=0, keepdims=True)
+
+    take_samples(eo, rcell, jnp.logical_not, put)
+    leave = pltpu.make_async_copy(staged, send, sem)
+    leave.start()
+
+    def adjoint(g, carry):
+        def high(k):
+            return get_plane(hi, TO_LO, g, k)
+
+        def low(k):
+            return get_plane(lo, TO_HI, g, k)
+
+        s = row_mask
+
+        def m_of(n, x):
+            return triple(mm if n <= x <= 6 - n else mo, g, x)
+
+        def m_step(n, nxt):
+            w = {8: nxt if n else (None, 0.0, 0.0)}
+
+            def scaled(x):
+                if x not in w:
+                    w[x] = tuple(tb[x] * f for f in lam(n, g, x))
+                return w[x]
+
+            for x in range(8):
+                if n <= x <= 6 - n:
+                    continue
+                k = curl_p(scaled(x), scaled(x + 1))
+                base = triple(tlh, g, x) if n == 0 else m_of(n - 1, x)
+                new = tuple(base[c] + (s if n else s * unstepped(16, -2)) * k[c] for c in range(3))
+                if n == 0:
+                    new = (new[0], new[1] - s * nxt[2], new[2] + s * nxt[1])
+                for c in range(3):
+                    mo[g, c, x] = new[c]
+
+        def l_step(n, prv):
+            out = (o1, o2)[n]
+            for x in range(8):
+                if inside(n, x):
+                    continue
+                k = curl_m(m_of(n, x), m_of(n, x - 1) if x else prv)
+                old = lam(n, g, x)
+                for c in range(3):
+                    out[g, c, x] = ta[x] * old[c] - CC * k[c]
+
+        m_step(0, (None, high(6), high(7)))
+        first = lam(0, g, 0)
+        dy, dz = -s * (tb[0] * first[2]), s * (tb[0] * first[1])
+        l_step(0, (None, left * (low(6) + dy), left * (low(7) + dz)))
+        last = m_of(0, 7)
+        m_step(1, (None, b8 * (high(8) - CC * last[2]), b8 * (high(9) + CC * last[1])))
+        wx, wy, wz = -CC * bl * (dmy(dz) - dmz(dy)), CC * bl * dz, -CC * bl * dy
+        first = lam(1, g, 0)
+        dy = dy + s * (dpz(wx) - (tb[0] * first[2] - wz))
+        dz = dz + s * ((tb[0] * first[1] - wy) - dpy(wx))
+        l_step(1, (None, left * (low(8) + dy), left * (low(9) + dz)))
+        for n in range(3):
+            for x in range(8):
+                if n == 0 and x in (1, 6):
+                    drive = tuple(d0[g, c, x // 6] for c in range(3))
+                elif inside(n, x):
+                    continue
+                else:
+                    drive = tuple(drives[g, n, c, x] for c in range(3))
+                total[x] += weighted(e_of(n, g, x), drive, lam(2 - n, g, x))
+        return carry
+
+    lax.fori_loop(0, groups, adjoint, 0, unroll=True)
     for x in range(8):
         for half in range(2):
             rows = pl.ds(half * 64 + x, 8, stride=8)
             inv = tb[x, half * 8 : half * 8 + 8] * (1.0 / CC)
             grad[rows, :] = total[x, half * 8 : half * 8 + 8] * inv * inv
-    send[...] = jnp.zeros_like(send)
-    for o in range(send.shape[0]):
-        count[o] = 0
-    r24, lane = lax.broadcasted_iota(jnp.int32, (SLOTS, 128), 0), lanes()
-    used = (r24 == lane) & (r24 < groups * 9)
-
-    def put(r, values):
-        o = rowner[r]
-        slot = count[o]
-        count[o] = slot + 1
-        values = jnp.sum(samp[r] + values, axis=-1, keepdims=True)
-        send[o, pl.ds(slot, 1), :] = jnp.sum(jnp.where(used, values, 0.0), axis=0, keepdims=True)
-
-    take_samples(eo, rcell, jnp.logical_not, put)
+    leave.wait()
 
 
 def outer(te, th, tle, tlh, ta, tb, kept, lo, hi, amp, tow, rcell, rowner, depth_n, lat_n):
@@ -841,10 +869,16 @@
             jax.ShapeDtypeStruct((lat_n, 2, 128), F32),
         ),
         in_specs=[vm] * 16 + [sm] * 4,
-        out_specs=(vm,) * 2,
+        out_specs=(vm, pl.BlockSpec(memory_space=pl.ANY)),
         scratch_shapes=[pltpu.VMEM((SLOTS * STRIDE, 128), F32)]
         + [pltpu.VMEM((g, 3, 8, ROWS, 128), F32)] * 4
-        + [pltpu.VMEM((8, 16, 128), F32), pltpu.SMEM((lat_n,), jnp.int32)],
+        + [
+            pltpu.VMEM((8, 16, 128), F32),
+            pltpu.VMEM((g, 3, 3, 8, 16, 128), F32),
+            pltpu.VMEM((lat_n, 2, 128), F32),
+            pltpu.SMEM((lat_n,), jnp.int32),
+            pltpu.SemaphoreType.DMA(()),
+        ],
         cost_estimate=pl.CostEstimate(flops=10_000_000, bytes_accessed=12_000_000, transcendentals=0),
         compiler_params=pltpu.CompilerParams(vmem_limit_bytes=24 * 1024 * 1024),
         name="outer",

time: 51.4 us -> 51.3 us (level)
  no operation moved by 1% of the time
where the time goes in v6:
time: 51.3 us; the launch traced here: 50.9 us
  starting transfers between devices  22.9 us (45%)
  waiting for transfers between devices  10.7 us (21%)
  Pallas kernels  9.28 us (18%)
  blocking collectives  7.32 us (14%)
  between operations  0.74 us (1%)
    all_to_all x1, starting transfers between devices, per_device(): got = lax.all_to_all(send, 'lat', split_axis=0, concat_axis=0, tiled=True)  12.3 us
    all_gather x1, blocking collectives, per_device(): every = lax.all_gather(grad, 'src', axis=0, tiled=False)  7.32 us
    ppermute x2, starting transfers between devices, shifted(): return lax.ppermute(block, axis, route)  5.84 us
    ppermute x2, waiting for transfers between devices, swapped(): lax.ppermute(block, axis, [p for i in lower for p in ((i, i + 1), (i + 1,...  5.82 us
    ppermute x2, starting transfers between devices, swapped(): lax.ppermute(block, axis, [p for i in lower for p in ((i, i + 1), (i + 1,...  4.72 us
    ppermute x2, waiting for transfers between devices, shifted(): return lax.ppermute(block, axis, route)  3.62 us
    pallas_call x1, Pallas kernels, outer(): pl.pallas_call(functools.partial(outer_kernel, depth_n, lat_n), out_shape...  2.56 us
    pallas_call x1, Pallas kernels, inner(): pl.pallas_call(functools.partial(inner_kernel, lat_n), out_shape=(field,...  2.14 us
  transfers between devices with their start and end apart: 5, of which 4 were waited for; matrix products, arithmetic and copies ran while one was open for 0% of the time, Pallas kernels for 7%

profile of v6, /device:TPU:32, one launch (start us, length us, event | category | flops | bytes accessed | tf_op | source)
XLA Modules:
  0.0 50.9 jit_solution(13937106136607647379)
XLA Ops:
  0.6 0.0 copy-start.1
  0.6 0.0 copy-start
  0.6 1.2 %pack.1 = (f32[2,3,64,128]{3,2,1,0:T(8,128)S(1)}, f32[2,3,64,128]{3,2,1,0:T(8,128)S(1)}) custom-call(f32[2,3,128,128]{3,2,1,0:T(8,128)} %bitcast.16, f32[2,3,128,128]{3,2,1,0:T(8,128)} %bitcast.18, f32[2,3,128,128]{3,2,1,0:T(8,128)} %bitcast.20, f32[2,3,128,128]{3,2,1,0:T(8,128)} %bitcast.22, f32[128,128]{1,0:T(8,128)} %bitcast.24), custom_call_target="tpu_custom_call" | custom-call | tf_op jit(solution)/shard_map/pack/pallas_call | solution.py:204
  1.9 0.0 copy-start.2
  1.9 2.6 %collective-permute-start = (f32[2,3,64,128]{3,2,1,0:T(8,128)S(1)}, f32[2,3,64,128]{3,2,1,0:T(8,128)S(1)}, u32[]{:S(2)}, u32[]{:S(2)}) collective-permute-start(f32[2,3,64,128]{3,2,1,0:T(8,128)S(1)} %get-tuple-element.38), channel_id=1, source_target_pairs={{0,16},{16,0},{32,48},{48,32},{64,80},{80,64},{96,112},{112,96},{1... | collective-permute-start | bytes 589832 | tf_op jit(solution)/shard_map/ppermute | solution.py:28
  4.5 2.1 %collective-permute-start.1 = (f32[2,3,64,128]{3,2,1,0:T(8,128)S(1)}, f32[2,3,64,128]{3,2,1,0:T(8,128)S(1)}, u32[]{:S(2)}, u32[]{:S(2)}) collective-permute-start(f32[2,3,64,128]{3,2,1,0:T(8,128)S(1)} %get-tuple-element.39), channel_id=1, source_target_pairs={{16,32},{32,16},{48,64},{64,48},{80,96},{96,80},{17,33},{33,17},{4... | collective-permute-start | bytes 589832 | tf_op jit(solution)/shard_map/ppermute | solution.py:28
  6.6 1.5 %own.1 = (f32[2,3,8,24,128]{4,3,2,1,0:T(8,128)S(1)}, f32[2,3,8,24,128]{4,3,2,1,0:T(8,128)S(1)}, f32[2,3,8,24,128]{4,3,2,1,0:T(8,128)S(1)}, f32[2,3,8,24,128]{4,3...) custom-call(f32[2,3,128,128]{3,2,1,0:T(8,128)} %bitcast.17, ...), custom_call_target="tpu_custom_call" | custom-call | flops 5000000 | bytes 8000000 | tf_op jit(solution)/shard_map/own/pallas_call | solution.py:292
  8.1 2.3 %collective-permute-done.one = f32[2,3,64,128]{3,2,1,0:T(8,128)S(1)} collective-permute-done((f32[2,3,64,128]{3,2,1,0:T(8,128)S(1)}, f32[2,3,64,128]{3,2,1,0:T(8,128)S(1)}, u32[]{:S(2)}, u32[]{:S(2)}) %collective-permute-start) | collective-permute-done | bytes 196640 | tf_op jit(solution)/shard_map/ppermute | solution.py:28
  10.4 3.5 %collective-permute-done.1.two = f32[2,3,64,128]{3,2,1,0:T(8,128)S(1)} collective-permute-done((f32[2,3,64,128]{3,2,1,0:T(8,128)S(1)}, f32[2,3,64,128]{3,2,1,0:T(8,128)S(1)}, u32[]{:S(2)}, u32[]{:S(2)}) %collective-permute-start.1) | collective-permute-done | bytes 196640 | tf_op jit(solution)/shard_map/ppermute | solution.py:28
  13.9 0.0 copy-done.1
  13.9 0.0 copy-done
  13.9 0.0 copy-start.3
  13.9 1.2 %planes.1 = (f32[2,3,8,24,128]{4,3,2,1,0:T(8,128)S(1)}, f32[2,3,8,24,128]{4,3,2,1,0:T(8,128)S(1)}, f32[2,3,8,24,128]{4,3,2,1,0:T(8,128)S(1)}, f32[2,3,8,24,128]{...) custom-call(f32[2,3,8,24,128]{4,3,2,1,0:T(8,128)S(1)} %get-tuple-ele, ...), custom_call_target="tpu_custom_call", output_to_operand_aliasing={{0}: (0, {}), {1}: (1, {}), {2}: (2, {}), {3}: (3, {}), {4}... | custom-call | tf_op jit(solution)/shard_map/planes/pallas_call | solution.py:485
  15.1 1.3 %collective-permute-start.3 = (f32[2,200,128]{2,1,0:T(8,128)S(1)}, f32[2,200,128]{2,1,0:T(8,128)S(1)}, u32[]{:S(2)}, u32[]{:S(2)}) collective-permute-start(f32[2,200,128]{2,1,0:T(8,128)S(1)} %get-tuple-element.55), channel_id=1, source_target_pairs={{1,0},{2,1},{3,2},{4,3},{5,4},{6,5},{7,6},{8,7},{9,8},{10,9},{11,1... | collective-permute-start | bytes 614408 | tf_op jit(solution)/shard_map/ppermute | solution.py:22
  16.4 4.6 %collective-permute-start.2 = (f32[2,192,128]{2,1,0:T(8,128)S(1)}, f32[2,192,128]{2,1,0:T(8,128)S(1)}, u32[]{:S(2)}, u32[]{:S(2)}) collective-permute-start(f32[2,192,128]{2,1,0:T(8,128)S(1)} %get-tuple-element.54), channel_id=1, source_target_pairs={{0,1},{1,2},{2,3},{3,4},{4,5},{5,6},{6,7},{7,8},{8,9},{9,10},{10,1... | collective-permute-start | bytes 589832 | tf_op jit(solution)/shard_map/ppermute | solution.py:22
  21.0 0.0 copy-done.2
  21.0 2.1 %inner.1 = (f32[2,3,8,24,128]{4,3,2,1,0:T(8,128)S(1)}, f32[2,3,8,24,128]{4,3,2,1,0:T(8,128)S(1)}, f32[2,3,8,24,128]{4,3,2,1,0:T(8,128)S(1)}, f32[2,3,8,24,128]{4...) custom-call(f32[2,3,8,24,128]{4,3,2,1,0:T(8,128)S(1)} %get-tuple-ele, ...), custom_call_target="tpu_custom_call" | custom-call | flops 20000000 | bytes 12000000 | tf_op jit(solution)/shard_map/inner/pallas_call | solution.py:622
  23.1 3.6 %collective-permute-done.2.lo = f32[2,192,128]{2,1,0:T(8,128)S(1)} collective-permute-done((f32[2,192,128]{2,1,0:T(8,128)S(1)}, f32[2,192,128]{2,1,0:T(8,128)S(1)}, u32[]{:S(2)}, u32[]{:S(2)}) %collective-permute-start.2) | collective-permute-done | bytes 196640 | tf_op jit(solution)/shard_map/ppermute | solution.py:22
  26.7 0.0 collective-permute-done.3.hi
  26.8 0.0 copy-done.3
  26.8 2.6 %outer.1 = (f32[128,128]{1,0:T(8,128)S(1)}, f32[16,2,128]{2,1,0:T(2,128)}) custom-call(f32[2,3,8,24,128]{4,3,2,1,0:T(8,128)S(1)} %get-tuple-element.40.te, f32[2,3,8,24,128]{4,3,2,1,0:T(8,128)S(1)} %get-tuple-element.41.th, f32[2,3,8,24,128]{4,3,2,1,0:T(8,128)S(1)} %get-tuple-element.42.tle, f32[2,3,8,24,128]{4,3,2,1,0:T(8,128)S(1)} %get-tuple-element.43.tlh, ...), custom_call_target="tpu_custom_call" | custom-call | flops 10000000 | bytes 12000000 | tf_op jit(solution)/shard_map/outer/pallas_call | solution.py:865
  29.3 12.3 %all-to-all-start = ((f32[16,2,128]{2,1,0:T(2,128)}), f32[16,2,128]{2,1,0:T(2,128)S(1)}, u32[]{:S(2)}, u32[]{:S(2)}) async-start(f32[16,2,128]{2,1,0:T(2,128)} %get-tuple-element.57), calls=%async_computation | async-start | bytes 32768 | tf_op jit(solution)/shard_map/all_to_all | solution.py:958
  41.7 7.3 %all-gather = f32[512,128]{1,0:T(8,128)S(1)} all-gather(f32[128,128]{1,0:T(8,128)S(1)} %get-tuple-element.56), channel_id=2, replica_groups=mesh['src'=4,'depth'=8,'lat'=16] {'src'}, dimensions={0}, use_global_device_ids=true | all-gather | bytes 327680 | tf_op jit(solution)/shard_map/all_gather | solution.py:959
  49.0 1.2 %all-to-all-done.got = f32[16,2,128]{2,1,0:T(2,128)S(1)} async-done(((f32[16,2,128]{2,1,0:T(2,128)}), f32[16,2,128]{2,1,0:T(2,128)S(1)}, u32[]{:S(2)}, u32[]{:S(2)}) %all-to-all-start) | async-done | bytes 16416 | tf_op jit(solution)/shard_map/all_to_all | solution.py:958
  50.2 0.7 %finish.1 = (f32[128,128]{1,0:T(8,128)}, f32[2,9,2,16]{3,2,1,0:T(2,128)}) custom-call(f32[128,128]{1,0:T(8,128)S(1)} %get-tuple-element.63.mine, f32[128,128]{1,0:T(8,128)S(1)} %get-tuple-element.62.theirs, f32[16,2,128]{2,1,0:T(2,128)S(1)} %all-to-all-done.got), custom_call_target="tpu_custom_call" | custom-call | tf_op jit(solution)/shard_map/finish/pallas_call | solution.py:898
  (1 shorter events, 0.0 us)
Async XLA Ops:
  0.6 13.3 %copy-start.1 = (s32[2]{0:T(128)S(1)}, s32[2]{0:T(128)}, u32[]{:S(2)}) copy-start(s32[2]{0:T(128)} %tow.5) | copy-start | bytes 28
  0.6 13.3 %copy-start = (f32[2,3]{1,0:T(2,128)S(1)}, f32[2,3]{1,0:T(2,128)}, u32[]{:S(2)}) copy-start(f32[2,3]{1,0:T(2,128)} %amp.5) | copy-start | bytes 76
  1.9 19.1 %copy-start.2 = (s32[1,1,16]{2,1,0:T(1,128)S(1)}, s32[1,1,16]{2,1,0:T(1,128)}, u32[]{:S(2)}) copy-start(s32[1,1,16]{2,1,0:T(1,128)} %param.16) | copy-start | bytes 196
  1.9 8.5 %collective-permute-start = (f32[2,3,64,128]{3,2,1,0:T(8,128)S(1)}, f32[2,3,64,128]{3,2,1,0:T(8,128)S(1)}, u32[]{:S(2)}, u32[]{:S(2)}) collective-permute-start(f32[2,3,64,128]{3,2,1,0:T(8,128)S(1)} %get-tuple-element.38), channel_id=1, source_target_pairs={{0,16},{16,0},{32,48},{48,32},{64,80},{80,64},{96,112},{112,96},{1... | collective-permute-start | bytes 589832 | tf_op jit(solution)/shard_map/ppermute | solution.py:28
  4.5 9.5 %collective-permute-start.1 = (f32[2,3,64,128]{3,2,1,0:T(8,128)S(1)}, f32[2,3,64,128]{3,2,1,0:T(8,128)S(1)}, u32[]{:S(2)}, u32[]{:S(2)}) collective-permute-start(f32[2,3,64,128]{3,2,1,0:T(8,128)S(1)} %get-tuple-element.39), channel_id=1, source_target_pairs={{16,32},{32,16},{48,64},{64,48},{80,96},{96,80},{17,33},{33,17},{4... | collective-permute-start | bytes 589832 | tf_op jit(solution)/shard_map/ppermute | solution.py:28
  13.9 12.8 %copy-start.3 = (s32[1,1,16,1]{2,3,1,0:T(1,128)S(1)}, s32[1,1,16,1]{2,3,1,0:T(1,128)}, u32[]{:S(2)}) copy-start(s32[1,1,16,1]{2,3,1,0:T(1,128)} %param.17) | copy-start | bytes 196
  15.1 11.6 %collective-permute-start.3 = (f32[2,200,128]{2,1,0:T(8,128)S(1)}, f32[2,200,128]{2,1,0:T(8,128)S(1)}, u32[]{:S(2)}, u32[]{:S(2)}) collective-permute-start(f32[2,200,128]{2,1,0:T(8,128)S(1)} %get-tuple-element.55), channel_id=1, source_target_pairs={{1,0},{2,1},{3,2},{4,3},{5,4},{6,5},{7,6},{8,7},{9,8},{10,9},{11,1... | collective-permute-start | bytes 614408 | tf_op jit(solution)/shard_map/ppermute | solution.py:22
  16.4 10.3 %collective-permute-start.2 = (f32[2,192,128]{2,1,0:T(8,128)S(1)}, f32[2,192,128]{2,1,0:T(8,128)S(1)}, u32[]{:S(2)}, u32[]{:S(2)}) collective-permute-start(f32[2,192,128]{2,1,0:T(8,128)S(1)} %get-tuple-element.54), channel_id=1, source_target_pairs={{0,1},{1,2},{2,3},{3,4},{4,5},{5,6},{6,7},{7,8},{8,9},{9,10},{10,1... | collective-permute-start | bytes 589832 | tf_op jit(solution)/shard_map/ppermute | solution.py:22
  29.3 20.9 %all-to-all-start = ((f32[16,2,128]{2,1,0:T(2,128)}), f32[16,2,128]{2,1,0:T(2,128)S(1)}, u32[]{:S(2)}, u32[]{:S(2)}) async-start(f32[16,2,128]{2,1,0:T(2,128)} %get-tuple-element.57), calls=%async_computation | async-start | bytes 32768 | tf_op jit(solution)/shard_map/all_to_all | solution.py:958

commit v7 on v6

--- a/solution.py
+++ b/solution.py
@@ -134,8 +134,6 @@
         )
     for c in copies:
         c.start()
-    for c in copies:
-        c.wait()
     sub = lax.broadcasted_iota(jnp.int32, (8, 128), 0)
 
     def xp(f):
@@ -151,6 +149,11 @@
         return vc[k * 8 : k * 8 + 8]
 
     def fill(up, dn):
+        def store(ref, g, c, slot, value):
+            ref[g, c, slot * 8 : slot * 8 + 8] = value
+
+        for c in copies[:4]:
+            c.wait()
         for g in range(e.shape[0]):
 
             def e_of(c, z, g=g):
@@ -159,35 +162,39 @@
             def h_of(c, z, g=g):
                 return tile(vh, g, c, z)
 
+            h17 = stepped(e_of, 1, h_of, -CC, xp)
+            h3 = stepped(e_of, 13, h_of, -CC, xp)
+            for c in range(3):
+                for k, value in enumerate((e_of(c, 0), e_of(c, 1), h_of(c, 0), h17[c])):
+                    store(up, g, c, k, value)
+                for k, z in ((0, 14), (1, 15)):
+                    store(dn, g, c, k, e_of(c, z))
+                    store(dn, g, c, 3 + k, h_of(c, z))
+                if c < 2:
+                    store(dn, g, c, 2, h3[c])
+        for c in copies[4:]:
+            c.wait()
+        for g in range(e.shape[0]):
+
             def w_of(c, z, g=g):
                 return CC / (1.0 + KK * layer(z)) * tile(vl, g, c, z)
 
             def m_of(c, z, g=g):
                 return tile(vm, g, c, z)
 
-            h17 = stepped(e_of, 1, h_of, -CC, xp)
-            h3 = stepped(e_of, 13, h_of, -CC, xp)
             m16 = stepped(w_of, 0, m_of, 1.0, xp)
             m2 = stepped(w_of, 14, m_of, 1.0, xp)
-            extra = jnp.where(sub == 0, e_of(2, 13), 0.0)
+            extra = jnp.where(sub == 0, tile(ve, g, 2, 13), 0.0)
             extra = jnp.where(sub == 1, pltpu.roll(tile(vl, g, 2, 14), 1, 0), extra)
+            store(dn, g, 2, 2, extra)
             for c in range(3):
                 blank = jnp.zeros((8, 128), F32)
-                ups = (e_of(c, 0), e_of(c, 1), h_of(c, 0), h17[c], tile(vl, g, c, 0), m16[c])
-                ups += (layer(0), layer(1)) if g == 0 and c == 0 else (blank, blank)
-                dns = (
-                    e_of(c, 14),
-                    e_of(c, 15),
-                    h3[c] if c < 2 else extra,
-                    h_of(c, 14),
-                    h_of(c, 15),
-                    tile(vl, g, c, 15),
-                    m2[c] if c < 2 else layer(14 + g % 2),
-                    m_of(c, 15),
-                )
-                for k in range(SPAN):
-                    up[g, c, k * 8 : k * 8 + 8] = ups[k]
-                    dn[g, c, k * 8 : k * 8 + 8] = dns[k]
+                last = (layer(0), layer(1)) if g == 0 and c == 0 else (blank, blank)
+                for k, value in enumerate((tile(vl, g, c, 0), m16[c]) + last):
+                    store(up, g, c, 4 + k, value)
+                store(dn, g, c, 5, tile(vl, g, c, 15))
+                store(dn, g, c, 6, m2[c] if c < 2 else layer(14 + g % 2))
+                store(dn, g, c, 7, m_of(c, 15))
 
     @pl.when(even)
     def _():

time: 51.3 us -> 51.3 us (level)
  no operation moved by 1% of the time
where the time goes in v7:
time: 51.3 us; the launch traced here: 51 us
  starting transfers between devices  22.9 us (45%)
  waiting for transfers between devices  10.7 us (21%)
  Pallas kernels  9.36 us (18%)
  blocking collectives  7.32 us (14%)
  between operations  0.74 us (1%)
    all_to_all x1, starting transfers between devices, per_device(): got = lax.all_to_all(send, 'lat', split_axis=0, concat_axis=0, tiled=True)  12.3 us
    all_gather x1, blocking collectives, per_device(): every = lax.all_gather(grad, 'src', axis=0, tiled=False)  7.32 us
    ppermute x2, starting transfers between devices, shifted(): return lax.ppermute(block, axis, route)  5.84 us
    ppermute x2, waiting for transfers between devices, swapped(): lax.ppermute(block, axis, [p for i in lower for p in ((i, i + 1), (i + 1,...  5.82 us
    ppermute x2, starting transfers between devices, swapped(): lax.ppermute(block, axis, [p for i in lower for p in ((i, i + 1), (i + 1,...  4.72 us
    ppermute x2, waiting for transfers between devices, shifted(): return lax.ppermute(block, axis, route)  3.62 us
    pallas_call x1, Pallas kernels, outer(): pl.pallas_call(functools.partial(outer_kernel, depth_n, lat_n), out_shape...  2.57 us
    pallas_call x1, Pallas kernels, inner(): pl.pallas_call(functools.partial(inner_kernel, lat_n), out_shape=(field,...  2.15 us
  transfers between devices with their start and end apart: 5, of which 4 were waited for; matrix products, arithmetic and copies ran while one was open for 0% of the time, Pallas kernels for 7%

profile of v7, /device:TPU:32, one launch (start us, length us, event | category | flops | bytes accessed | tf_op | source)
XLA Modules:
  0.0 51.0 jit_solution(12902015218582296479)
XLA Ops:
  0.6 0.0 copy-start.1
  0.6 0.0 copy-start
  0.6 1.3 %pack.1 = (f32[2,3,64,128]{3,2,1,0:T(8,128)S(1)}, f32[2,3,64,128]{3,2,1,0:T(8,128)S(1)}) custom-call(f32[2,3,128,128]{3,2,1,0:T(8,128)} %bitcast.16, f32[2,3,128,128]{3,2,1,0:T(8,128)} %bitcast.18, f32[2,3,128,128]{3,2,1,0:T(8,128)} %bitcast.20, f32[2,3,128,128]{3,2,1,0:T(8,128)} %bitcast.22, f32[128,128]{1,0:T(8,128)} %bitcast.24), custom_call_target="tpu_custom_call" | custom-call | tf_op jit(solution)/shard_map/pack/pallas_call | solution.py:211
  1.9 0.0 copy-start.2
  1.9 2.6 %collective-permute-start = (f32[2,3,64,128]{3,2,1,0:T(8,128)S(1)}, f32[2,3,64,128]{3,2,1,0:T(8,128)S(1)}, u32[]{:S(2)}, u32[]{:S(2)}) collective-permute-start(f32[2,3,64,128]{3,2,1,0:T(8,128)S(1)} %get-tuple-element.38), channel_id=1, source_target_pairs={{0,16},{16,0},{32,48},{48,32},{64,80},{80,64},{96,112},{112,96},{1... | collective-permute-start | bytes 589832 | tf_op jit(solution)/shard_map/ppermute | solution.py:28
  4.5 2.1 %collective-permute-start.1 = (f32[2,3,64,128]{3,2,1,0:T(8,128)S(1)}, f32[2,3,64,128]{3,2,1,0:T(8,128)S(1)}, u32[]{:S(2)}, u32[]{:S(2)}) collective-permute-start(f32[2,3,64,128]{3,2,1,0:T(8,128)S(1)} %get-tuple-element.39), channel_id=1, source_target_pairs={{16,32},{32,16},{48,64},{64,48},{80,96},{96,80},{17,33},{33,17},{4... | collective-permute-start | bytes 589832 | tf_op jit(solution)/shard_map/ppermute | solution.py:28
  6.7 1.5 %own.1 = (f32[2,3,8,24,128]{4,3,2,1,0:T(8,128)S(1)}, f32[2,3,8,24,128]{4,3,2,1,0:T(8,128)S(1)}, f32[2,3,8,24,128]{4,3,2,1,0:T(8,128)S(1)}, f32[2,3,8,24,128]{4,3...) custom-call(f32[2,3,128,128]{3,2,1,0:T(8,128)} %bitcast.17, ...), custom_call_target="tpu_custom_call" | custom-call | flops 5000000 | bytes 8000000 | tf_op jit(solution)/shard_map/own/pallas_call | solution.py:299
  8.2 2.3 %collective-permute-done.one = f32[2,3,64,128]{3,2,1,0:T(8,128)S(1)} collective-permute-done((f32[2,3,64,128]{3,2,1,0:T(8,128)S(1)}, f32[2,3,64,128]{3,2,1,0:T(8,128)S(1)}, u32[]{:S(2)}, u32[]{:S(2)}) %collective-permute-start) | collective-permute-done | bytes 196640 | tf_op jit(solution)/shard_map/ppermute | solution.py:28
  10.5 3.5 %collective-permute-done.1.two = f32[2,3,64,128]{3,2,1,0:T(8,128)S(1)} collective-permute-done((f32[2,3,64,128]{3,2,1,0:T(8,128)S(1)}, f32[2,3,64,128]{3,2,1,0:T(8,128)S(1)}, u32[]{:S(2)}, u32[]{:S(2)}) %collective-permute-start.1) | collective-permute-done | bytes 196640 | tf_op jit(solution)/shard_map/ppermute | solution.py:28
  14.0 0.0 copy-done.1
  14.0 0.0 copy-done
  14.0 0.0 copy-start.3
  14.0 1.2 %planes.1 = (f32[2,3,8,24,128]{4,3,2,1,0:T(8,128)S(1)}, f32[2,3,8,24,128]{4,3,2,1,0:T(8,128)S(1)}, f32[2,3,8,24,128]{4,3,2,1,0:T(8,128)S(1)}, f32[2,3,8,24,128]{...) custom-call(f32[2,3,8,24,128]{4,3,2,1,0:T(8,128)S(1)} %get-tuple-ele, ...), custom_call_target="tpu_custom_call", output_to_operand_aliasing={{0}: (0, {}), {1}: (1, {}), {2}: (2, {}), {3}: (3, {}), {4}... | custom-call | tf_op jit(solution)/shard_map/planes/pallas_call | solution.py:492
  15.2 1.3 %collective-permute-start.3 = (f32[2,200,128]{2,1,0:T(8,128)S(1)}, f32[2,200,128]{2,1,0:T(8,128)S(1)}, u32[]{:S(2)}, u32[]{:S(2)}) collective-permute-start(f32[2,200,128]{2,1,0:T(8,128)S(1)} %get-tuple-element.55), channel_id=1, source_target_pairs={{1,0},{2,1},{3,2},{4,3},{5,4},{6,5},{7,6},{8,7},{9,8},{10,9},{11,1... | collective-permute-start | bytes 614408 | tf_op jit(solution)/shard_map/ppermute | solution.py:22
  16.5 4.6 %collective-permute-start.2 = (f32[2,192,128]{2,1,0:T(8,128)S(1)}, f32[2,192,128]{2,1,0:T(8,128)S(1)}, u32[]{:S(2)}, u32[]{:S(2)}) collective-permute-start(f32[2,192,128]{2,1,0:T(8,128)S(1)} %get-tuple-element.54), channel_id=1, source_target_pairs={{0,1},{1,2},{2,3},{3,4},{4,5},{5,6},{6,7},{7,8},{8,9},{9,10},{10,1... | collective-permute-start | bytes 589832 | tf_op jit(solution)/shard_map/ppermute | solution.py:22
  21.0 0.0 copy-done.2
  21.1 2.1 %inner.1 = (f32[2,3,8,24,128]{4,3,2,1,0:T(8,128)S(1)}, f32[2,3,8,24,128]{4,3,2,1,0:T(8,128)S(1)}, f32[2,3,8,24,128]{4,3,2,1,0:T(8,128)S(1)}, f32[2,3,8,24,128]{4...) custom-call(f32[2,3,8,24,128]{4,3,2,1,0:T(8,128)S(1)} %get-tuple-ele, ...), custom_call_target="tpu_custom_call" | custom-call | flops 20000000 | bytes 12000000 | tf_op jit(solution)/shard_map/inner/pallas_call | solution.py:629
  23.2 3.6 %collective-permute-done.2.lo = f32[2,192,128]{2,1,0:T(8,128)S(1)} collective-permute-done((f32[2,192,128]{2,1,0:T(8,128)S(1)}, f32[2,192,128]{2,1,0:T(8,128)S(1)}, u32[]{:S(2)}, u32[]{:S(2)}) %collective-permute-start.2) | collective-permute-done | bytes 196640 | tf_op jit(solution)/shard_map/ppermute | solution.py:22
  26.8 0.0 collective-permute-done.3.hi
  26.8 0.0 copy-done.3
  26.8 2.6 %outer.1 = (f32[128,128]{1,0:T(8,128)S(1)}, f32[16,2,128]{2,1,0:T(2,128)}) custom-call(f32[2,3,8,24,128]{4,3,2,1,0:T(8,128)S(1)} %get-tuple-element.40.te, f32[2,3,8,24,128]{4,3,2,1,0:T(8,128)S(1)} %get-tuple-element.41.th, f32[2,3,8,24,128]{4,3,2,1,0:T(8,128)S(1)} %get-tuple-element.42.tle, f32[2,3,8,24,128]{4,3,2,1,0:T(8,128)S(1)} %get-tuple-element.43.tlh, ...), custom_call_target="tpu_custom_call" | custom-call | flops 10000000 | bytes 12000000 | tf_op jit(solution)/shard_map/outer/pallas_call | solution.py:872
  29.4 12.3 %all-to-all-start = ((f32[16,2,128]{2,1,0:T(2,128)}), f32[16,2,128]{2,1,0:T(2,128)S(1)}, u32[]{:S(2)}, u32[]{:S(2)}) async-start(f32[16,2,128]{2,1,0:T(2,128)} %get-tuple-element.57), calls=%async_computation | async-start | bytes 32768 | tf_op jit(solution)/shard_map/all_to_all | solution.py:965
  41.7 7.3 %all-gather = f32[512,128]{1,0:T(8,128)S(1)} all-gather(f32[128,128]{1,0:T(8,128)S(1)} %get-tuple-element.56), channel_id=2, replica_groups=mesh['src'=4,'depth'=8,'lat'=16] {'src'}, dimensions={0}, use_global_device_ids=true | all-gather | bytes 327680 | tf_op jit(solution)/shard_map/all_gather | solution.py:966
  49.1 1.2 %all-to-all-done.got = f32[16,2,128]{2,1,0:T(2,128)S(1)} async-done(((f32[16,2,128]{2,1,0:T(2,128)}), f32[16,2,128]{2,1,0:T(2,128)S(1)}, u32[]{:S(2)}, u32[]{:S(2)}) %all-to-all-start) | async-done | bytes 16416 | tf_op jit(solution)/shard_map/all_to_all | solution.py:965
  50.3 0.7 %finish.1 = (f32[128,128]{1,0:T(8,128)}, f32[2,9,2,16]{3,2,1,0:T(2,128)}) custom-call(f32[128,128]{1,0:T(8,128)S(1)} %get-tuple-element.63.mine, f32[128,128]{1,0:T(8,128)S(1)} %get-tuple-element.62.theirs, f32[16,2,128]{2,1,0:T(2,128)S(1)} %all-to-all-done.got), custom_call_target="tpu_custom_call" | custom-call | tf_op jit(solution)/shard_map/finish/pallas_call | solution.py:905
  (1 shorter events, 0.0 us)
Async XLA Ops:
  0.6 13.4 %copy-start.1 = (s32[2]{0:T(128)S(1)}, s32[2]{0:T(128)}, u32[]{:S(2)}) copy-start(s32[2]{0:T(128)} %tow.5) | copy-start | bytes 28
  0.6 13.4 %copy-start = (f32[2,3]{1,0:T(2,128)S(1)}, f32[2,3]{1,0:T(2,128)}, u32[]{:S(2)}) copy-start(f32[2,3]{1,0:T(2,128)} %amp.5) | copy-start | bytes 76
  1.9 19.1 %copy-start.2 = (s32[1,1,16]{2,1,0:T(1,128)S(1)}, s32[1,1,16]{2,1,0:T(1,128)}, u32[]{:S(2)}) copy-start(s32[1,1,16]{2,1,0:T(1,128)} %param.16) | copy-start | bytes 196
  1.9 8.5 %collective-permute-start = (f32[2,3,64,128]{3,2,1,0:T(8,128)S(1)}, f32[2,3,64,128]{3,2,1,0:T(8,128)S(1)}, u32[]{:S(2)}, u32[]{:S(2)}) collective-permute-start(f32[2,3,64,128]{3,2,1,0:T(8,128)S(1)} %get-tuple-element.38), channel_id=1, source_target_pairs={{0,16},{16,0},{32,48},{48,32},{64,80},{80,64},{96,112},{112,96},{1... | collective-permute-start | bytes 589832 | tf_op jit(solution)/shard_map/ppermute | solution.py:28
  4.5 9.5 %collective-permute-start.1 = (f32[2,3,64,128]{3,2,1,0:T(8,128)S(1)}, f32[2,3,64,128]{3,2,1,0:T(8,128)S(1)}, u32[]{:S(2)}, u32[]{:S(2)}) collective-permute-start(f32[2,3,64,128]{3,2,1,0:T(8,128)S(1)} %get-tuple-element.39), channel_id=1, source_target_pairs={{16,32},{32,16},{48,64},{64,48},{80,96},{96,80},{17,33},{33,17},{4... | collective-permute-start | bytes 589832 | tf_op jit(solution)/shard_map/ppermute | solution.py:28
  14.0 12.8 %copy-start.3 = (s32[1,1,16,1]{2,3,1,0:T(1,128)S(1)}, s32[1,1,16,1]{2,3,1,0:T(1,128)}, u32[]{:S(2)}) copy-start(s32[1,1,16,1]{2,3,1,0:T(1,128)} %param.17) | copy-start | bytes 196
  15.2 11.6 %collective-permute-start.3 = (f32[2,200,128]{2,1,0:T(8,128)S(1)}, f32[2,200,128]{2,1,0:T(8,128)S(1)}, u32[]{:S(2)}, u32[]{:S(2)}) collective-permute-start(f32[2,200,128]{2,1,0:T(8,128)S(1)} %get-tuple-element.55), channel_id=1, source_target_pairs={{1,0},{2,1},{3,2},{4,3},{5,4},{6,5},{7,6},{8,7},{9,8},{10,9},{11,1... | collective-permute-start | bytes 614408 | tf_op jit(solution)/shard_map/ppermute | solution.py:22
  16.5 10.3 %collective-permute-start.2 = (f32[2,192,128]{2,1,0:T(8,128)S(1)}, f32[2,192,128]{2,1,0:T(8,128)S(1)}, u32[]{:S(2)}, u32[]{:S(2)}) collective-permute-start(f32[2,192,128]{2,1,0:T(8,128)S(1)} %get-tuple-element.54), channel_id=1, source_target_pairs={{0,1},{1,2},{2,3},{3,4},{4,5},{5,6},{6,7},{7,8},{8,9},{9,10},{10,1... | collective-permute-start | bytes 589832 | tf_op jit(solution)/shard_map/ppermute | solution.py:22
  29.4 20.9 %all-to-all-start = ((f32[16,2,128]{2,1,0:T(2,128)}), f32[16,2,128]{2,1,0:T(2,128)S(1)}, u32[]{:S(2)}, u32[]{:S(2)}) async-start(f32[16,2,128]{2,1,0:T(2,128)} %get-tuple-element.57), calls=%async_computation | async-start | bytes 32768 | tf_op jit(solution)/shard_map/all_to_all | solution.py:965
